TPU v7x, 256 devices: a whole 4x4x8 slice. The times are simulated.
256 devices in a mesh: ctx: 32 (over z, y_hi, core), exp: 8 (over y_lo, x).
Axes of the slice: x: 4, y: 4 (y_hi: 2, y_lo: 2; y = y_hi * 2 + y_lo), z: 8, core: 2. Of those that a mesh axis runs over, the one named last changes fastest.
Arguments:
- hidden_in: bfloat16 [8, 6144, 1024], P('exp', 'ctx'), may hold values from -6 to 6
- queries: bfloat16 [8, 6144, 1024], P('exp', 'ctx'), may hold values from -128 to 128
- key_proj: bfloat16 [8, 6144, 256], P('exp', 'ctx'), may hold values from -16 to 16
- value_proj: bfloat16 [8, 6144, 256], P('exp', 'ctx'), may hold values from -6 to 6
- tile_mask: int32 [8, 192, 192], P('exp', 'ctx'), may hold values from 0 to 1, as said below
- out_weight: bfloat16 [1024, 1024], replicated, may hold values from -0.1875 to 0.1875
- moe_gain: float32 [1024], replicated, may hold values from 0.1 to 1.9
- gate_weight: bfloat16 [8, 1024, 1792], P('exp', 'ctx'), may hold values from -0.1875 to 0.1875
- up_weight: bfloat16 [8, 1024, 1792], P('exp', 'ctx'), may hold values from -0.1875 to 0.1875
- down_weight: bfloat16 [8, 1024, 1792], P('exp', 'ctx'), may hold values from -0.125 to 0.125
- expert_ids: int32 [8, 6144, 2], P('exp', 'ctx'), may hold values from 0 to 7, all different within a row; in each aligned block of 192 rows (0 to 191, 192 to 383, ..., all dimensions but the last counted through in order) at most 72 rows name the same one
- gate_probs: float32 [8, 6144, 2], P('exp', 'ctx'), may hold values from 0.05 to 0.95, as said below
Outputs:
- attention_out: bfloat16 [8, 6144, 1024], P('exp', 'ctx')
- layer_out: bfloat16 [8, 6144, 1024], P('exp', 'ctx')
Inputs may be any that keep to these rules, and one draw needn't show every extreme that they name: `expert_ids`: within one block of 192 tokens of a sequence (the tokens of one device), no expert is named by more than 72 pairs; the 2 ids of a token differ. tile_mask[s, i, i] = 1 for every tile i. `gate_probs`: the 2 weights of a token sum to 1.
All inputs are finite; a program needn't handle non-finite values.
Results may differ from a plain program's by a relative error of at most 0.0065.
Values may be sent and summed in bfloat16 or wider, within the bound.
A program may use at most 128 MiB of HBM per device.

v0:
```python
import jax
import jax.numpy as jnp
from jax import lax
from jax.sharding import PartitionSpec as P

D = 1024
HEADS = 8
KV_HEADS = 2
EXPERTS = 8
TOP = 2
TILE = 32
CAP = 72


def rms_scale(row_block, gain):
    widened = row_block.astype(jnp.float32)
    inverse = lax.rsqrt(jnp.mean(widened * widened, axis=-1, keepdims=True) + 1e-05)
    return widened * inverse * gain


def shards(
    hidden_in,
    queries,
    key_proj,
    value_proj,
    tile_mask,
    out_weight,
    moe_gain,
    gate_weight,
    up_weight,
    down_weight,
    expert_ids,
    gate_probs,
):
    query_rows = queries[0]
    row_count = query_rows.shape[0]
    groups = HEADS // KV_HEADS
    head_size = D // HEADS
    query_heads = query_rows.reshape(row_count, KV_HEADS, groups, head_size)
    mask_block = tile_mask[0]
    key_piece = lax.all_gather(key_proj[0], "ctx", axis=0, tiled=True)
    value_piece = lax.all_gather(value_proj[0], "ctx", axis=0, tiled=True)
    piece_rows = key_piece.shape[0]
    running_max = jnp.full((KV_HEADS, groups, row_count, 1), -1e30, jnp.float32)
    allowed = jnp.repeat(jnp.repeat(mask_block, TILE, axis=0), TILE, axis=1) > 0
    key_heads = key_piece.reshape(piece_rows, KV_HEADS, head_size)
    value_heads = value_piece.reshape(piece_rows, KV_HEADS, head_size)
    scores = jnp.einsum(
        "qkgd,rkd->kgqr", query_heads, key_heads, preferred_element_type=jnp.float32
    ) * head_size ** (-0.5)
    scores = jnp.where(allowed, scores, -1e30)
    newest_max = jnp.maximum(running_max, jnp.max(scores, axis=-1, keepdims=True))
    weights = jnp.where(allowed, jnp.exp(scores - newest_max), 0.0)
    denominator = jnp.sum(weights, axis=-1, keepdims=True)
    accumulated = jnp.einsum(
        "kgqr,rkd->kgqd",
        weights.astype(jnp.bfloat16),
        value_heads,
        preferred_element_type=jnp.float32,
    )
    running_max, denominator, accumulated = (newest_max, denominator, accumulated)
    attended = (
        (accumulated / denominator).transpose(2, 0, 1, 3).reshape(row_count, D).astype(jnp.bfloat16)
    )
    projected = jnp.dot(attended, out_weight, preferred_element_type=jnp.float32)
    attention_out = projected.astype(jnp.bfloat16)
    residual = (hidden_in[0].astype(jnp.float32) + projected).astype(jnp.bfloat16)
    normed = rms_scale(residual, moe_gain).astype(jnp.bfloat16)
    id_row = expert_ids[0].reshape(-1)
    onehot = (id_row[:, None] == jnp.arange(EXPERTS, dtype=jnp.int32)[None, :]).astype(jnp.int32)
    before = jnp.cumsum(onehot, axis=0) - onehot
    slot_index = jnp.sum(before * onehot, axis=1)
    target = id_row * CAP + slot_index
    selector = (jnp.arange(EXPERTS * CAP, dtype=jnp.int32)[:, None] == target[None, :]).astype(
        jnp.bfloat16
    )
    repeated = jnp.repeat(normed, TOP, axis=0)
    outgoing = (
        jnp.dot(selector, repeated, preferred_element_type=jnp.float32)
        .astype(jnp.bfloat16)
        .reshape(EXPERTS, CAP, D)
    )
    arrived = lax.all_to_all(outgoing, "exp", split_axis=0, concat_axis=1, tiled=True)
    gate_piece = lax.all_gather(gate_weight, "ctx", axis=1, tiled=True)
    up_piece = lax.all_gather(up_weight, "ctx", axis=1, tiled=True)
    gate_sum = jnp.einsum("esd,edf->esf", arrived, gate_piece, preferred_element_type=jnp.float32)
    up_sum = jnp.einsum("esd,edf->esf", arrived, up_piece, preferred_element_type=jnp.float32)
    hidden = (jax.nn.silu(gate_sum) * up_sum).astype(jnp.bfloat16)
    expert_rows = jnp.einsum(
        "esf,edf->esd",
        hidden,
        lax.all_gather(down_weight, "ctx", axis=1, tiled=True),
        preferred_element_type=jnp.float32,
    ).astype(jnp.bfloat16)
    returned = lax.all_to_all(expert_rows, "exp", split_axis=1, concat_axis=0, tiled=True)
    picked = jnp.take(returned.reshape(EXPERTS * CAP, D), target, axis=0).reshape(row_count, TOP, D)
    mixture = jnp.sum(picked.astype(jnp.float32) * gate_probs[0][:, :, None], axis=1)
    layer_out = (residual.astype(jnp.float32) + mixture).astype(jnp.bfloat16)
    return (attention_out[None], layer_out[None])


def solution(mesh):
    return jax.shard_map(
        shards,
        mesh=mesh,
        in_specs=(
            P("exp", "ctx", None),
            P("exp", "ctx", None),
            P("exp", "ctx", None),
            P("exp", "ctx", None),
            P("exp", "ctx", None),
            P(),
            P(),
            P("exp", "ctx", None),
            P("exp", "ctx", None),
            P("exp", "ctx", None),
            P("exp", "ctx", None),
            P("exp", "ctx", None),
        ),
        out_specs=(P("exp", "ctx", None), P("exp", "ctx", None)),
        check_vma=False,
    )
```

profile of v0, /device:TPU:1, one launch (start us, length us, event | category | flops | bytes accessed | tf_op | source)
XLA Modules:
  0.0 501.6 jit_solution(1660429453021570174)
XLA Ops:
  7.2 0.7 all-gather.14.cloned.1.call-update
  8.0 0.7 all-gather.16.cloned.1.call-update
  8.7 0.7 all-gather.10.cloned.1.call-update
  9.4 0.5 all-gather.12.cloned.1.call-update
  10.0 0.5 all-gather.8.cloned.1.call-update
  10.6 0.8 copy.75
  11.7 0.7 broadcast_compare_fusion
  12.4 0.1 copy.67
  12.5 1.5 broadcast_in_dim.48
  14.1 3.6 copy.68
  17.7 2.0 reshape_squeeze.6
  19.7 0.8 reduce-window.6
  20.6 0.2 slice_reduce_fusion
  20.9 77.4 %all-gather.14.cloned.1.call-done = bf16[1,6144,256]{2,1,0:T(8,128)(2,1)} async-done(((bf16[1,192,256]{2,1,0:T(8,128)(2,1)}), bf16[1,6144,256]{2,1,0:T(8,128)(2,1)}) %all-gather.14.cloned.1.call-update) | async-done | bytes 3145744 | tf_op jit(solution)/shard_map/all_gather | solution.py:41
  98.3 4.7 copy.69
  103.0 17.0 %fusion = (f32[2,4,192]{2,1,0:T(4,128)S(1)}, f32[2,6144,192,4]{1,2,3,0:T(8,128)}) fusion(pred[192,6144]{1,0:T(8,128)(4,1)S(1)} %copy.68, bf16[6144,2,128,1]{0,2,3,1:T(8,128)(2,1)} %bitcast.105, bf16[192,2,4,128]{3,2,1,0:T(4,128)(2,1)} %reshape_squeeze.6), kind=kOutput, calls=%fused_computation.3 | convolution fusion | flops 2444229120 | bytes 42473472 | tf_op jit(solution)/shard_map/qkgd,rkd->kgqr/dot_general | solution.py:48
  120.0 18.6 %fusion.1 = f32[2,4,192]{2,1,0:T(4,128)S(1)} fusion(f32[2,6144,192,4]{1,2,3,0:T(8,128)} %get-tuple-element.6, f32[2,4,192]{2,1,0:T(4,128)S(1)} %broadcast_maximum_fusion, pred[192,6144]{1,0:T(8,128)(4,1)S(1)} %copy.68), kind=kLoop, calls=%fused_computation.4 | loop fusion | flops 47184384 | bytes 38940672 | tf_op jit(solution)/shard_map/reduce_sum | solution.py:54
  138.6 42.6 %all-gather.16.cloned.1.call-done = bf16[1,6144,256]{2,1,0:T(8,128)(2,1)} async-done(((bf16[1,192,256]{2,1,0:T(8,128)(2,1)}), bf16[1,6144,256]{2,1,0:T(8,128)(2,1)}) %all-gather.16.cloned.1.call-update) | async-done | bytes 3145744 | tf_op jit(solution)/shard_map/all_gather | solution.py:42
  181.2 4.7 copy.72
  185.8 17.7 %fusion.32 = bf16[192,2,4,128]{3,0,2,1:T(8,128)(2,1)} fusion(bf16[6144,2,128,1]{0,2,3,1:T(8,128)(2,1)} %bitcast.104, f32[2,6144,192,4]{1,2,3,0:T(8,128)} %get-tuple-element.6, f32[2,4,192]{2,1,0:T(4,128)S(1)} %broadcast_maximum_fusion, pred[192,6144]{1,0:T(8,128)(4,1)S(1)} %copy.68, f32[192,2,4]{0,2,1:T(4,128)S(1)} %bitcast.110), kind=kOutput, calls=%fused_computation.27 | convolution fusion | flops 2463498240 | bytes 42479616 | tf_op jit(solution)/shard_map/kgqr,rkd->kgqd/dot_general | solution.py:55
  203.6 1.3 copy.74
  204.9 0.3 convert_element_type.57
  205.2 2.4 fusion.35
  207.5 0.7 copy-done.1
  208.3 0.2 fusion.37
  208.4 0.4 broadcast_in_dim.55
  208.9 1.2 reshape.154
  210.1 2.9 convolution_convert_fusion
  213.0 4.0 all-to-all-start
  217.0 48.8 %all-gather.10.cloned.1.call-done = bf16[1,1024,1792]{2,1,0:T(8,128)(2,1)} async-done(((bf16[1,32,1792]{2,1,0:T(8,128)(2,1)}), bf16[1,1024,1792]{2,1,0:T(8,128)(2,1)}) %all-gather.10.cloned.1.call-update) | async-done | bytes 3670032 | tf_op jit(solution)/shard_map/all_gather | solution.py:85
  265.8 6.7 %fusion.8 = f32[576,1792]{1,0:T(8,128)} fusion(bf16[576,1024]{1,0:T(8,128)(2,1)S(1)} %bitcast.106, bf16[1,1024,1792]{2,1,0:T(8,128)(2,1)} %all-gather.10.cloned.1.call-done), kind=kOutput, calls=%fused_computation.11 | convolution fusion | flops 2113929216 | bytes 8978432 | tf_op jit(solution)/shard_map/esd,edf->esf/dot_general | solution.py:87
  272.5 77.9 %all-gather.12.cloned.1.call-done = bf16[1,1024,1792]{2,1,0:T(8,128)(2,1)} async-done(((bf16[1,32,1792]{2,1,0:T(8,128)(2,1)}), bf16[1,1024,1792]{2,1,0:T(8,128)(2,1)}) %all-gather.12.cloned.1.call-update) | async-done | bytes 3670032 | tf_op jit(solution)/shard_map/all_gather | solution.py:92
  350.3 84.4 %all-gather.8.cloned.1.call-done = bf16[1,1024,1792]{2,1,0:T(8,128)(2,1)} async-done(((bf16[1,32,1792]{2,1,0:T(8,128)(2,1)}), bf16[1,1024,1792]{2,1,0:T(8,128)(2,1)}) %all-gather.8.cloned.1.call-update) | async-done | bytes 3670032 | tf_op jit(solution)/shard_map/all_gather | solution.py:84
  434.7 9.2 %fusion.21 = bf16[1,576,1024]{2,1,0:T(8,128)(2,1)S(1)} fusion(bf16[1,1024,1792]{2,1,0:T(8,128)(2,1)} %all-gather.12.cloned.1.call-done, f32[576,1792]{1,0:T(8,128)} %fusion.8, bf16[576,1024]{1,0:T(8,128)(2,1)} %bitcast.107, bf16[1,1024,1792]{2,1,0:T(8,128)(2,1)} %all-gather.8.cloned.1.call-done), kind=kOutput, calls=%fused_computation.19 | convolution fusion | flops 4234641408 | bytes 13828096 | tf_op jit(solution)/shard_map/esf,edf->esd/dot_general | solution.py:89
  444.0 3.2 copy.99
  447.2 0.5 broadcast.107
  447.7 9.0 %reduce.4 = bf16[576,1024]{1,0:T(8,128)(2,1)S(1)} reduce(bf16[576,1,1024]{2,1,0:T(2,128)(2,1)} %bitcast.101, bf16[]{:T(256)} %broadcast.107), dimensions={1}, to_apply=%bitcast.98.reduce_sub_computation | reduce | bytes 2359298
  456.7 1.6 reshape.178
  458.3 4.0 all-to-all-start.1
  462.6 0.1 mul.96
  462.9 0.2 copy.78
  463.2 16.4 %all-to-all-done.1 = bf16[8,2,36864]{2,1,0:T(2,128)(2,1)S(1)} async-done(((bf16[8,2,36864]{2,1,0:T(2,128)(2,1)}), bf16[8,2,36864]{2,1,0:T(2,128)(2,1)S(1)}, u32[]{:S(2)}, u32[]{:S(2)}) %all-to-all-start.1) | async-done | bytes 1179680 | tf_op jit(solution)/shard_map/all_to_all | solution.py:95
  479.6 3.6 reshape.179
  483.1 2.1 copy.97
  485.2 2.7 gather_fusion
  487.9 2.1 gather.7
  490.1 3.1 multiply_reduce_fusion
  493.2 1.8 fusion.41
  (35 shorter events, 1.2 us)
Async XLA Ops:
  7.2 198.0 %copy-start = (bf16[1024,1024]{1,0:T(8,128)(2,1)S(1)}, bf16[1024,1024]{1,0:T(8,128)(2,1)}, u32[]{:S(2)}) copy-start(bf16[1024,1024]{1,0:T(8,128)(2,1)} %param.17) | copy-start | bytes 6291460
  7.2 91.1 %all-gather.14.cloned.1.call-start = ((), (), s32[]{:S(2)}) async-start(), calls=%async_computation.5 | async-start | bytes 3244032 | tf_op jit(solution)/shard_map/all_gather | solution.py:41
  7.9 173.3 %all-gather.16.cloned.1.call-start = ((), (), s32[]{:S(2)}) async-start(), calls=%async_computation.6 | async-start | bytes 3244032 | tf_op jit(solution)/shard_map/all_gather | solution.py:42
  8.7 257.1 %all-gather.10.cloned.1.call-start = ((), (), s32[]{:S(2)}) async-start(), calls=%async_computation.3 | async-start | bytes 3784704 | tf_op jit(solution)/shard_map/all_gather | solution.py:85
  9.4 340.9 %all-gather.12.cloned.1.call-start = ((), (), s32[]{:S(2)}) async-start(), calls=%async_computation.4 | async-start | bytes 3784704 | tf_op jit(solution)/shard_map/all_gather | solution.py:92
  10.0 424.8 %all-gather.8.cloned.1.call-start = ((), (), s32[]{:S(2)}) async-start(), calls=%async_computation.2 | async-start | bytes 3784704 | tf_op jit(solution)/shard_map/all_gather | solution.py:84
  203.6 4.7 copy-start.4
  207.5 0.7 copy-start.1
  213.0 52.8 %all-to-all-start = ((bf16[8,72,1024]{2,1,0:T(8,128)(2,1)}), bf16[8,72,1024]{2,1,0:T(8,128)(2,1)S(1)}, u32[]{:S(2)}, u32[]{:S(2)}) async-start(bf16[8,72,1024]{2,1,0:T(8,128)(2,1)} %bitcast.108), calls=%async_computation | async-start | bytes 2359296 | tf_op jit(solution)/shard_map/all_to_all | solution.py:83
  265.8 6.7 %copy-start.2 = (bf16[8,72,1024]{2,1,0:T(8,128)(2,1)}, bf16[8,72,1024]{2,1,0:T(8,128)(2,1)S(1)}, u32[]{:S(2)}) copy-start(bf16[8,72,1024]{2,1,0:T(8,128)(2,1)S(1)} %all-to-all-done) | copy-start | bytes 3538948
  447.7 14.7 %copy-start.3 = (s32[1,192,2]{1,2,0:T(2,128)S(1)}, s32[1,192,2]{1,2,0:T(2,128)}, u32[]{:S(2)}) copy-start(s32[1,192,2]{1,2,0:T(2,128)} %param.22) | copy-start | bytes 4612
  447.7 15.3 %copy-start.5 = (f32[1,192,2]{1,2,0:T(2,128)S(1)}, f32[1,192,2]{1,2,0:T(2,128)}, u32[]{:S(2)}) copy-start(f32[1,192,2]{1,2,0:T(2,128)} %param.23) | copy-start | bytes 4612
  458.3 21.3 %all-to-all-start.1 = ((bf16[8,2,36864]{2,1,0:T(2,128)(2,1)}), bf16[8,2,36864]{2,1,0:T(2,128)(2,1)S(1)}, u32[]{:S(2)}, u32[]{:S(2)}) async-start(bf16[8,2,36864]{2,1,0:T(2,128)(2,1)} %reshape.178), calls=%async_computation.1 | async-start | bytes 2359296 | tf_op jit(solution)/shard_map/all_to_all | solution.py:95
Sparse Core Ops, SparseCore 0:
  10.8 87.4 all-gather.13
  101.1 80.0 all-gather.15
  184.0 81.7 all-gather.9
  268.4 81.8 all-gather.11
  352.9 81.7 all-gather.7
where the time goes:
time: 503 us; the launch traced here: 502 us
  waiting for transfers between devices  351 us (70%)
  matrix products  55.9 us (11%)
  local copies, waits for them, and re-layouts  38.5 us (8%)
  other arithmetic  34.5 us (7%)
  between operations  14 us (3%)
  starting transfers between devices  8.18 us (2%)
    all_gather x1, waiting for transfers between devices, shards(): gate_piece = lax.all_gather(gate_weight, 'ctx', axis=1, tiled=True)  84.4 us
    all_gather x1, waiting for transfers between devices, shards(): lax.all_gather(down_weight, 'ctx', axis=1, tiled=True)  77.9 us
    all_gather x1, waiting for transfers between devices, shards(): key_piece = lax.all_gather(key_proj[0], 'ctx', axis=0, tiled=True)  77.4 us
    all_gather x1, waiting for transfers between devices, shards(): up_piece = lax.all_gather(up_weight, 'ctx', axis=1, tiled=True)  48.8 us
    all_gather x1, waiting for transfers between devices, shards(): value_piece = lax.all_gather(value_proj[0], 'ctx', axis=0, tiled=True)  42.6 us
    reduce_sum x1, other arithmetic, shards(): denominator = jnp.sum(weights, axis=-1, keepdims=True)  18.6 us
    dot_general x1, matrix products, shards(): jnp.einsum('kgqr,rkd->kgqd', weights.astype(jnp.bfloat16), value_heads, p...  17.7 us
    dot_general x1, matrix products, shards(): jnp.einsum('qkgd,rkd->kgqr', query_heads, key_heads, preferred_element_ty...  17 us
  transfers between devices with their start and end apart: 7, of which 6 were waited for; matrix products, arithmetic and copies ran while one was open for 18% of the time, Pallas kernels for 0%

commit v1 on v0

--- a/solution.py
+++ b/solution.py
@@ -38,8 +38,12 @@
     head_size = D // HEADS
     query_heads = query_rows.reshape(row_count, KV_HEADS, groups, head_size)
     mask_block = tile_mask[0]
-    key_piece = lax.all_gather(key_proj[0], "ctx", axis=0, tiled=True)
-    value_piece = lax.all_gather(value_proj[0], "ctx", axis=0, tiled=True)
+    kv_width = key_proj.shape[-1]
+    kv_piece = lax.all_gather(
+        jnp.concatenate([key_proj[0], value_proj[0]], axis=-1), "ctx", axis=0, tiled=True
+    )
+    key_piece = kv_piece[:, :kv_width]
+    value_piece = kv_piece[:, kv_width:]
     piece_rows = key_piece.shape[0]
     running_max = jnp.full((KV_HEADS, groups, row_count, 1), -1e30, jnp.float32)
     allowed = jnp.repeat(jnp.repeat(mask_block, TILE, axis=0), TILE, axis=1) > 0
@@ -81,15 +85,20 @@
         .reshape(EXPERTS, CAP, D)
     )
     arrived = lax.all_to_all(outgoing, "exp", split_axis=0, concat_axis=1, tiled=True)
-    gate_piece = lax.all_gather(gate_weight, "ctx", axis=1, tiled=True)
-    up_piece = lax.all_gather(up_weight, "ctx", axis=1, tiled=True)
+    ff = gate_weight.shape[-1]
+    weight_piece = lax.all_gather(
+        jnp.concatenate([gate_weight, up_weight, down_weight], axis=-1), "ctx", axis=1, tiled=True
+    )
+    gate_piece = weight_piece[..., :ff]
+    up_piece = weight_piece[..., ff : 2 * ff]
+    down_piece = weight_piece[..., 2 * ff :]
     gate_sum = jnp.einsum("esd,edf->esf", arrived, gate_piece, preferred_element_type=jnp.float32)
     up_sum = jnp.einsum("esd,edf->esf", arrived, up_piece, preferred_element_type=jnp.float32)
     hidden = (jax.nn.silu(gate_sum) * up_sum).astype(jnp.bfloat16)
     expert_rows = jnp.einsum(
         "esf,edf->esd",
         hidden,
-        lax.all_gather(down_weight, "ctx", axis=1, tiled=True),
+        down_piece,
         preferred_element_type=jnp.float32,
     ).astype(jnp.bfloat16)
     returned = lax.all_to_all(expert_rows, "exp", split_axis=1, concat_axis=0, tiled=True)

time: 503 us -> 303 us (0.60)
  waiting for transfers between devices: 351 us -> 118 us
  blocking collectives: 0 us -> 21.7 us
  local copies, waits for them, and re-layouts: 38.5 us -> 44.4 us
    all_gather x5 -> x2, waiting for transfers between devices: 331 us -> 102 us  [the longest x1 88.9 us: shards(): lax.all_gather(jnp.concatenate([key_proj[0], value_proj[0]], axis=-1), 'c...]
    all_to_all x0 -> x1, blocking collectives: none -> 21.7 us  [shards(): lax.all_to_all(outgoing, 'exp', split_axis=0, concat_axis=1, tiled=True)]
    unnamed x18 -> x20, local copies, waits for them, and re-layouts: 9.3 us -> 18.7 us
    all_gather x2 -> x0, local copies, waits for them, and re-layouts: 9.33 us -> none  [the longest x1 4.67 us: shards(): value_piece = lax.all_gather(value_proj[0], 'ctx', axis=0, tiled=True)]
    all_to_all x1, starting transfers between devices: 3.99 us -> 10.1 us  [shards(): lax.all_to_all(expert_rows, 'exp', split_axis=1, concat_axis=0, tiled=True)]
    slice x1 -> x2, local copies, waits for them, and re-layouts: 0.21 us -> 6.12 us  [the longest x1 5.9 us: shards(): key_piece = kv_piece[:, :kv_width]]
  transfers between devices with their start and end apart: 7 -> 3, of which waited for: 6 -> 3; matrix products, arithmetic and copies ran while one was open for 18% -> 30% of each run, Pallas kernels for 0% -> 0%
where the time goes in v1:
time: 303 us; the launch traced here: 302 us
  waiting for transfers between devices  118 us (39%)
  matrix products  54.9 us (18%)
  local copies, waits for them, and re-layouts  44.4 us (15%)
  other arithmetic  38 us (13%)
  blocking collectives  21.7 us (7%)
  between operations  14.3 us (5%)
  starting transfers between devices  10.2 us (3%)
    all_gather x1, waiting for transfers between devices, shards(): lax.all_gather(jnp.concatenate([key_proj[0], value_proj[0]], axis=-1), 'c...  88.9 us
    all_to_all x1, blocking collectives, shards(): lax.all_to_all(outgoing, 'exp', split_axis=0, concat_axis=1, tiled=True)  21.7 us
    unnamed x20, local copies, waits for them, and re-layouts  18.7 us
    reduce_sum x1, other arithmetic, shards(): denominator = jnp.sum(weights, axis=-1, keepdims=True)  18.6 us
    dot_general x1, matrix products, shards(): jnp.einsum('kgqr,rkd->kgqd', weights.astype(jnp.bfloat16), value_heads, p...  18 us
    dot_general x1, matrix products, shards(): jnp.einsum('qkgd,rkd->kgqr', query_heads, key_heads, preferred_element_ty...  17.1 us
    all_to_all x1, waiting for transfers between devices, shards(): lax.all_to_all(expert_rows, 'exp', split_axis=1, concat_axis=0, tiled=True)  16.4 us
    all_gather x1, waiting for transfers between devices, shards(): lax.all_gather(jnp.concatenate([gate_weight, up_weight, down_weight], axi...  12.9 us
  transfers between devices with their start and end apart: 3, of which 3 were waited for; matrix products, arithmetic and copies ran while one was open for 30% of the time, Pallas kernels for 0%

profile of v1, /device:TPU:1, one launch (start us, length us, event | category | flops | bytes accessed | tf_op | source)
XLA Modules:
  0.0 301.6 jit_solution(6274974701964415556)
XLA Ops:
  7.2 1.8 pad_maximum_fusion.1
  9.1 1.8 pad_maximum_fusion
  10.9 0.8 copy.75
  11.7 0.1 eq.39
  11.8 0.1 reshape_squeeze.7
  12.0 0.7 broadcast_compare_fusion
  12.7 0.1 copy.67
  12.8 1.6 broadcast_in_dim.48
  14.4 3.6 %copy.68 = pred[192,6144]{1,0:T(8,128)(4,1)S(1)} copy(pred[192,6144]{0,1:T(8,128)(4,1)} %bitcast.105) | data formatting | bytes 2359296 | tf_op jit(solution)/shard_map/gt | solution.py:49
  18.0 2.0 reshape_squeeze.6
  20.0 0.8 reduce-window.6
  20.9 0.2 slice_reduce_fusion
  21.2 88.9 %all-gather.3.cloned.1.call-done = bf16[6144,512]{1,0:T(8,128)(2,1)} async-done(((bf16[192,512]{1,0:T(8,128)(2,1)}), bf16[6144,512]{1,0:T(8,128)(2,1)}) %all-gather.3.cloned.1.call-update) | async-done | bytes 6291472 | tf_op jit(solution)/shard_map/all_gather | solution.py:42
  110.2 5.9 %fusion.38 = (bf16[6144,256]{1,0:T(8,128)(2,1)}, bf16[6144,256]{1,0:T(8,128)(2,1)}) fusion(bf16[6144,512]{1,0:T(8,128)(2,1)} %all-gather.3.cloned.1.call-done), kind=kLoop, calls=%fused_computation.64 | loop fusion | bytes 12582912 | tf_op jit(solution)/shard_map/slice | solution.py:45
  116.1 4.7 %copy.91 = bf16[6144,256]{0,1:T(8,128)(2,1)} copy(bf16[6144,256]{1,0:T(8,128)(2,1)} %get-tuple-element.5) | data formatting | bytes 6291456
  120.8 4.7 %copy.90 = bf16[6144,256]{0,1:T(8,128)(2,1)} copy(bf16[6144,256]{1,0:T(8,128)(2,1)} %get-tuple-element.4) | data formatting | bytes 6291456
  125.5 17.1 %fusion = (f32[2,4,192]{2,1,0:T(4,128)S(1)}, f32[2,6144,192,4]{1,2,3,0:T(8,128)}) fusion(pred[192,6144]{1,0:T(8,128)(4,1)S(1)} %copy.68, bf16[6144,2,128,1]{0,2,3,1:T(8,128)(2,1)} %bitcast.107, bf16[192,2,4,128]{3,2,1,0:T(4,128)(2,1)} %reshape_squeeze.6), kind=kOutput, calls=%fused_computation.3 | convolution fusion | flops 2444229120 | bytes 42473472 | tf_op jit(solution)/shard_map/qkgd,rkd->kgqr/dot_general | solution.py:52
  142.6 18.6 %fusion.1 = f32[2,4,192]{2,1,0:T(4,128)S(1)} fusion(f32[2,6144,192,4]{1,2,3,0:T(8,128)} %get-tuple-element.8, f32[2,4,192]{2,1,0:T(4,128)S(1)} %broadcast_maximum_fusion, pred[192,6144]{1,0:T(8,128)(4,1)S(1)} %copy.68), kind=kLoop, calls=%fused_computation.4 | loop fusion | flops 47184384 | bytes 38940672 | tf_op jit(solution)/shard_map/reduce_sum | solution.py:58
  161.2 18.0 %fusion.17 = bf16[192,2,4,128]{3,0,2,1:T(8,128)(2,1)} fusion(bf16[6144,2,128,1]{0,2,3,1:T(8,128)(2,1)} %bitcast.106, f32[2,6144,192,4]{1,2,3,0:T(8,128)} %get-tuple-element.8, f32[2,4,192]{2,1,0:T(4,128)S(1)} %broadcast_maximum_fusion, pred[192,6144]{1,0:T(8,128)(4,1)S(1)} %copy.68, f32[192,2,4]{0,2,1:T(4,128)S(1)} %bitcast.114), kind=kOutput, calls=%fused_computation.27 | convolution fusion | flops 2463498240 | bytes 42479616 | tf_op jit(solution)/shard_map/kgqr,rkd->kgqd/dot_general | solution.py:59
  179.1 1.3 copy.74
  180.5 0.3 convert_element_type.57
  180.7 2.4 fusion.20
  183.1 0.7 copy-done.1
  183.9 0.2 fusion.22
  184.0 0.4 broadcast_in_dim.55
  184.4 1.2 reshape.154
  185.6 1.9 convolution_convert_fusion
  187.5 21.7 %all_to_all.8 = bf16[8,72,1024]{2,1,0:T(8,128)(2,1)S(1)} all-to-all(bf16[8,72,1024]{2,1,0:T(8,128)(2,1)S(1)} %bitcast.110), channel_id=1, replica_groups=mesh['ctx'=32,'exp'=8] {'exp'}, dimensions={0} | all-to-all | bytes 2359296 | tf_op jit(solution)/shard_map/all_to_all | solution.py:87
  209.2 12.9 %all-gather.5.cloned.1.call-done = bf16[1,1024,5376]{2,1,0:T(8,128)(2,1)} async-done(((bf16[1,32,5376]{2,1,0:T(8,128)(2,1)}), bf16[1,1024,5376]{2,1,0:T(8,128)(2,1)}) %all-gather.5.cloned.1.call-update) | async-done | bytes 11010064 | tf_op jit(solution)/shard_map/all_gather | solution.py:89
  222.1 6.3 %fusion.7 = f32[576,1792]{1,0:T(8,128)} fusion(bf16[576,1024]{1,0:T(8,128)(2,1)S(1)} %bitcast.108, bf16[1,1024,5376]{2,1,0:T(8,128)(2,1)} %all-gather.5.cloned.1.call-done), kind=kOutput, calls=%fused_computation.12 | convolution fusion | flops 2113929216 | bytes 8978432 | tf_op jit(solution)/shard_map/esd,edf->esf/dot_general | solution.py:96
  228.4 9.3 %fusion.10 = bf16[1,576,1024]{2,1,0:T(8,128)(2,1)S(1)} fusion(bf16[1,1024,5376]{2,1,0:T(8,128)(2,1)} %all-gather.5.cloned.1.call-done, f32[576,1792]{1,0:T(8,128)} %fusion.7, bf16[576,1024]{1,0:T(8,128)(2,1)} %bitcast.109), kind=kOutput, calls=%fused_computation.19 | convolution fusion | flops 4234641408 | bytes 13828096 | tf_op jit(solution)/shard_map/esf,edf->esd/dot_general | solution.py:98
  237.6 3.2 %copy.101 = bf16[1,576,1024]{2,0,1:T(2,128)(2,1)} copy(bf16[1,576,1024]{2,1,0:T(8,128)(2,1)S(1)} %fusion.10) | data formatting | bytes 2359296 | tf_op jit(solution)/shard_map/convert_element_type | solution.py:103
  240.9 0.5 broadcast.107
  241.4 9.0 %reduce.4 = bf16[576,1024]{1,0:T(8,128)(2,1)S(1)} reduce(bf16[576,1,1024]{2,1,0:T(2,128)(2,1)} %bitcast.103, bf16[]{:T(256)} %broadcast.107), dimensions={1}, to_apply=%bitcast.100.reduce_sub_computation | reduce | bytes 2359298
  250.4 1.6 reshape.174
  252.0 10.1 %all-to-all-start.1 = ((bf16[8,2,36864]{2,1,0:T(2,128)(2,1)}), bf16[8,2,36864]{2,1,0:T(2,128)(2,1)S(1)}, u32[]{:S(2)}, u32[]{:S(2)}) async-start(bf16[8,2,36864]{2,1,0:T(2,128)(2,1)} %reshape.174), calls=%async_computation.1 | async-start | bytes 2359296 | tf_op jit(solution)/shard_map/all_to_all | solution.py:104
  262.1 0.1 reduce_sum.42
  262.2 0.1 copy.80
  262.3 0.1 mul.96
  262.6 0.2 copy.78
  262.8 0.1 copy.81
  262.9 16.4 %all-to-all-done.1 = bf16[8,2,36864]{2,1,0:T(2,128)(2,1)S(1)} async-done(((bf16[8,2,36864]{2,1,0:T(2,128)(2,1)}), bf16[8,2,36864]{2,1,0:T(2,128)(2,1)S(1)}, u32[]{:S(2)}, u32[]{:S(2)}) %all-to-all-start.1) | async-done | bytes 1179680 | tf_op jit(solution)/shard_map/all_to_all | solution.py:104
  279.3 3.6 %reshape.175 = bf16[576,1,1024]{2,1,0:T(2,128)(2,1)} reshape(bf16[8,2,36864]{2,1,0:T(2,128)(2,1)S(1)} %all-to-all-done.1) | data formatting | bytes 2359296
  282.9 2.1 copy.99
  285.0 2.7 gather_fusion
  287.7 2.1 gather.7
  289.8 3.1 %multiply_reduce_fusion = f32[192,1024]{1,0:T(8,128)S(1)} fusion(bf16[192,2,1024]{2,1,0:T(2,128)(2,1)S(1)} %gather.7, pred[192,2]{1,0:T(8,128)(4,1)S(1)} %copy.78, f32[192,2]{1,0:T(8,128)S(1)} %copy.81), kind=kLoop, calls=%fused_computation.15 | loop fusion | flops 1376256 | bytes 1574784 | tf_op jit(solution)/shard_map/reduce_sum | solution.py:106
  293.0 1.8 fusion.26
  (28 shorter events, 0.4 us)
Async XLA Ops:
  7.2 173.6 %copy-start = (bf16[1024,1024]{1,0:T(8,128)(2,1)S(1)}, bf16[1024,1024]{1,0:T(8,128)(2,1)}, u32[]{:S(2)}) copy-start(bf16[1024,1024]{1,0:T(8,128)(2,1)} %param.17) | copy-start | bytes 6291460
  7.2 103.0 %all-gather.3.cloned.1.call-start = ((), (), s32[]{:S(2)}) async-start(), calls=%async_computation.2 | async-start | bytes 6488064 | tf_op jit(solution)/shard_map/all_gather | solution.py:42
  9.0 213.1 %all-gather.5.cloned.1.call-start = ((), (), s32[]{:S(2)}) async-start(), calls=%async_computation.3 | async-start | bytes 11354112 | tf_op jit(solution)/shard_map/all_gather | solution.py:89
  179.1 4.7 %copy-start.4 = (f32[1024]{0:T(1024)S(1)}, f32[1024]{0:T(1024)}, u32[]{:S(2)}) copy-start(f32[1024]{0:T(1024)} %param.18) | copy-start | bytes 12292
  183.1 0.7 copy-start.1
  209.2 12.9 %copy-start.2 = (bf16[8,72,1024]{2,1,0:T(8,128)(2,1)}, bf16[8,72,1024]{2,1,0:T(8,128)(2,1)S(1)}, u32[]{:S(2)}) copy-start(bf16[8,72,1024]{2,1,0:T(8,128)(2,1)S(1)} %all_to_all.8) | copy-start | bytes 3538948
  241.4 20.8 %copy-start.3 = (s32[1,192,2]{1,2,0:T(2,128)S(1)}, s32[1,192,2]{1,2,0:T(2,128)}, u32[]{:S(2)}) copy-start(s32[1,192,2]{1,2,0:T(2,128)} %param.22) | copy-start | bytes 4612
  241.4 21.4 %copy-start.5 = (f32[1,192,2]{1,2,0:T(2,128)S(1)}, f32[1,192,2]{1,2,0:T(2,128)}, u32[]{:S(2)}) copy-start(f32[1,192,2]{1,2,0:T(2,128)} %param.23) | copy-start | bytes 4612
  252.0 27.4 %all-to-all-start.1 = ((bf16[8,2,36864]{2,1,0:T(2,128)(2,1)}), bf16[8,2,36864]{2,1,0:T(2,128)(2,1)S(1)}, u32[]{:S(2)}, u32[]{:S(2)}) async-start(bf16[8,2,36864]{2,1,0:T(2,128)(2,1)} %reshape.174), calls=%async_computation.1 | async-start | bytes 2359296 | tf_op jit(solution)/shard_map/all_to_all | solution.py:104
Sparse Core Ops, SparseCore 0:
  11.4 98.7 all-gather.2
  113.0 109.0 all-gather.4

commit v2 on v1

--- a/solution.py
+++ b/solution.py
@@ -16,6 +16,15 @@
     widened = row_block.astype(jnp.float32)
     inverse = lax.rsqrt(jnp.mean(widened * widened, axis=-1, keepdims=True) + 1e-05)
     return widened * inverse * gain
+
+
+CTX_AXES = ("z", "yh", "core")
+
+
+def gather_ctx(block, axis):
+    for name in reversed(CTX_AXES):
+        block = lax.all_gather(block, name, axis=axis, tiled=True)
+    return block
 
 
 def shards(
@@ -39,9 +48,7 @@
     query_heads = query_rows.reshape(row_count, KV_HEADS, groups, head_size)
     mask_block = tile_mask[0]
     kv_width = key_proj.shape[-1]
-    kv_piece = lax.all_gather(
-        jnp.concatenate([key_proj[0], value_proj[0]], axis=-1), "ctx", axis=0, tiled=True
-    )
+    kv_piece = gather_ctx(jnp.concatenate([key_proj[0], value_proj[0]], axis=-1), 0)
     key_piece = kv_piece[:, :kv_width]
     value_piece = kv_piece[:, kv_width:]
     piece_rows = key_piece.shape[0]
@@ -86,9 +93,7 @@
     )
     arrived = lax.all_to_all(outgoing, "exp", split_axis=0, concat_axis=1, tiled=True)
     ff = gate_weight.shape[-1]
-    weight_piece = lax.all_gather(
-        jnp.concatenate([gate_weight, up_weight, down_weight], axis=-1), "ctx", axis=1, tiled=True
-    )
+    weight_piece = gather_ctx(jnp.concatenate([gate_weight, up_weight, down_weight], axis=-1), 1)
     gate_piece = weight_piece[..., :ff]
     up_piece = weight_piece[..., ff : 2 * ff]
     down_piece = weight_piece[..., 2 * ff :]
@@ -109,23 +114,27 @@
 
 
 def solution(mesh):
+    n_ctx = mesh.shape["ctx"]
+    split = jax.sharding.Mesh(
+        mesh.devices.reshape(n_ctx // 4, 2, 2, mesh.shape["exp"]), CTX_AXES + ("exp",)
+    )
     return jax.shard_map(
         shards,
-        mesh=mesh,
+        mesh=split,
         in_specs=(
-            P("exp", "ctx", None),
-            P("exp", "ctx", None),
-            P("exp", "ctx", None),
-            P("exp", "ctx", None),
-            P("exp", "ctx", None),
+            P("exp", CTX_AXES, None),
+            P("exp", CTX_AXES, None),
+            P("exp", CTX_AXES, None),
+            P("exp", CTX_AXES, None),
+            P("exp", CTX_AXES, None),
             P(),
             P(),
-            P("exp", "ctx", None),
-            P("exp", "ctx", None),
-            P("exp", "ctx", None),
-            P("exp", "ctx", None),
-            P("exp", "ctx", None),
+            P("exp", CTX_AXES, None),
+            P("exp", CTX_AXES, None),
+            P("exp", CTX_AXES, None),
+            P("exp", CTX_AXES, None),
+            P("exp", CTX_AXES, None),
         ),
-        out_specs=(P("exp", "ctx", None), P("exp", "ctx", None)),
+        out_specs=(P("exp", CTX_AXES, None), P("exp", CTX_AXES, None)),
         check_vma=False,
     )

time: 303 us -> 317 us (1.046)
  blocking collectives: 21.7 us -> 40.8 us
  waiting for transfers between devices: 118 us -> 133 us
  local copies, waits for them, and re-layouts: 44.4 us -> 33.7 us
  starting transfers between devices: 10.2 us -> 5.01 us
    all_gather x0 -> x3, blocking collectives: none -> 20 us  [gather_ctx(): block = lax.all_gather(block, name, axis=axis, tiled=True)]
    all_gather x2 -> x3, waiting for transfers between devices: 102 us -> 116 us  [gather_ctx(): block = lax.all_gather(block, name, axis=axis, tiled=True)]
    unnamed x20, local copies, waits for them, and re-layouts: 18.7 us -> 8.63 us
    all_to_all x1, starting transfers between devices: 10.1 us -> 4.88 us  [shards(): lax.all_to_all(expert_rows, 'exp', split_axis=1, concat_axis=0, tiled=True)]
  transfers between devices with their start and end apart: 3 -> 4, of which waited for: 3 -> 4; matrix products, arithmetic and copies ran while one was open for 30% -> 24% of each run, Pallas kernels for 0% -> 0%
where the time goes in v2:
time: 317 us; the launch traced here: 316 us
  waiting for transfers between devices  133 us (42%)
  matrix products  53.4 us (17%)
  blocking collectives  40.8 us (13%)
  other arithmetic  36 us (11%)
  local copies, waits for them, and re-layouts  33.7 us (11%)
  between operations  14 us (4%)
  starting transfers between devices  5.01 us (2%)
    all_gather x3, waiting for transfers between devices, gather_ctx(): block = lax.all_gather(block, name, axis=axis, tiled=True)  116 us
    all_to_all x1, blocking collectives, shards(): lax.all_to_all(outgoing, 'exp', split_axis=0, concat_axis=1, tiled=True)  20.8 us
    all_gather x3, blocking collectives, gather_ctx(): block = lax.all_gather(block, name, axis=axis, tiled=True)  20 us
    reduce_sum x1, other arithmetic, shards(): denominator = jnp.sum(weights, axis=-1, keepdims=True)  18.7 us
    dot_general x1, matrix products, shards(): jnp.einsum('kgqr,rkd->kgqd', weights.astype(jnp.bfloat16), value_heads, p...  18 us
    all_to_all x1, waiting for transfers between devices, shards(): lax.all_to_all(expert_rows, 'exp', split_axis=1, concat_axis=0, tiled=True)  16.3 us
    dot_general x1, matrix products, shards(): jnp.einsum('qkgd,rkd->kgqr', query_heads, key_heads, preferred_element_ty...  15.6 us
    dot_general x1, matrix products, shards(): jnp.einsum('esf,edf->esd', hidden, down_piece, preferred_element_type=jnp...  9.26 us
  transfers between devices with their start and end apart: 4, of which 4 were waited for; matrix products, arithmetic and copies ran while one was open for 24% of the time, Pallas kernels for 0%

profile of v2, /device:TPU:1, one launch (start us, length us, event | category | flops | bytes accessed | tf_op | source)
XLA Modules:
  0.0 315.7 jit_solution(3074867281685239616)
XLA Ops:
  7.2 1.2 pad_maximum_fusion
  8.4 5.3 %all_gather.21 = bf16[1,64,5376]{2,1,0:T(8,128)(2,1)} all-gather(bf16[1,32,5376]{2,1,0:T(8,128)(2,1)S(1)} %pad_maximum_fusion), channel_id=1, replica_groups=mesh['z'=8,'yh'=2,'core'=2,'exp'=8] {'core'}, dimensions={1}, use_global_device_ids=true | all-gather | bytes 1032192 | tf_op jit(solution)/shard_map/all_gather | solution.py:26
  13.8 1.0 pad_maximum_fusion.1
  14.8 2.1 all_gather.18
  16.8 0.2 copy.67
  17.1 12.6 %all_gather.19 = bf16[768,512]{0,1:T(8,128)(2,1)} all-gather(bf16[384,512]{0,1:T(8,128)(2,1)S(1)} %copy.67), channel_id=1, replica_groups=mesh['z'=8,'yh'=2,'core'=2,'exp'=8] {'yh'}, dimensions={0}, use_global_device_ids=true | all-gather | bytes 1179648 | tf_op jit(solution)/shard_map/all_gather | solution.py:26
  29.8 16.7 %all-gather.6.cloned.1.call-done = bf16[1,128,5376]{2,1,0:T(8,128)(2,1)} async-done(((bf16[1,64,5376]{2,1,0:T(8,128)(2,1)}), bf16[1,128,5376]{2,1,0:T(8,128)(2,1)}) %all-gather.6.cloned.1.call-update) | async-done | bytes 1376272 | tf_op jit(solution)/shard_map/all_gather | solution.py:26
  46.5 0.1 copy.72
  46.6 0.1 eq.39
  46.7 0.1 reshape_squeeze.7
  47.0 0.1 copy.65
  47.1 1.6 broadcast_in_dim.48
  48.7 3.6 %copy.66 = pred[192,6144]{1,0:T(8,128)(4,1)S(1)} copy(pred[192,6144]{0,1:T(8,128)(4,1)} %bitcast.105) | data formatting | bytes 2359296 | tf_op jit(solution)/shard_map/gt | solution.py:56
  52.3 2.0 reshape_squeeze.6
  54.3 0.8 reduce-window.6
  55.1 0.2 slice_reduce_fusion
  55.5 67.1 %all-gather.4.cloned.1.call-done = bf16[6144,512]{0,1:T(8,128)(2,1)} async-done(((bf16[768,512]{0,1:T(8,128)(2,1)}), bf16[6144,512]{0,1:T(8,128)(2,1)}) %all-gather.4.cloned.1.call-update) | async-done | bytes 6291472 | tf_op jit(solution)/shard_map/all_gather | solution.py:26
  122.6 5.0 %fusion.38 = (bf16[6144,256]{0,1:T(8,128)(2,1)S(1)}, bf16[6144,256]{0,1:T(8,128)(2,1)}) fusion(bf16[6144,512]{0,1:T(8,128)(2,1)} %all-gather.4.cloned.1.call-done), kind=kLoop, calls=%fused_computation.64 | loop fusion | bytes 12582912 | tf_op jit(solution)/shard_map/slice | solution.py:52
  127.6 15.6 %fusion = (f32[2,4,192]{2,1,0:T(4,128)S(1)}, f32[2,6144,192,4]{1,2,3,0:T(8,128)}) fusion(pred[192,6144]{1,0:T(8,128)(4,1)S(1)} %copy.66, bf16[6144,2,128,1]{0,2,3,1:T(8,128)(2,1)S(1)} %bitcast.107, bf16[192,2,4,128]{3,2,1,0:T(4,128)(2,1)} %reshape_squeeze.6), kind=kOutput, calls=%fused_computation.3 | convolution fusion | flops 2444229120 | bytes 42473472 | tf_op jit(solution)/shard_map/qkgd,rkd->kgqr/dot_general | solution.py:59
  143.2 18.7 %fusion.1 = f32[2,4,192]{2,1,0:T(4,128)S(1)} fusion(f32[2,6144,192,4]{1,2,3,0:T(8,128)} %get-tuple-element.8, f32[2,4,192]{2,1,0:T(4,128)S(1)} %broadcast_maximum_fusion, pred[192,6144]{1,0:T(8,128)(4,1)S(1)} %copy.66), kind=kLoop, calls=%fused_computation.4 | loop fusion | flops 47184384 | bytes 38940672 | tf_op jit(solution)/shard_map/reduce_sum | solution.py:65
  161.9 18.0 %fusion.17 = bf16[192,2,4,128]{3,0,2,1:T(8,128)(2,1)} fusion(bf16[6144,2,128,1]{0,2,3,1:T(8,128)(2,1)} %bitcast.106, f32[2,6144,192,4]{1,2,3,0:T(8,128)} %get-tuple-element.8, f32[2,4,192]{2,1,0:T(4,128)S(1)} %broadcast_maximum_fusion, pred[192,6144]{1,0:T(8,128)(4,1)S(1)} %copy.66, f32[192,2,4]{0,2,1:T(4,128)S(1)} %bitcast.114), kind=kOutput, calls=%fused_computation.27 | convolution fusion | flops 2463498240 | bytes 42479616 | tf_op jit(solution)/shard_map/kgqr,rkd->kgqd/dot_general | solution.py:66
  179.9 1.3 copy.71
  181.2 0.3 convert_element_type.57
  181.5 2.4 fusion.20
  183.9 0.7 copy-done.1
  184.6 0.2 fusion.22
  184.8 0.4 broadcast_in_dim.55
  185.2 1.2 reshape.154
  186.4 1.9 convolution_convert_fusion
  188.3 20.8 %all_to_all.8 = bf16[8,72,1024]{2,1,0:T(8,128)(2,1)S(1)} all-to-all(bf16[8,72,1024]{2,1,0:T(8,128)(2,1)S(1)} %bitcast.110), channel_id=1, replica_groups=mesh['z'=8,'yh'=2,'core'=2,'exp'=8] {'exp'}, dimensions={0} | all-to-all | bytes 2359296 | tf_op jit(solution)/shard_map/all_to_all | solution.py:94
  209.1 32.6 %all-gather.8.cloned.1.call-done = bf16[1,1024,5376]{2,1,0:T(8,128)(2,1)} async-done(((bf16[1,128,5376]{2,1,0:T(8,128)(2,1)}), bf16[1,1024,5376]{2,1,0:T(8,128)(2,1)}) %all-gather.8.cloned.1.call-update) | async-done | bytes 11010064 | tf_op jit(solution)/shard_map/all_gather | solution.py:26
  241.8 6.3 %fusion.7 = f32[576,1792]{1,0:T(8,128)} fusion(bf16[576,1024]{1,0:T(8,128)(2,1)S(1)} %bitcast.108, bf16[1,1024,5376]{2,1,0:T(8,128)(2,1)} %all-gather.8.cloned.1.call-done), kind=kOutput, calls=%fused_computation.12 | convolution fusion | flops 2113929216 | bytes 8978432 | tf_op jit(solution)/shard_map/esd,edf->esf/dot_general | solution.py:101
  248.0 9.3 %fusion.10 = bf16[1,576,1024]{2,1,0:T(8,128)(2,1)S(1)} fusion(bf16[1,1024,5376]{2,1,0:T(8,128)(2,1)} %all-gather.8.cloned.1.call-done, f32[576,1792]{1,0:T(8,128)} %fusion.7, bf16[576,1024]{1,0:T(8,128)(2,1)} %bitcast.109), kind=kOutput, calls=%fused_computation.19 | convolution fusion | flops 4234641408 | bytes 13828096 | tf_op jit(solution)/shard_map/esf,edf->esd/dot_general | solution.py:103
  257.3 3.2 %copy.96 = bf16[1,576,1024]{2,0,1:T(2,128)(2,1)} copy(bf16[1,576,1024]{2,1,0:T(8,128)(2,1)S(1)} %fusion.10) | data formatting | bytes 2359296 | tf_op jit(solution)/shard_map/convert_element_type | solution.py:108
  260.5 0.5 broadcast.107
  261.0 9.0 %reduce.4 = bf16[576,1024]{1,0:T(8,128)(2,1)S(1)} reduce(bf16[576,1,1024]{2,1,0:T(2,128)(2,1)} %bitcast.103, bf16[]{:T(256)} %broadcast.107), dimensions={1}, to_apply=%bitcast.100.reduce_sub_computation | reduce | bytes 2359298
  270.0 1.6 reshape.174
  271.6 4.9 %all-to-all-start.1 = ((bf16[8,2,36864]{2,1,0:T(2,128)(2,1)}), bf16[8,2,36864]{2,1,0:T(2,128)(2,1)S(1)}, u32[]{:S(2)}, u32[]{:S(2)}) async-start(bf16[8,2,36864]{2,1,0:T(2,128)(2,1)} %reshape.174), calls=%async_computation.1 | async-start | bytes 2359296 | tf_op jit(solution)/shard_map/all_to_all | solution.py:109
  276.5 0.1 reduce_sum.42
  276.8 0.1 mul.96
  277.0 0.2 copy.75
  277.4 16.3 %all-to-all-done.1 = bf16[8,2,36864]{2,1,0:T(2,128)(2,1)S(1)} async-done(((bf16[8,2,36864]{2,1,0:T(2,128)(2,1)}), bf16[8,2,36864]{2,1,0:T(2,128)(2,1)S(1)}, u32[]{:S(2)}, u32[]{:S(2)}) %all-to-all-start.1) | async-done | bytes 1179680 | tf_op jit(solution)/shard_map/all_to_all | solution.py:109
  293.7 3.6 %reshape.175 = bf16[576,1,1024]{2,1,0:T(2,128)(2,1)} reshape(bf16[8,2,36864]{2,1,0:T(2,128)(2,1)S(1)} %all-to-all-done.1) | data formatting | bytes 2359296
  297.2 2.1 copy.94
  299.3 2.7 gather_fusion
  302.0 2.1 gather.7
  304.2 3.1 multiply_reduce_fusion
  307.3 1.8 fusion.26
  (35 shorter events, 0.7 us)
Async XLA Ops:
  7.2 174.3 %copy-start = (bf16[1024,1024]{1,0:T(8,128)(2,1)S(1)}, bf16[1024,1024]{1,0:T(8,128)(2,1)}, u32[]{:S(2)}) copy-start(bf16[1024,1024]{1,0:T(8,128)(2,1)} %param.17) | copy-start | bytes 6291460
  7.2 39.3 %copy-start.3 = (s32[1,192,2]{1,2,0:T(2,128)S(1)}, s32[1,192,2]{1,2,0:T(2,128)}, u32[]{:S(2)}) copy-start(s32[1,192,2]{1,2,0:T(2,128)} %param.22) | copy-start | bytes 4612
  7.2 39.7 %copy-start.4 = (s32[1,6,192]{2,0,1:T(1,128)S(1)}, s32[1,6,192]{2,0,1:T(1,128)}, u32[]{:S(2)}) copy-start(s32[1,6,192]{2,0,1:T(1,128)} %param.16) | copy-start | bytes 13828
  7.2 39.2 %all-gather.6.cloned.1.call-start = ((), (), s32[]{:S(2)}) async-start(), calls=%async_computation.3 | async-start | bytes 2064384 | tf_op jit(solution)/shard_map/all_gather | solution.py:26
  13.7 108.9 %all-gather.4.cloned.1.call-start = ((), (), s32[]{:S(2)}) async-start(), calls=%async_computation.2 | async-start | bytes 7077888 | tf_op jit(solution)/shard_map/all_gather | solution.py:26
  29.7 212.0 %all-gather.8.cloned.1.call-start = ((), (), s32[]{:S(2)}) async-start(), calls=%async_computation.4 | async-start | bytes 12386304 | tf_op jit(solution)/shard_map/all_gather | solution.py:26
  179.9 4.7 %copy-start.5 = (f32[1024]{0:T(1024)S(1)}, f32[1024]{0:T(1024)}, u32[]{:S(2)}) copy-start(f32[1024]{0:T(1024)} %param.18) | copy-start | bytes 12292
  183.9 0.7 copy-start.1
  209.1 32.6 %copy-start.2 = (bf16[8,72,1024]{2,1,0:T(8,128)(2,1)}, bf16[8,72,1024]{2,1,0:T(8,128)(2,1)S(1)}, u32[]{:S(2)}) copy-start(bf16[8,72,1024]{2,1,0:T(8,128)(2,1)S(1)} %all_to_all.8) | copy-start | bytes 3538948
  261.0 16.2 %copy-start.6 = (f32[1,192,2]{1,2,0:T(2,128)S(1)}, f32[1,192,2]{1,2,0:T(2,128)}, u32[]{:S(2)}) copy-start(f32[1,192,2]{1,2,0:T(2,128)} %param.23) | copy-start | bytes 4612
  271.6 22.1 %all-to-all-start.1 = ((bf16[8,2,36864]{2,1,0:T(2,128)(2,1)}), bf16[8,2,36864]{2,1,0:T(2,128)(2,1)S(1)}, u32[]{:S(2)}, u32[]{:S(2)}) async-start(bf16[8,2,36864]{2,1,0:T(2,128)(2,1)} %reshape.174), calls=%async_computation.1 | async-start | bytes 2359296 | tf_op jit(solution)/shard_map/all_to_all | solution.py:109
Sparse Core Ops, SparseCore 0:
  13.9 32.5 all-gather.5
  48.2 74.3 all-gather.3
  124.4 117.3 all-gather.7

commit v3 on v2

--- a/solution.py
+++ b/solution.py
@@ -1,6 +1,10 @@
+import functools
+
 import jax
 import jax.numpy as jnp
 from jax import lax
+from jax.experimental import pallas as pl
+from jax.experimental.pallas import tpu as pltpu
 from jax.sharding import PartitionSpec as P
 
 D = 1024
@@ -21,10 +25,99 @@
 CTX_AXES = ("z", "yh", "core")
 
 
-def gather_ctx(block, axis):
-    for name in reversed(CTX_AXES):
-        block = lax.all_gather(block, name, axis=axis, tiled=True)
-    return block
+MESH = pl.DeviceIdType.MESH
+
+
+def gather_kernel(n_z, shard_ref, out_ref, local_sem, send_sem, recv_sem):
+    z = lax.axis_index("z")
+    yh = lax.axis_index("yh")
+    core = lax.axis_index("core")
+    ex = lax.axis_index("exp")
+
+    def slot(zz, hh, cc):
+        return (zz * 2 + hh) * 2 + cc
+
+    def ring(offset):
+        return lax.rem(z + offset + 4 * n_z, n_z)
+
+    partner_h = 1 - yh
+    sibling_c = 1 - core
+    to_right = (ring(1), yh, core, ex)
+    to_left = (ring(-1), yh, core, ex)
+    to_partner = (z, partner_h, core, ex)
+    to_sibling = (z, yh, sibling_c, ex)
+    barrier = pltpu.get_barrier_semaphore()
+    for dev in (to_right, to_left, to_partner, to_sibling):
+        pl.semaphore_signal(barrier, 1, device_id=dev, device_id_type=MESH)
+    pl.semaphore_wait(barrier, 4)
+
+    me = slot(z, yh, core)
+    own = pltpu.make_async_copy(shard_ref, out_ref.at[me], local_sem)
+    own.start()
+    sends = []
+
+    def send(src, s, dev, k):
+        copy = pltpu.make_async_remote_copy(
+            src, out_ref.at[s], send_sem.at[k, s], recv_sem.at[s], device_id=dev, device_id_type=MESH
+        )
+        copy.start()
+        sends.append(copy)
+
+    def arrive(s):
+        pltpu.make_async_remote_copy(
+            out_ref.at[s], out_ref.at[s], send_sem.at[0, s], recv_sem.at[s],
+            device_id=to_right, device_id_type=MESH,
+        ).wait_recv()
+
+    for k, dev in enumerate((to_right, to_left, to_partner, to_sibling)):
+        send(shard_ref, me, dev, k)
+    half = n_z // 2
+    for t in range(1, half + 1):
+        s = slot(ring(-t), yh, core)
+        arrive(s)
+        if t < half:
+            send(out_ref.at[s], s, to_right, 0)
+        send(out_ref.at[s], s, to_partner, 2)
+        send(out_ref.at[s], s, to_sibling, 3)
+        if t < n_z - half:
+            s = slot(ring(t), yh, core)
+            arrive(s)
+            if t < n_z - half - 1:
+                send(out_ref.at[s], s, to_left, 1)
+            send(out_ref.at[s], s, to_partner, 2)
+            send(out_ref.at[s], s, to_sibling, 3)
+    partner_order = [0]
+    for t in range(1, half + 1):
+        partner_order.append(-t)
+        if t < n_z - half:
+            partner_order.append(t)
+    for offset in partner_order:
+        s = slot(ring(offset), partner_h, core)
+        arrive(s)
+        send(out_ref.at[s], s, to_sibling, 3)
+    for hh in (yh, partner_h):
+        for offset in partner_order:
+            arrive(slot(ring(offset), hh, sibling_c))
+    own.wait()
+    for copy in sends:
+        copy.wait_send()
+
+
+def gather_ctx_kernel(block):
+    n_z = lax.axis_size("z")
+    n_all = n_z * 4
+    return pl.pallas_call(
+        functools.partial(gather_kernel, n_z),
+        out_shape=jax.ShapeDtypeStruct((n_all,) + block.shape, block.dtype),
+        in_specs=[pl.BlockSpec(memory_space=pl.ANY)],
+        out_specs=pl.BlockSpec(memory_space=pl.ANY),
+        scratch_shapes=[
+            pltpu.SemaphoreType.DMA(()),
+            pltpu.SemaphoreType.DMA((4, n_all)),
+            pltpu.SemaphoreType.DMA((n_all,)),
+        ],
+        compiler_params=pltpu.CompilerParams(collective_id=0, has_side_effects=True),
+    )(block)
 
 
 def shards(
@@ -48,7 +141,8 @@
     query_heads = query_rows.reshape(row_count, KV_HEADS, groups, head_size)
     mask_block = tile_mask[0]
     kv_width = key_proj.shape[-1]
-    kv_piece = gather_ctx(jnp.concatenate([key_proj[0], value_proj[0]], axis=-1), 0)
+    kv_local = jnp.concatenate([key_proj[0], value_proj[0]], axis=-1)
+    kv_piece = gather_ctx_kernel(kv_local).reshape(-1, 2 * kv_width)
     key_piece = kv_piece[:, :kv_width]
     value_piece = kv_piece[:, kv_width:]
     piece_rows = key_piece.shape[0]
@@ -93,7 +187,9 @@
     )
     arrived = lax.all_to_all(outgoing, "exp", split_axis=0, concat_axis=1, tiled=True)
     ff = gate_weight.shape[-1]
-    weight_piece = gather_ctx(jnp.concatenate([gate_weight, up_weight, down_weight], axis=-1), 1)
+    weight_piece = lax.all_gather(
+        jnp.concatenate([gate_weight, up_weight, down_weight], axis=-1), CTX_AXES, axis=1, tiled=True
+    )
     gate_piece = weight_piece[..., :ff]
     up_piece = weight_piece[..., ff : 2 * ff]
     down_piece = weight_piece[..., 2 * ff :]

time: 317 us -> 247 us (0.78)
  waiting for transfers between devices: 133 us -> 16.3 us
  Pallas kernels: 0 us -> 52.6 us
  blocking collectives: 40.8 us -> 21 us
  local copies, waits for them, and re-layouts: 33.7 us -> 45.7 us
    all_gather x3 -> x1, waiting for transfers between devices: 116 us -> 0.01 us  [shards(): lax.all_gather(jnp.concatenate([gate_weight, up_weight, down_weight], axi...]
    pallas_call x0 -> x1, Pallas kernels: none -> 52.6 us  [gather_ctx_kernel(): pl.pallas_call(functools.partial(gather_kernel, n_z), out_shape=jax.Shape...]
    all_gather x3 -> x0, blocking collectives: 20 us -> none  [gather_ctx(): block = lax.all_gather(block, name, axis=axis, tiled=True)]
    unnamed x20 -> x22, local copies, waits for them, and re-layouts: 8.63 us -> 20 us
  transfers between devices with their start and end apart: 4 -> 2, of which waited for: 4 -> 1; matrix products, arithmetic and copies ran while one was open for 24% -> 36% of each run, Pallas kernels for 0% -> 21%
where the time goes in v3:
time: 247 us; the launch traced here: 246 us
  matrix products  54.9 us (22%)
  Pallas kernels  52.6 us (21%)
  local copies, waits for them, and re-layouts  45.7 us (19%)
  other arithmetic  37.7 us (15%)
  blocking collectives  21 us (9%)
  waiting for transfers between devices  16.3 us (7%)
  between operations  14.3 us (6%)
  starting transfers between devices  3.6 us (1%)
    pallas_call x1, Pallas kernels, gather_ctx_kernel(): pl.pallas_call(functools.partial(gather_kernel, n_z), out_shape=jax.Shape...  52.6 us
    all_to_all x1, blocking collectives, shards(): lax.all_to_all(outgoing, 'exp', split_axis=0, concat_axis=1, tiled=True)  21 us
    unnamed x22, local copies, waits for them, and re-layouts  20 us
    reduce_sum x1, other arithmetic, shards(): denominator = jnp.sum(weights, axis=-1, keepdims=True)  18.9 us
    dot_general x1, matrix products, shards(): jnp.einsum('kgqr,rkd->kgqd', weights.astype(jnp.bfloat16), value_heads, p...  17.9 us
    dot_general x1, matrix products, shards(): jnp.einsum('qkgd,rkd->kgqr', query_heads, key_heads, preferred_element_ty...  17.2 us
    all_to_all x1, waiting for transfers between devices, shards(): lax.all_to_all(expert_rows, 'exp', split_axis=1, concat_axis=0, tiled=True)  16.3 us
    dot_general x1, matrix products, shards(): jnp.einsum('esf,edf->esd', hidden, down_piece, preferred_element_type=jnp...  9.25 us
  transfers between devices with their start and end apart: 2, of which 1 were waited for; matrix products, arithmetic and copies ran while one was open for 36% of the time, Pallas kernels for 21%

profile of v3, /device:TPU:1, one launch (start us, length us, event | category | flops | bytes accessed | tf_op | source)
XLA Modules:
  0.0 246.0 jit_solution(4019198312632270184)
XLA Ops:
  7.2 1.9 pad_maximum_fusion
  9.2 0.8 copy.75
  10.0 0.1 eq.39
  10.1 0.1 reshape_squeeze.7
  10.2 1.6 pad_maximum_fusion.1.shard_ref
  11.9 52.6 %shard_map.131 = bf16[32,192,512]{2,1,0:T(8,128)(2,1)} custom-call(bf16[192,512]{1,0:T(8,128)(2,1)} %pad_maximum_fusion.1.shard_ref), custom_call_target="tpu_custom_call" | custom-call | tf_op jit(solution)/shard_map/pallas_call | solution.py:109
  64.5 5.9 %fusion.38 = (bf16[6144,256]{1,0:T(8,128)(2,1)}, bf16[6144,256]{1,0:T(8,128)(2,1)}) fusion(bf16[6144,512]{1,0:T(8,128)(2,1)} %bitcast.104), kind=kLoop, calls=%fused_computation.64 | loop fusion | bytes 12582912 | tf_op jit(solution)/shard_map/slice | solution.py:146
  70.4 5.0 %copy.91 = bf16[6144,256]{0,1:T(8,128)(2,1)} copy(bf16[6144,256]{1,0:T(8,128)(2,1)} %get-tuple-element.5) | data formatting | bytes 6291456
  75.4 0.1 copy.67
  75.6 1.6 broadcast_in_dim.48
  77.1 3.6 %copy.68 = pred[192,6144]{1,0:T(8,128)(4,1)S(1)} copy(pred[192,6144]{0,1:T(8,128)(4,1)} %bitcast.107) | data formatting | bytes 2359296 | tf_op jit(solution)/shard_map/gt | solution.py:150
  80.8 4.7 %copy.90 = bf16[6144,256]{0,1:T(8,128)(2,1)} copy(bf16[6144,256]{1,0:T(8,128)(2,1)} %get-tuple-element.4) | data formatting | bytes 6291456
  85.4 2.0 reshape_squeeze.6
  87.4 17.2 %fusion = (f32[2,4,192]{2,1,0:T(4,128)S(1)}, f32[2,6144,192,4]{1,2,3,0:T(8,128)}) fusion(pred[192,6144]{1,0:T(8,128)(4,1)S(1)} %copy.68, bf16[6144,2,128,1]{0,2,3,1:T(8,128)(2,1)} %bitcast.109, bf16[192,2,4,128]{3,2,1,0:T(4,128)(2,1)} %reshape_squeeze.6), kind=kOutput, calls=%fused_computation.3 | convolution fusion | flops 2444229120 | bytes 42473472 | tf_op jit(solution)/shard_map/qkgd,rkd->kgqr/dot_general | solution.py:153
  104.7 18.9 %fusion.1 = f32[2,4,192]{2,1,0:T(4,128)S(1)} fusion(f32[2,6144,192,4]{1,2,3,0:T(8,128)} %get-tuple-element.8, f32[2,4,192]{2,1,0:T(4,128)S(1)} %broadcast_maximum_fusion, pred[192,6144]{1,0:T(8,128)(4,1)S(1)} %copy.68), kind=kLoop, calls=%fused_computation.4 | loop fusion | flops 47184384 | bytes 38940672 | tf_op jit(solution)/shard_map/reduce_sum | solution.py:159
  123.6 17.9 %fusion.17 = bf16[192,2,4,128]{3,0,2,1:T(8,128)(2,1)} fusion(bf16[6144,2,128,1]{0,2,3,1:T(8,128)(2,1)} %bitcast.108, f32[2,6144,192,4]{1,2,3,0:T(8,128)} %get-tuple-element.8, f32[2,4,192]{2,1,0:T(4,128)S(1)} %broadcast_maximum_fusion, pred[192,6144]{1,0:T(8,128)(4,1)S(1)} %copy.68, f32[192,2,4]{0,2,1:T(4,128)S(1)} %bitcast.116), kind=kOutput, calls=%fused_computation.27 | convolution fusion | flops 2463498240 | bytes 42479616 | tf_op jit(solution)/shard_map/kgqr,rkd->kgqd/dot_general | solution.py:160
  141.5 1.3 copy.74
  142.8 0.3 convert_element_type.57
  143.1 2.4 fusion.20
  145.5 0.7 copy-done.1
  146.2 0.2 fusion.22
  146.4 0.4 broadcast_in_dim.55
  146.8 1.2 reshape.158
  148.0 0.8 reduce-window.6
  148.8 0.2 slice_reduce_fusion
  149.1 0.1 fusion.30
  149.2 1.9 convolution_convert_fusion
  151.1 21.0 %all_to_all.8 = bf16[8,72,1024]{2,1,0:T(8,128)(2,1)S(1)} all-to-all(bf16[8,72,1024]{2,1,0:T(8,128)(2,1)S(1)} %bitcast.112), channel_id=1, replica_groups=mesh['z'=8,'yh'=2,'core'=2,'exp'=8] {'exp'}, dimensions={0} | all-to-all | bytes 2359296 | tf_op jit(solution)/shard_map/all_to_all | solution.py:188
  172.1 1.0 copy-done.2
  173.1 6.3 %fusion.7 = f32[576,1792]{1,0:T(8,128)} fusion(bf16[576,1024]{1,0:T(8,128)(2,1)S(1)} %bitcast.110, bf16[1,1024,5376]{2,1,0:T(8,128)(2,1)} %all-gather.2.cloned.1.call-done), kind=kOutput, calls=%fused_computation.12 | convolution fusion | flops 2113929216 | bytes 8978432 | tf_op jit(solution)/shard_map/esd,edf->esf/dot_general | solution.py:197
  179.4 9.3 %fusion.10 = bf16[1,576,1024]{2,1,0:T(8,128)(2,1)S(1)} fusion(bf16[1,1024,5376]{2,1,0:T(8,128)(2,1)} %all-gather.2.cloned.1.call-done, f32[576,1792]{1,0:T(8,128)} %fusion.7, bf16[576,1024]{1,0:T(8,128)(2,1)} %bitcast.111), kind=kOutput, calls=%fused_computation.19 | convolution fusion | flops 4234641408 | bytes 13828096 | tf_op jit(solution)/shard_map/esf,edf->esd/dot_general | solution.py:199
  188.7 3.2 %copy.101 = bf16[1,576,1024]{2,0,1:T(2,128)(2,1)} copy(bf16[1,576,1024]{2,1,0:T(8,128)(2,1)S(1)} %fusion.10) | data formatting | bytes 2359296 | tf_op jit(solution)/shard_map/convert_element_type | solution.py:204
  191.9 0.5 broadcast.107
  192.4 9.0 %reduce.4 = bf16[576,1024]{1,0:T(8,128)(2,1)S(1)} reduce(bf16[576,1,1024]{2,1,0:T(2,128)(2,1)} %bitcast.105, bf16[]{:T(256)} %broadcast.107), dimensions={1}, to_apply=%bitcast.101.reduce_sub_computation | reduce | bytes 2359298
  201.4 1.6 reshape.178
  203.0 3.6 %all-to-all-start.1 = ((bf16[8,2,36864]{2,1,0:T(2,128)(2,1)}), bf16[8,2,36864]{2,1,0:T(2,128)(2,1)S(1)}, u32[]{:S(2)}, u32[]{:S(2)}) async-start(bf16[8,2,36864]{2,1,0:T(2,128)(2,1)} %reshape.178), calls=%async_computation.1 | async-start | bytes 2359296 | tf_op jit(solution)/shard_map/all_to_all | solution.py:205
  206.6 0.1 reduce_sum.42
  206.7 0.1 copy.80
  206.9 0.1 mul.96
  207.1 0.2 copy.78
  207.3 0.1 copy.81
  207.4 16.3 %all-to-all-done.1 = bf16[8,2,36864]{2,1,0:T(2,128)(2,1)S(1)} async-done(((bf16[8,2,36864]{2,1,0:T(2,128)(2,1)}), bf16[8,2,36864]{2,1,0:T(2,128)(2,1)S(1)}, u32[]{:S(2)}, u32[]{:S(2)}) %all-to-all-start.1) | async-done | bytes 1179680 | tf_op jit(solution)/shard_map/all_to_all | solution.py:205
  223.7 3.6 %reshape.179 = bf16[576,1,1024]{2,1,0:T(2,128)(2,1)} reshape(bf16[8,2,36864]{2,1,0:T(2,128)(2,1)S(1)} %all-to-all-done.1) | data formatting | bytes 2359296
  227.3 2.1 copy.99
  229.4 2.7 %gather_fusion = bf16[384,1024]{1,0:T(8,128)(2,1)} fusion(bf16[576,1024]{1,0:T(8,128)(2,1)S(1)} %bitcast.103, s32[1024]{0:T(1024)S(1)} %pad_clamp_fusion), kind=kCustom, calls=%fused_computation | custom fusion | bytes 1574400 | tf_op jit(solution)/shard_map/jit(_take)/gather | solution.py:206
  232.1 2.1 gather.7
  234.2 3.1 %multiply_reduce_fusion = f32[192,1024]{1,0:T(8,128)S(1)} fusion(bf16[192,2,1024]{2,1,0:T(2,128)(2,1)S(1)} %gather.7, pred[192,2]{1,0:T(8,128)(4,1)S(1)} %copy.78, f32[192,2]{1,0:T(8,128)S(1)} %copy.81), kind=kLoop, calls=%fused_computation.15 | loop fusion | flops 1376256 | bytes 1574784 | tf_op jit(solution)/shard_map/reduce_sum | solution.py:207
  237.3 1.8 fusion.26
  (28 shorter events, 0.3 us)
Async XLA Ops:
  7.2 136.0 %copy-start = (bf16[1024,1024]{1,0:T(8,128)(2,1)S(1)}, bf16[1024,1024]{1,0:T(8,128)(2,1)}, u32[]{:S(2)}) copy-start(bf16[1024,1024]{1,0:T(8,128)(2,1)} %param.17) | copy-start | bytes 6291460
  7.2 164.9 %all-gather.2.cloned.1.call-start = ((), (), s32[]{:S(2)}) async-start(), calls=%async_computation.2 | async-start | bytes 11354112 | tf_op jit(solution)/shard_map/all_gather | solution.py:190
  70.4 5.0 %copy-start.4 = (s32[1,6,192]{2,0,1:T(1,128)S(1)}, s32[1,6,192]{2,0,1:T(1,128)}, u32[]{:S(2)}) copy-start(s32[1,6,192]{2,0,1:T(1,128)} %param.16) | copy-start | bytes 13828
  141.5 4.7 %copy-start.5 = (f32[1024]{0:T(1024)S(1)}, f32[1024]{0:T(1024)}, u32[]{:S(2)}) copy-start(f32[1024]{0:T(1024)} %param.18) | copy-start | bytes 12292
  145.5 0.7 copy-start.1
  172.1 1.0 copy-start.2
  192.4 14.3 %copy-start.3 = (s32[1,192,2]{1,2,0:T(2,128)S(1)}, s32[1,192,2]{1,2,0:T(2,128)}, u32[]{:S(2)}) copy-start(s32[1,192,2]{1,2,0:T(2,128)} %param.22) | copy-start | bytes 4612
  192.4 14.9 %copy-start.6 = (f32[1,192,2]{1,2,0:T(2,128)S(1)}, f32[1,192,2]{1,2,0:T(2,128)}, u32[]{:S(2)}) copy-start(f32[1,192,2]{1,2,0:T(2,128)} %param.23) | copy-start | bytes 4612
  203.0 20.7 %all-to-all-start.1 = ((bf16[8,2,36864]{2,1,0:T(2,128)(2,1)}), bf16[8,2,36864]{2,1,0:T(2,128)(2,1)S(1)}, u32[]{:S(2)}, u32[]{:S(2)}) async-start(bf16[8,2,36864]{2,1,0:T(2,128)(2,1)} %reshape.178), calls=%async_computation.1 | async-start | bytes 2359296 | tf_op jit(solution)/shard_map/all_to_all | solution.py:205
Sparse Core Ops, SparseCore 0:
  10.8 118.9 all-gather.1

commit v4 on v3

--- a/solution.py
+++ b/solution.py
@@ -120,6 +120,83 @@
     )(block)
 
 
+KEY_BLOCK = 128
+
+
+def attention_kernel(groups, head_size, flag_ref, q_ref, kv_ref, mask_ref, out_ref, top_ref, sum_ref, acc_ref):
+    n_blocks = flag_ref.shape[0]
+    kv_heads = kv_ref.shape[1] // (2 * head_size)
+    heads = kv_heads * groups
+    value_at = kv_heads * head_size
+    scale = head_size ** (-0.5)
+    top_ref[...] = jnp.full(top_ref.shape, -1e30, jnp.float32)
+    sum_ref[...] = jnp.zeros(sum_ref.shape, jnp.float32)
+    acc_ref[...] = jnp.zeros(acc_ref.shape, jnp.float32)
+
+    def scores(j, h):
+        rows = pl.ds(pl.multiple_of(j * KEY_BLOCK, KEY_BLOCK), KEY_BLOCK)
+        key = kv_ref[rows, pl.ds((h // groups) * head_size, head_size)]
+        query = q_ref[:, pl.ds(h * head_size, head_size)]
+        raw = lax.dot_general(
+            query, key, (((1,), (1,)), ((), ())), preferred_element_type=jnp.float32
+        )
+        return raw * scale, mask_ref[:, rows] > 0
+
+    def first_pass(j, carry):
+        @pl.when(flag_ref[j] > 0)
+        def _():
+            for h in range(heads):
+                s, allowed = scores(j, h)
+                top_ref[h] = jnp.maximum(top_ref[h], jnp.where(allowed, s, -1e30))
+        return carry
+
+    lax.fori_loop(0, n_blocks, first_pass, 0)
+    for h in range(heads):
+        top_ref[h] = jnp.broadcast_to(jnp.max(top_ref[h], axis=1, keepdims=True), top_ref.shape[1:])
+
+    def second_pass(j, carry):
+        @pl.when(flag_ref[j] > 0)
+        def _():
+            rows = pl.ds(pl.multiple_of(j * KEY_BLOCK, KEY_BLOCK), KEY_BLOCK)
+            for h in range(heads):
+                s, allowed = scores(j, h)
+                weights = jnp.where(allowed, jnp.exp(s - top_ref[h]), 0.0)
+                sum_ref[h] += weights
+                value = kv_ref[rows, pl.ds(value_at + (h // groups) * head_size, head_size)]
+                acc_ref[h] += jnp.dot(
+                    weights.astype(jnp.bfloat16), value, preferred_element_type=jnp.float32
+                )
+        return carry
+
+    lax.fori_loop(0, n_blocks, second_pass, 0)
+    for h in range(heads):
+        denominator = jnp.sum(sum_ref[h], axis=1, keepdims=True)
+        out_ref[:, pl.ds(h * head_size, head_size)] = (acc_ref[h] / denominator).astype(out_ref.dtype)
+
+
+def block_attention(query_rows, kv_rows, mask_block, groups, head_size):
+    row_count = query_rows.shape[0]
+    key_count = kv_rows.shape[0]
+    heads = query_rows.shape[1] // head_size
+    allowed = jnp.repeat(jnp.repeat(mask_block, TILE, axis=0), TILE, axis=1).astype(jnp.bfloat16)
+    tiles_per_block = KEY_BLOCK // TILE
+    flags = jnp.max(
+        mask_block.reshape(mask_block.shape[0], -1, tiles_per_block), axis=(0, 2)
+    ).astype(jnp.int32)
+    vmem = pl.BlockSpec(memory_space=pltpu.VMEM)
+    return pl.pallas_call(
+        functools.partial(attention_kernel, groups, head_size),
+        out_shape=jax.ShapeDtypeStruct((row_count, heads * head_size), jnp.bfloat16),
+        in_specs=[pl.BlockSpec(memory_space=pltpu.SMEM), vmem, vmem, vmem],
+        out_specs=vmem,
+        scratch_shapes=[
+            pltpu.VMEM((heads, row_count, KEY_BLOCK), jnp.float32),
+            pltpu.VMEM((heads, row_count, KEY_BLOCK), jnp.float32),
+            pltpu.VMEM((heads, row_count, head_size), jnp.float32),
+        ],
+    )(flags, query_rows, kv_rows, allowed)
+
+
 def shards(
     hidden_in,
     queries,
@@ -143,30 +220,7 @@
     kv_width = key_proj.shape[-1]
     kv_local = jnp.concatenate([key_proj[0], value_proj[0]], axis=-1)
     kv_piece = gather_ctx_kernel(kv_local).reshape(-1, 2 * kv_width)
-    key_piece = kv_piece[:, :kv_width]
-    value_piece = kv_piece[:, kv_width:]
-    piece_rows = key_piece.shape[0]
-    running_max = jnp.full((KV_HEADS, groups, row_count, 1), -1e30, jnp.float32)
-    allowed = jnp.repeat(jnp.repeat(mask_block, TILE, axis=0), TILE, axis=1) > 0
-    key_heads = key_piece.reshape(piece_rows, KV_HEADS, head_size)
-    value_heads = value_piece.reshape(piece_rows, KV_HEADS, head_size)
-    scores = jnp.einsum(
-        "qkgd,rkd->kgqr", query_heads, key_heads, preferred_element_type=jnp.float32
-    ) * head_size ** (-0.5)
-    scores = jnp.where(allowed, scores, -1e30)
-    newest_max = jnp.maximum(running_max, jnp.max(scores, axis=-1, keepdims=True))
-    weights = jnp.where(allowed, jnp.exp(scores - newest_max), 0.0)
-    denominator = jnp.sum(weights, axis=-1, keepdims=True)
-    accumulated = jnp.einsum(
-        "kgqr,rkd->kgqd",
-        weights.astype(jnp.bfloat16),
-        value_heads,
-        preferred_element_type=jnp.float32,
-    )
-    running_max, denominator, accumulated = (newest_max, denominator, accumulated)
-    attended = (
-        (accumulated / denominator).transpose(2, 0, 1, 3).reshape(row_count, D).astype(jnp.bfloat16)
-    )
+    attended = block_attention(query_rows, kv_piece, mask_block, groups, head_size)
     projected = jnp.dot(attended, out_weight, preferred_element_type=jnp.float32)
     attention_out = projected.astype(jnp.bfloat16)
     residual = (hidden_in[0].astype(jnp.float32) + projected).astype(jnp.bfloat16)

time: 247 us -> 204 us (0.83)
  matrix products: 54.9 us -> 19.9 us
  Pallas kernels: 52.6 us -> 75.3 us
  other arithmetic: 37.7 us -> 19.1 us
  local copies, waits for them, and re-layouts: 45.7 us -> 27.1 us
  waiting for transfers between devices: 16.3 us -> 19.5 us
    dot_general x2 -> x0, matrix products: 35.1 us -> none  [the longest x1 17.9 us: shards(): jnp.einsum('kgqr,rkd->kgqd', weights.astype(jnp.bfloat16), value_heads, p...]
    pallas_call x0 -> x1, Pallas kernels: none -> 22.7 us  [block_attention(): pl.pallas_call(functools.partial(attention_kernel, groups, head_size), ou...]
    reduce_sum x1 -> x0, other arithmetic: 18.9 us -> none  [shards(): denominator = jnp.sum(weights, axis=-1, keepdims=True)]
    unnamed x22, local copies, waits for them, and re-layouts: 20 us -> 9.32 us
    slice x2 -> x1, local copies, waits for them, and re-layouts: 6.13 us -> 0.21 us  [the longest x1 5.91 us: shards(): key_piece = kv_piece[:, :kv_width]]
    gt x2 -> x0, local copies, waits for them, and re-layouts: 3.76 us -> none  [shards(): allowed = jnp.repeat(jnp.repeat(mask_block, TILE, axis=0), TILE, axis=1) > 0]
    convert_element_type x2, local copies, waits for them, and re-layouts: 1.58 us -> 4.87 us  [block_attention(): jnp.repeat(jnp.repeat(mask_block, TILE, axis=0), TILE, axis=1)]
    all_gather x1, waiting for transfers between devices: 0.01 us -> 3.08 us  [shards(): lax.all_gather(jnp.concatenate([gate_weight, up_weight, down_weight], axi...]
  transfers between devices with their start and end apart: 2 -> 2, of which waited for: 1 -> 2; matrix products, arithmetic and copies ran while one was open for 36% -> 9% of each run, Pallas kernels for 21% -> 37%
where the time goes in v4:
time: 204 us; the launch traced here: 203 us
  Pallas kernels  75.3 us (37%)
  local copies, waits for them, and re-layouts  27.1 us (13%)
  blocking collectives  23.4 us (11%)
  matrix products  19.9 us (10%)
  waiting for transfers between devices  19.5 us (10%)
  other arithmetic  19.1 us (9%)
  between operations  14.3 us (7%)
  starting transfers between devices  4.02 us (2%)
    pallas_call x1, Pallas kernels, gather_ctx_kernel(): pl.pallas_call(functools.partial(gather_kernel, n_z), out_shape=jax.Shape...  52.6 us
    all_to_all x1, blocking collectives, shards(): lax.all_to_all(outgoing, 'exp', split_axis=0, concat_axis=1, tiled=True)  23.4 us
    pallas_call x1, Pallas kernels, block_attention(): pl.pallas_call(functools.partial(attention_kernel, groups, head_size), ou...  22.7 us
    all_to_all x1, waiting for transfers between devices, shards(): lax.all_to_all(expert_rows, 'exp', split_axis=1, concat_axis=0, tiled=True)  16.4 us
    unnamed x22, local copies, waits for them, and re-layouts  9.32 us
    dot_general x1, matrix products, shards(): jnp.einsum('esf,edf->esd', hidden, down_piece, preferred_element_type=jnp...  9.23 us
    unnamed x1, other arithmetic  8.96 us
    dot_general x1, matrix products, shards(): jnp.einsum('esd,edf->esf', arrived, up_piece, preferred_element_type=jnp....  6.38 us
  transfers between devices with their start and end apart: 2, of which 2 were waited for; matrix products, arithmetic and copies ran while one was open for 9% of the time, Pallas kernels for 37%

profile of v4, /device:TPU:1, one launch (start us, length us, event | category | flops | bytes accessed | tf_op | source)
XLA Modules:
  0.0 202.6 jit_solution(2485005870698258745)
XLA Ops:
  7.2 0.0 copy-start
  7.2 0.0 all-gather.2.cloned.1.call-start
  7.2 1.9 pad_maximum_fusion
  9.1 0.0 all-gather.2.cloned.1.call-update
  9.2 0.8 copy.44
  10.0 0.1 eq.39
  10.1 0.1 reshape_squeeze.4
  10.2 0.8 fusion.18
  11.0 0.1 reduce_max.14
  11.1 1.6 pad_maximum_fusion.1.shard_ref
  12.8 52.6 %shard_map.131 = bf16[32,192,512]{2,1,0:T(8,128)(2,1)} custom-call(bf16[192,512]{1,0:T(8,128)(2,1)} %pad_maximum_fusion.1.shard_ref), custom_call_target="tpu_custom_call" | custom-call | tf_op jit(solution)/shard_map/pallas_call | solution.py:109
  65.4 0.1 copy.42
  65.5 1.9 broadcast_in_dim.31
  67.4 4.8 %copy.43.mask_ref = bf16[192,6144]{1,0:T(8,128)(2,1)} copy(bf16[192,6144]{0,1:T(8,128)(2,1)} %bitcast.70) | data formatting | bytes 4718592 | tf_op jit(solution)/shard_map/convert_element_type | solution.py:181
  72.2 0.6 reduce_max.18.flag_ref
  72.8 22.7 %shard_map.132 = bf16[192,1024]{1,0:T(8,128)(2,1)} custom-call(s32[48]{0:T(128)} %reduce_max.18.flag_ref, bf16[192,1024]{1,0:T(8,128)(2,1)} %bitcast.76, bf16[6144,512]{1,0:T(8,128)(2,1)} %bitcast.69, bf16[192,6144]{1,0:T(8,128)(2,1)} %copy.43.mask_ref), custom_call_target="tpu_custom_call" | custom-call | tf_op jit(solution)/shard_map/pallas_call | solution.py:187
  95.4 2.4 %fusion.5 = (f32[192]{0:T(256)S(1)}, bf16[192,1024]{1,0:T(8,128)(2,1)S(1)}, bf16[1,192,1024]{2,1,0:T(8,128)(2,1)}) fusion(bf16[1,192,1024]{2,1,0:T(8,128)(2,1)S(1)} %copy-done.4, bf16[192,1024]{1,0:T(8,128)(2,1)} %shard_map.132, bf16[1024,1024]{1,0:T(8,128)(2,1)S(1)} %copy-done), kind=kOutput, calls=%fused_computation.18 | convolution fusion | flops 404029248 | bytes 3670784 | tf_op jit(solution)/shard_map/dot_general | solution.py:224
  97.8 0.7 copy-done.1
  98.6 0.2 fusion.7
  98.7 0.4 broadcast_in_dim.34
  99.1 1.2 reshape.141
  100.4 0.8 reduce-window.6
  101.2 0.2 slice_reduce_fusion
  101.5 0.1 fusion.13
  101.6 1.9 convolution_convert_fusion
  103.5 23.4 %all_to_all.8 = bf16[8,72,1024]{2,1,0:T(8,128)(2,1)S(1)} all-to-all(bf16[8,72,1024]{2,1,0:T(8,128)(2,1)S(1)} %bitcast.75), channel_id=1, replica_groups=mesh['z'=8,'yh'=2,'core'=2,'exp'=8] {'exp'}, dimensions={0} | all-to-all | bytes 2359296 | tf_op jit(solution)/shard_map/all_to_all | solution.py:242
  126.9 3.1 %all-gather.2.cloned.1.call-done = bf16[1,1024,5376]{2,1,0:T(8,128)(2,1)} async-done(((bf16[1,32,5376]{2,1,0:T(8,128)(2,1)}), bf16[1,1024,5376]{2,1,0:T(8,128)(2,1)}) %all-gather.2.cloned.1.call-update) | async-done | bytes 11010064 | tf_op jit(solution)/shard_map/all_gather | solution.py:244
  130.0 6.4 %fusion.1 = f32[576,1792]{1,0:T(8,128)} fusion(bf16[576,1024]{1,0:T(8,128)(2,1)S(1)} %bitcast.73, bf16[1,1024,5376]{2,1,0:T(8,128)(2,1)} %all-gather.2.cloned.1.call-done), kind=kOutput, calls=%fused_computation.5 | convolution fusion | flops 2113929216 | bytes 8978432 | tf_op jit(solution)/shard_map/esd,edf->esf/dot_general | solution.py:251
  136.4 9.2 %fusion.4 = bf16[1,576,1024]{2,1,0:T(8,128)(2,1)S(1)} fusion(bf16[1,1024,5376]{2,1,0:T(8,128)(2,1)} %all-gather.2.cloned.1.call-done, f32[576,1792]{1,0:T(8,128)} %fusion.1, bf16[576,1024]{1,0:T(8,128)(2,1)} %bitcast.74), kind=kOutput, calls=%fused_computation.12 | convolution fusion | flops 4234641408 | bytes 13828096 | tf_op jit(solution)/shard_map/esf,edf->esd/dot_general | solution.py:253
  145.6 3.2 %copy.58 = bf16[1,576,1024]{2,0,1:T(2,128)(2,1)} copy(bf16[1,576,1024]{2,1,0:T(8,128)(2,1)S(1)} %fusion.4) | data formatting | bytes 2359296 | tf_op jit(solution)/shard_map/convert_element_type | solution.py:258
  148.8 0.5 broadcast.91
  149.4 9.0 %reduce.6 = bf16[576,1024]{1,0:T(8,128)(2,1)S(1)} reduce(bf16[576,1,1024]{2,1,0:T(2,128)(2,1)} %bitcast.71, bf16[]{:T(256)} %broadcast.91), dimensions={1}, to_apply=%bitcast.66.reduce_sub_computation | reduce | bytes 2359298
  158.3 0.0 copy-start.5
  158.3 1.6 reshape.159
  159.9 4.0 %all-to-all-start.1 = ((bf16[8,2,36864]{2,1,0:T(2,128)(2,1)}), bf16[8,2,36864]{2,1,0:T(2,128)(2,1)S(1)}, u32[]{:S(2)}, u32[]{:S(2)}) async-start(bf16[8,2,36864]{2,1,0:T(2,128)(2,1)} %reshape.159), calls=%async_computation.1 | async-start | bytes 2359296 | tf_op jit(solution)/shard_map/all_to_all | solution.py:259
  163.9 0.1 reduce_sum.32
  164.1 0.1 copy.49
  164.2 0.1 mul.84
  164.4 0.1 copy.46
  164.5 0.2 copy.47
  164.6 0.1 copy.50
  164.8 16.4 %all-to-all-done.1 = bf16[8,2,36864]{2,1,0:T(2,128)(2,1)S(1)} async-done(((bf16[8,2,36864]{2,1,0:T(2,128)(2,1)}), bf16[8,2,36864]{2,1,0:T(2,128)(2,1)S(1)}, u32[]{:S(2)}, u32[]{:S(2)}) %all-to-all-start.1) | async-done | bytes 1179680 | tf_op jit(solution)/shard_map/all_to_all | solution.py:259
  181.2 3.6 %reshape.160 = bf16[576,1,1024]{2,1,0:T(2,128)(2,1)} reshape(bf16[8,2,36864]{2,1,0:T(2,128)(2,1)S(1)} %all-to-all-done.1) | data formatting | bytes 2359296
  184.7 2.1 %copy.56 = bf16[1,576,1024]{2,1,0:T(8,128)(2,1)S(1)} copy(bf16[1,576,1024]{2,0,1:T(2,128)(2,1)} %bitcast.72) | data formatting | bytes 2359296
  186.8 2.7 %gather_fusion = bf16[384,1024]{1,0:T(8,128)(2,1)} fusion(bf16[576,1024]{1,0:T(8,128)(2,1)S(1)} %bitcast.68, s32[1024]{0:T(1024)S(1)} %pad_clamp_fusion), kind=kCustom, calls=%fused_computation | custom fusion | bytes 1574400 | tf_op jit(solution)/shard_map/jit(_take)/gather | solution.py:260
  189.5 2.2 %gather.7 = bf16[192,2,1024]{2,1,0:T(2,128)(2,1)S(1)} reshape(bf16[384,1024]{1,0:T(8,128)(2,1)} %gather_fusion) | data formatting | bytes 1572864 | tf_op jit(solution)/shard_map/jit(_take)/gather | solution.py:260
  191.7 3.1 %multiply_reduce_fusion = f32[192,1024]{1,0:T(8,128)S(1)} fusion(bf16[192,2,1024]{2,1,0:T(2,128)(2,1)S(1)} %gather.7, pred[192,2]{1,0:T(8,128)(4,1)S(1)} %copy.47, f32[192,2]{1,0:T(8,128)S(1)} %copy.50), kind=kLoop, calls=%fused_computation.8 | loop fusion | flops 1376256 | bytes 1574784 | tf_op jit(solution)/shard_map/reduce_sum | solution.py:261
  194.9 0.8 fusion.11
  (23 shorter events, 0.1 us)
Async XLA Ops:
  7.2 88.3 %copy-start = (bf16[1024,1024]{1,0:T(8,128)(2,1)S(1)}, bf16[1024,1024]{1,0:T(8,128)(2,1)}, u32[]{:S(2)}) copy-start(bf16[1024,1024]{1,0:T(8,128)(2,1)} %param.17) | copy-start | bytes 6291460
  7.2 122.8 %all-gather.2.cloned.1.call-start = ((), (), s32[]{:S(2)}) async-start(), calls=%async_computation.2 | async-start | bytes 11354112 | tf_op jit(solution)/shard_map/all_gather | solution.py:244
  72.8 22.7 %copy-start.4 = (bf16[1,192,1024]{2,1,0:T(8,128)(2,1)S(1)}, bf16[1,192,1024]{2,1,0:T(8,128)(2,1)}, u32[]{:S(2)}) copy-start(bf16[1,192,1024]{2,1,0:T(8,128)(2,1)} %param.12) | copy-start | bytes 1179652
  95.4 3.1 %copy-start.6 = (f32[1024]{0:T(1024)S(1)}, f32[1024]{0:T(1024)}, u32[]{:S(2)}) copy-start(f32[1024]{0:T(1024)} %param.18) | copy-start | bytes 12292
  97.8 0.7 copy-start.1
  126.9 3.1 %copy-start.3 = (bf16[8,72,1024]{2,1,0:T(8,128)(2,1)}, bf16[8,72,1024]{2,1,0:T(8,128)(2,1)S(1)}, u32[]{:S(2)}) copy-start(bf16[8,72,1024]{2,1,0:T(8,128)(2,1)S(1)} %all_to_all.8) | copy-start | bytes 3538948
  158.3 5.7 %copy-start.5 = (s32[1,192,2]{1,2,0:T(2,128)S(1)}, s32[1,192,2]{1,2,0:T(2,128)}, u32[]{:S(2)}) copy-start(s32[1,192,2]{1,2,0:T(2,128)} %param.22) | copy-start | bytes 4612
  158.3 6.3 %copy-start.7 = (f32[1,192,2]{1,2,0:T(2,128)S(1)}, f32[1,192,2]{1,2,0:T(2,128)}, u32[]{:S(2)}) copy-start(f32[1,192,2]{1,2,0:T(2,128)} %param.23) | copy-start | bytes 4612
  159.9 21.3 %all-to-all-start.1 = ((bf16[8,2,36864]{2,1,0:T(2,128)(2,1)}), bf16[8,2,36864]{2,1,0:T(2,128)(2,1)S(1)}, u32[]{:S(2)}, u32[]{:S(2)}) async-start(bf16[8,2,36864]{2,1,0:T(2,128)(2,1)} %reshape.159), calls=%async_computation.1 | async-start | bytes 2359296 | tf_op jit(solution)/shard_map/all_to_all | solution.py:259
  189.5 5.3 %copy-start.2 = (bf16[192,1024]{1,0:T(8,128)(2,1)S(1)}, bf16[192,1024]{1,0:T(8,128)(2,1)}, u32[]{:S(2)}) copy-start(bf16[192,1024]{1,0:T(8,128)(2,1)} %copy-done.1) | copy-start | bytes 1179652
Sparse Core Ops, SparseCore 0:
  10.8 119.1 all-gather.1

commit v5 on v4

--- a/solution.py
+++ b/solution.py
@@ -118,6 +118,57 @@
         ],
         compiler_params=pltpu.CompilerParams(collective_id=0, has_side_effects=True),
     )(block)
+
+
+def exchange_kernel(n_exp, chunk_ref, out_ref, local_sem, send_sem, recv_sem):
+    me = lax.axis_index("exp")
+    z = lax.axis_index("z")
+    yh = lax.axis_index("yh")
+    core = lax.axis_index("core")
+
+    def peer(offset):
+        return lax.rem(me + offset, n_exp)
+
+    barrier = pltpu.get_barrier_semaphore()
+    for offset in range(1, n_exp):
+        pl.semaphore_signal(barrier, 1, device_id=(z, yh, core, peer(offset)), device_id_type=MESH)
+    pl.semaphore_wait(barrier, n_exp - 1)
+    own = pltpu.make_async_copy(chunk_ref.at[me], out_ref.at[me], local_sem)
+    own.start()
+    sends = []
+    for offset in range(1, n_exp):
+        target = peer(offset)
+        copy = pltpu.make_async_remote_copy(
+            chunk_ref.at[target], out_ref.at[me], send_sem.at[offset], recv_sem.at[me],
+            device_id=(z, yh, core, target), device_id_type=MESH,
+        )
+        copy.start()
+        sends.append(copy)
+    for offset in range(1, n_exp):
+        source = peer(n_exp - offset)
+        pltpu.make_async_remote_copy(
+            out_ref.at[source], out_ref.at[source], send_sem.at[offset], recv_sem.at[source],
+            device_id=(z, yh, core, source), device_id_type=MESH,
+        ).wait_recv()
+    own.wait()
+    for copy in sends:
+        copy.wait_send()
+
+
+def exchange_exp(chunks, collective_id):
+    n_exp = chunks.shape[0]
+    return pl.pallas_call(
+        functools.partial(exchange_kernel, n_exp),
+        out_shape=jax.ShapeDtypeStruct(chunks.shape, chunks.dtype),
+        in_specs=[pl.BlockSpec(memory_space=pl.ANY)],
+        out_specs=pl.BlockSpec(memory_space=pl.ANY),
+        scratch_shapes=[
+            pltpu.SemaphoreType.DMA(()),
+            pltpu.SemaphoreType.DMA((n_exp,)),
+            pltpu.SemaphoreType.DMA((n_exp,)),
+        ],
+        compiler_params=pltpu.CompilerParams(collective_id=collective_id, has_side_effects=True),
+    )(chunks)
 
 
 KEY_BLOCK = 128
@@ -239,7 +290,7 @@
         .astype(jnp.bfloat16)
         .reshape(EXPERTS, CAP, D)
     )
-    arrived = lax.all_to_all(outgoing, "exp", split_axis=0, concat_axis=1, tiled=True)
+    arrived = exchange_exp(outgoing, 1).reshape(1, EXPERTS * CAP, D)
     ff = gate_weight.shape[-1]
     weight_piece = lax.all_gather(
         jnp.concatenate([gate_weight, up_weight, down_weight], axis=-1), CTX_AXES, axis=1, tiled=True
@@ -256,7 +307,7 @@
         down_piece,
         preferred_element_type=jnp.float32,
     ).astype(jnp.bfloat16)
-    returned = lax.all_to_all(expert_rows, "exp", split_axis=1, concat_axis=0, tiled=True)
+    returned = exchange_exp(expert_rows.reshape(EXPERTS, CAP, D), 2)
     picked = jnp.take(returned.reshape(EXPERTS * CAP, D), target, axis=0).reshape(row_count, TOP, D)
     mixture = jnp.sum(picked.astype(jnp.float32) * gate_probs[0][:, :, None], axis=1)
     layer_out = (residual.astype(jnp.float32) + mixture).astype(jnp.bfloat16)

time: 204 us -> 185 us (0.907)
  Pallas kernels: 75.3 us -> 116 us
  blocking collectives: 23.4 us -> 0 us
  waiting for transfers between devices: 19.5 us -> 4.22 us
  local copies, waits for them, and re-layouts: 27.1 us -> 17.5 us
  other arithmetic: 19.1 us -> 10.1 us
  starting transfers between devices: 4.02 us -> 0.04 us
  matrix products: 19.9 us -> 22.3 us
    pallas_call x0 -> x2, Pallas kernels: none -> 45.5 us  [exchange_exp(): pl.pallas_call(functools.partial(exchange_kernel, n_exp), out_shape=jax.S...]
    all_to_all x1 -> x0, blocking collectives: 23.4 us -> none  [shards(): lax.all_to_all(outgoing, 'exp', split_axis=0, concat_axis=1, tiled=True)]
    all_to_all x1 -> x0, waiting for transfers between devices: 16.4 us -> none  [shards(): lax.all_to_all(expert_rows, 'exp', split_axis=1, concat_axis=0, tiled=True)]
    unnamed x1 -> x0, other arithmetic: 8.96 us -> none
    unnamed x22 -> x12, local copies, waits for them, and re-layouts: 9.32 us -> 0.83 us
    pallas_call x1, Pallas kernels: 22.7 us -> 17.8 us  [block_attention(): pl.pallas_call(functools.partial(attention_kernel, groups, head_size), ou...]
    all_to_all x1 -> x0, starting transfers between devices: 3.98 us -> none  [shards(): lax.all_to_all(expert_rows, 'exp', split_axis=1, concat_axis=0, tiled=True)]
    convert_element_type x1 -> x0, local copies, waits for them, and re-layouts: 3.23 us -> none  [shards(): expert_rows = jnp.einsum('esf,edf->esd', hidden, down_piece, preferred_el...]
  transfers between devices with their start and end apart: 2 -> 1, of which waited for: 2 -> 1; matrix products, arithmetic and copies ran while one was open for 9% -> 11% of each run, Pallas kernels for 37% -> 52%
where the time goes in v5:
time: 185 us; the launch traced here: 184 us
  Pallas kernels  116 us (63%)
  matrix products  22.3 us (12%)
  local copies, waits for them, and re-layouts  17.5 us (9%)
  between operations  14.2 us (8%)
  other arithmetic  10.1 us (5%)
  waiting for transfers between devices  4.22 us (2%)
    pallas_call x1, Pallas kernels, gather_ctx_kernel(): pl.pallas_call(functools.partial(gather_kernel, n_z), out_shape=jax.Shape...  52.6 us
    pallas_call x2, Pallas kernels, exchange_exp(): pl.pallas_call(functools.partial(exchange_kernel, n_exp), out_shape=jax.S...  45.5 us
    pallas_call x1, Pallas kernels, block_attention(): pl.pallas_call(functools.partial(attention_kernel, groups, head_size), ou...  17.8 us
    dot_general x1, matrix products, shards(): jnp.einsum('esf,edf->esd', hidden, down_piece, preferred_element_type=jnp...  10.3 us
    gather x2, local copies, waits for them, and re-layouts, shards(): jnp.take(returned.reshape(EXPERTS * CAP, D), target, axis=0)  6.94 us
    dot_general x1, matrix products, shards(): jnp.einsum('esd,edf->esf', arrived, up_piece, preferred_element_type=jnp....  6.74 us
    convert_element_type x2, local copies, waits for them, and re-layouts, block_attention(): jnp.repeat(jnp.repeat(mask_block, TILE, axis=0), TILE, axis=1)  4.87 us
    all_gather x1, waiting for transfers between devices, shards(): lax.all_gather(jnp.concatenate([gate_weight, up_weight, down_weight], axi...  4.2 us
  transfers between devices with their start and end apart: 1, of which 1 were waited for; matrix products, arithmetic and copies ran while one was open for 11% of the time, Pallas kernels for 52%

profile of v5, /device:TPU:1, one launch (start us, length us, event | category | flops | bytes accessed | tf_op | source)
XLA Modules:
  0.0 184.4 jit_solution(4253999476154077115)
XLA Ops:
  7.2 0.0 copy-start
  7.2 0.0 all-gather.2.cloned.1.call-start
  7.2 1.9 %pad_maximum_fusion = bf16[1,32,5376]{2,1,0:T(8,128)(2,1)} fusion(bf16[1,32,1792]{2,1,0:T(8,128)(2,1)} %param.21, bf16[1,32,1792]{2,1,0:T(8,128)(2,1)} %param.20, bf16[1,32,1792]{2,1,0:T(8,128)(2,1)} %param.19), kind=kLoop, calls=%fused_computation.25 | loop fusion | flops 1032192 | bytes 688128 | tf_op jit(solution)/shard_map/concatenate | solution.py:296
  9.1 0.0 all-gather.2.cloned.1.call-update
  9.2 0.8 copy.30
  10.0 0.1 eq.39
  10.1 0.1 reshape_squeeze.4
  10.2 0.8 fusion.17
  11.0 0.1 reduce_max.14
  11.1 1.6 pad_maximum_fusion.1.shard_ref
  12.8 52.6 %shard_map.131 = bf16[32,192,512]{2,1,0:T(8,128)(2,1)} custom-call(bf16[192,512]{1,0:T(8,128)(2,1)} %pad_maximum_fusion.1.shard_ref), custom_call_target="tpu_custom_call" | custom-call | tf_op jit(solution)/shard_map/pallas_call | solution.py:109
  65.4 0.1 copy.28
  65.5 1.9 %broadcast_in_dim.31 = bf16[192,192,32]{0,2,1:T(8,128)(2,1)} broadcast(bf16[192,192]{0,1:T(8,128)(2,1)S(1)} %copy.28), dimensions={0,1} | broadcast | bytes 2433024 | tf_op jit(solution)/shard_map/broadcast_in_dim | solution.py:232
  67.4 4.8 %copy.29.mask_ref = bf16[192,6144]{1,0:T(8,128)(2,1)} copy(bf16[192,6144]{0,1:T(8,128)(2,1)} %bitcast.59) | data formatting | bytes 4718592 | tf_op jit(solution)/shard_map/convert_element_type | solution.py:232
  72.2 0.6 reduce_max.18.flag_ref
  72.8 0.0 copy-start.1
  72.8 17.8 %shard_map.132 = bf16[192,1024]{1,0:T(8,128)(2,1)} custom-call(s32[48]{0:T(128)} %reduce_max.18.flag_ref, bf16[192,1024]{1,0:T(8,128)(2,1)} %bitcast.64, bf16[6144,512]{1,0:T(8,128)(2,1)} %bitcast.58, bf16[192,6144]{1,0:T(8,128)(2,1)} %copy.29.mask_ref), custom_call_target="tpu_custom_call" | custom-call | tf_op jit(solution)/shard_map/pallas_call | solution.py:238
  90.6 0.0 copy-done
  90.6 0.0 copy-done.1
  90.6 0.0 copy-start.3
  90.6 2.4 %fusion.4 = (f32[192]{0:T(256)S(1)}, bf16[192,1024]{1,0:T(8,128)(2,1)S(1)}, bf16[1,192,1024]{2,1,0:T(8,128)(2,1)}) fusion(bf16[1,192,1024]{2,1,0:T(8,128)(2,1)S(1)} %copy-done.1, bf16[192,1024]{1,0:T(8,128)(2,1)} %shard_map.132, bf16[1024,1024]{1,0:T(8,128)(2,1)S(1)} %copy-done), kind=kOutput, calls=%fused_computation.16 | convolution fusion | flops 404029248 | bytes 3670784 | tf_op jit(solution)/shard_map/dot_general | solution.py:275
  93.0 0.0 copy-done.3
  93.0 0.2 fusion.6
  93.2 0.4 broadcast_in_dim.34
  93.6 0.0 copy-start.2
  93.6 0.0 copy-start.4
  93.6 1.2 reshape.139
  94.8 0.8 reduce-window.6
  95.6 0.2 slice_reduce_fusion
  95.9 0.1 fusion.12
  96.0 0.1 reduce_sum.32
  96.2 2.9 %convolution_convert_fusion = bf16[576,1024]{1,0:T(8,128)(2,1)} fusion(bf16[384,1024]{1,0:T(8,128)(2,1)} %reshape.139, s32[384]{0:T(512)S(1)} %multiply_add_fusion), kind=kOutput, calls=%fused_computation.10 | convolution fusion | flops 453795840 | bytes 1967616 | tf_op jit(solution)/shard_map/dot_general | solution.py:289
  99.1 25.9 %shard_map.133 = bf16[8,72,1024]{2,1,0:T(8,128)(2,1)} custom-call(bf16[8,72,1024]{2,1,0:T(8,128)(2,1)} %bitcast.63), custom_call_target="tpu_custom_call" | custom-call | tf_op jit(solution)/shard_map/pallas_call | solution.py:160
  125.0 0.0 copy-done.2
  125.1 0.1 copy.34
  125.2 0.1 mul.84
  125.3 0.1 copy.32
  125.4 0.2 copy.33
  125.6 0.0 copy-done.4
  125.6 0.1 copy.35
  125.8 4.2 %all-gather.2.cloned.1.call-done = bf16[1,1024,5376]{2,1,0:T(8,128)(2,1)} async-done(((bf16[1,32,5376]{2,1,0:T(8,128)(2,1)}), bf16[1,1024,5376]{2,1,0:T(8,128)(2,1)}) %all-gather.2.cloned.1.call-update) | async-done | bytes 11010064 | tf_op jit(solution)/shard_map/all_gather | solution.py:295
  130.0 6.7 %fusion.1 = f32[576,1792]{1,0:T(8,128)} fusion(bf16[576,1024]{1,0:T(8,128)(2,1)} %bitcast.60, bf16[1,1024,5376]{2,1,0:T(8,128)(2,1)} %all-gather.2.cloned.1.call-done), kind=kOutput, calls=%fused_computation.5 | convolution fusion | flops 2113929216 | bytes 8978432 | tf_op jit(solution)/shard_map/esd,edf->esf/dot_general | solution.py:302
  136.7 10.3 %fusion.3 = bf16[576,1024]{1,0:T(8,128)(2,1)} fusion(bf16[1,1024,5376]{2,1,0:T(8,128)(2,1)} %all-gather.2.cloned.1.call-done, f32[576,1792]{1,0:T(8,128)} %fusion.1, bf16[576,1024]{1,0:T(8,128)(2,1)} %bitcast.61), kind=kOutput, calls=%fused_computation.11 | convolution fusion | flops 4234641408 | bytes 13828096 | tf_op jit(solution)/shard_map/esf,edf->esd/dot_general | solution.py:304
  147.0 19.6 %shard_map.134 = bf16[8,72,1024]{2,1,0:T(8,128)(2,1)} custom-call(bf16[8,72,1024]{2,1,0:T(8,128)(2,1)} %bitcast.62), custom_call_target="tpu_custom_call" | custom-call | tf_op jit(solution)/shard_map/pallas_call | solution.py:160
  166.6 4.8 %gather_fusion = bf16[384,1024]{1,0:T(8,128)(2,1)} fusion(bf16[576,1024]{1,0:T(8,128)(2,1)} %bitcast.57, s32[1024]{0:T(1024)S(1)} %pad_clamp_fusion), kind=kCustom, calls=%fused_computation | custom fusion | bytes 1574400 | tf_op jit(solution)/shard_map/jit(_take)/gather | solution.py:311
  171.4 2.1 %gather.7 = bf16[192,2,1024]{2,1,0:T(2,128)(2,1)S(1)} reshape(bf16[384,1024]{1,0:T(8,128)(2,1)} %gather_fusion) | data formatting | bytes 1572864 | tf_op jit(solution)/shard_map/jit(_take)/gather | solution.py:311
  173.5 3.1 %multiply_reduce_fusion = f32[192,1024]{1,0:T(8,128)S(1)} fusion(bf16[192,2,1024]{2,1,0:T(2,128)(2,1)S(1)} %gather.7, pred[192,2]{1,0:T(8,128)(4,1)S(1)} %copy.33, f32[192,2]{1,0:T(8,128)S(1)} %copy.35), kind=kLoop, calls=%fused_computation.8 | loop fusion | flops 1376256 | bytes 1574784 | tf_op jit(solution)/shard_map/reduce_sum | solution.py:312
  176.7 0.8 fusion.10
  (10 shorter events, 0.1 us)
Async XLA Ops:
  7.2 83.4 %copy-start = (bf16[1024,1024]{1,0:T(8,128)(2,1)S(1)}, bf16[1024,1024]{1,0:T(8,128)(2,1)}, u32[]{:S(2)}) copy-start(bf16[1024,1024]{1,0:T(8,128)(2,1)} %param.17) | copy-start | bytes 6291460
  7.2 122.8 %all-gather.2.cloned.1.call-start = ((), (), s32[]{:S(2)}) async-start(), calls=%async_computation | async-start | bytes 11354112 | tf_op jit(solution)/shard_map/all_gather | solution.py:295
  72.8 17.8 %copy-start.1 = (bf16[1,192,1024]{2,1,0:T(8,128)(2,1)S(1)}, bf16[1,192,1024]{2,1,0:T(8,128)(2,1)}, u32[]{:S(2)}) copy-start(bf16[1,192,1024]{2,1,0:T(8,128)(2,1)} %param.12) | copy-start | bytes 1179652
  90.6 2.4 %copy-start.3 = (f32[1024]{0:T(1024)S(1)}, f32[1024]{0:T(1024)}, u32[]{:S(2)}) copy-start(f32[1024]{0:T(1024)} %param.18) | copy-start | bytes 12292
  93.6 31.5 %copy-start.2 = (s32[1,192,2]{1,2,0:T(2,128)S(1)}, s32[1,192,2]{1,2,0:T(2,128)}, u32[]{:S(2)}) copy-start(s32[1,192,2]{1,2,0:T(2,128)} %param.22) | copy-start | bytes 4612
  93.6 32.0 %copy-start.4 = (f32[1,192,2]{1,2,0:T(2,128)S(1)}, f32[1,192,2]{1,2,0:T(2,128)}, u32[]{:S(2)}) copy-start(f32[1,192,2]{1,2,0:T(2,128)} %param.23) | copy-start | bytes 4612
Sparse Core Ops, SparseCore 0:
  10.8 119.1 all-gather.1

commit v6 on v5

--- a/solution.py
+++ b/solution.py
@@ -184,6 +184,13 @@
     sum_ref[...] = jnp.zeros(sum_ref.shape, jnp.float32)
     acc_ref[...] = jnp.zeros(acc_ref.shape, jnp.float32)
 
+    def allowed_block(j):
+        tile_count = mask_ref.shape[1]
+        tile_at = lax.broadcasted_iota(jnp.int32, (tile_count, KEY_BLOCK), 0)
+        column_tile = lax.broadcasted_iota(jnp.int32, (tile_count, KEY_BLOCK), 1) // TILE
+        spread = (tile_at == j * (KEY_BLOCK // TILE) + column_tile).astype(jnp.bfloat16)
+        return jnp.dot(mask_ref[...], spread, preferred_element_type=jnp.float32) > 0
+
     def scores(j, h):
         rows = pl.ds(pl.multiple_of(j * KEY_BLOCK, KEY_BLOCK), KEY_BLOCK)
         key = kv_ref[rows, pl.ds((h // groups) * head_size, head_size)]
@@ -191,7 +198,7 @@
         raw = lax.dot_general(
             query, key, (((1,), (1,)), ((), ())), preferred_element_type=jnp.float32
         )
-        return raw * scale, mask_ref[:, rows] > 0
+        return raw * scale, allowed_block(j)
 
     def first_pass(j, carry):
         @pl.when(flag_ref[j] > 0)
@@ -229,7 +236,7 @@
     row_count = query_rows.shape[0]
     key_count = kv_rows.shape[0]
     heads = query_rows.shape[1] // head_size
-    allowed = jnp.repeat(jnp.repeat(mask_block, TILE, axis=0), TILE, axis=1).astype(jnp.bfloat16)
+    allowed = jnp.repeat(mask_block, TILE, axis=0).astype(jnp.bfloat16)
     tiles_per_block = KEY_BLOCK // TILE
     flags = jnp.max(
         mask_block.reshape(mask_block.shape[0], -1, tiles_per_block), axis=(0, 2)
@@ -308,8 +315,20 @@
         preferred_element_type=jnp.float32,
     ).astype(jnp.bfloat16)
     returned = exchange_exp(expert_rows.reshape(EXPERTS, CAP, D), 2)
-    picked = jnp.take(returned.reshape(EXPERTS * CAP, D), target, axis=0).reshape(row_count, TOP, D)
-    mixture = jnp.sum(picked.astype(jnp.float32) * gate_probs[0][:, :, None], axis=1)
+    combine = jnp.sum(
+        jnp.where(
+            jnp.arange(EXPERTS * CAP, dtype=jnp.int32)[None, None, :] == target.reshape(row_count, TOP)[:, :, None],
+            gate_probs[0][:, :, None],
+            0.0,
+        ),
+        axis=1,
+    )
+    mixture = jnp.dot(
+        combine,
+        returned.reshape(EXPERTS * CAP, D).astype(jnp.float32),
+        precision=lax.Precision.HIGHEST,
+        preferred_element_type=jnp.float32,
+    )
     layer_out = (residual.astype(jnp.float32) + mixture).astype(jnp.bfloat16)
     return (attention_out[None], layer_out[None])
 

time: 185 us -> 176 us (0.951)
  local copies, waits for them, and re-layouts: 17.5 us -> 3.89 us
  Pallas kernels: 116 us -> 125 us
  waiting for transfers between devices: 4.22 us -> 0.04 us
  other arithmetic: 10.1 us -> 6.37 us
  matrix products: 22.3 us -> 25.4 us
    gather x2 -> x0, local copies, waits for them, and re-layouts: 6.94 us -> none  [shards(): jnp.take(returned.reshape(EXPERTS * CAP, D), target, axis=0)]
    pallas_call x2, Pallas kernels: 45.5 us -> 50.7 us  [exchange_exp(): pl.pallas_call(functools.partial(exchange_kernel, n_exp), out_shape=jax.S...]
    convert_element_type x2 -> x0, local copies, waits for them, and re-layouts: 4.87 us -> none  [block_attention(): jnp.repeat(jnp.repeat(mask_block, TILE, axis=0), TILE, axis=1)]
    pallas_call x1, Pallas kernels: 17.8 us -> 22 us  [block_attention(): pl.pallas_call(functools.partial(attention_kernel, groups, head_size), ou...]
    all_gather x1, waiting for transfers between devices: 4.2 us -> 0.02 us  [shards(): lax.all_gather(jnp.concatenate([gate_weight, up_weight, down_weight], axi...]
    dot_general x0 -> x1, matrix products: none -> 3.11 us  [shards(): jnp.dot(combine, returned.reshape(EXPERTS * CAP, D).astype(jnp.float32),...]
    reduce_sum x1, other arithmetic: 3.13 us -> 0.19 us  [shards(): jnp.sum(jnp.where(jnp.arange(EXPERTS * CAP, dtype=jnp.int32)[None, None,...]
  transfers between devices with their start and end apart: 1 -> 1, of which waited for: 1 -> 0; matrix products, arithmetic and copies ran while one was open for 11% -> 8% of each run, Pallas kernels for 52% -> 63%
where the time goes in v6:
time: 176 us; the launch traced here: 175 us
  Pallas kernels  125 us (71%)
  matrix products  25.4 us (14%)
  between operations  14.2 us (8%)
  other arithmetic  6.37 us (4%)
  local copies, waits for them, and re-layouts  3.89 us (2%)
    pallas_call x1, Pallas kernels, gather_ctx_kernel(): pl.pallas_call(functools.partial(gather_kernel, n_z), out_shape=jax.Shape...  52.6 us
    pallas_call x2, Pallas kernels, exchange_exp(): pl.pallas_call(functools.partial(exchange_kernel, n_exp), out_shape=jax.S...  50.7 us
    pallas_call x1, Pallas kernels, block_attention(): pl.pallas_call(functools.partial(attention_kernel, groups, head_size), ou...  22 us
    dot_general x1, matrix products, shards(): jnp.einsum('esf,edf->esd', hidden, down_piece, preferred_element_type=jnp...  10.3 us
    dot_general x1, matrix products, shards(): jnp.einsum('esd,edf->esf', arrived, up_piece, preferred_element_type=jnp....  6.74 us
  transfers between devices with their start and end apart: 1, of which 0 were waited for; matrix products, arithmetic and copies ran while one was open for 8% of the time, Pallas kernels for 63%

profile of v6, /device:TPU:1, one launch (start us, length us, event | category | flops | bytes accessed | tf_op | source)
XLA Modules:
  0.0 175.3 jit_solution(5669438628703748305)
XLA Ops:
  7.2 0.0 copy-start
  7.2 0.0 all-gather.2.cloned.1.call-start
  7.2 1.9 %pad_maximum_fusion = bf16[1,32,5376]{2,1,0:T(8,128)(2,1)} fusion(bf16[1,32,1792]{2,1,0:T(8,128)(2,1)} %param.21, bf16[1,32,1792]{2,1,0:T(8,128)(2,1)} %param.20, bf16[1,32,1792]{2,1,0:T(8,128)(2,1)} %param.19), kind=kLoop, calls=%fused_computation.24 | loop fusion | flops 1032192 | bytes 688128 | tf_op jit(solution)/shard_map/concatenate | solution.py:303
  9.1 0.0 all-gather.2.cloned.1.call-update
  9.1 0.8 copy.20
  10.0 0.1 eq.56
  10.1 0.1 eq.52
  10.3 0.9 reduce-window.6
  11.1 0.2 slice_reduce_fusion
  11.4 0.8 fusion.16
  12.2 0.1 reduce_max.14
  12.3 1.6 pad_maximum_fusion.1.shard_ref
  13.9 52.6 %shard_map.131 = bf16[32,192,512]{2,1,0:T(8,128)(2,1)} custom-call(bf16[192,512]{1,0:T(8,128)(2,1)} %pad_maximum_fusion.1.shard_ref), custom_call_target="tpu_custom_call" | custom-call | tf_op jit(solution)/shard_map/pallas_call | solution.py:109
  66.5 0.0 copy-start.1
  66.5 0.6 reduce_max.18.flag_ref
  67.2 0.6 broadcast_in_dim.32
  67.8 0.0 copy-start.2
  67.8 22.0 %shard_map.132 = bf16[192,1024]{1,0:T(8,128)(2,1)} custom-call(s32[48]{0:T(128)} %reduce_max.18.flag_ref, bf16[192,1024]{1,0:T(8,128)(2,1)} %bitcast.63, bf16[6144,512]{1,0:T(8,128)(2,1)} %bitcast.56, bf16[192,192]{1,0:T(8,128)(2,1)} %bitcast.62), custom_call_target="tpu_custom_call" | custom-call | tf_op jit(solution)/shard_map/pallas_call | solution.py:245
  89.9 0.0 copy-done
  89.9 0.0 copy-done.1
  89.9 2.4 %fusion.6 = (f32[192]{0:T(256)S(1)}, bf16[192,1024]{1,0:T(8,128)(2,1)S(1)}, bf16[1,192,1024]{2,1,0:T(8,128)(2,1)}) fusion(bf16[1,192,1024]{2,1,0:T(8,128)(2,1)S(1)} %copy-done.1, bf16[192,1024]{1,0:T(8,128)(2,1)} %shard_map.132, bf16[1024,1024]{1,0:T(8,128)(2,1)S(1)} %copy-done), kind=kOutput, calls=%fused_computation.17 | convolution fusion | flops 404029248 | bytes 3670784 | tf_op jit(solution)/shard_map/dot_general | solution.py:282
  92.3 0.0 copy-done.2
  92.3 0.2 fusion.8
  92.4 0.0 copy-start.3
  92.4 0.4 broadcast_in_dim.37
  92.9 1.2 reshape.104
  94.1 0.1 fusion.12
  94.1 0.1 reduce_sum.30
  94.3 2.9 %convolution_convert_fusion = bf16[576,1024]{1,0:T(8,128)(2,1)} fusion(bf16[384,1024]{1,0:T(8,128)(2,1)} %reshape.104, s32[384]{0:T(512)S(1)} %multiply_add_fusion), kind=kOutput, calls=%fused_computation.7 | convolution fusion | flops 453795840 | bytes 1967616 | tf_op jit(solution)/shard_map/dot_general | solution.py:296
  97.2 36.4 %shard_map.133 = bf16[8,72,1024]{2,1,0:T(8,128)(2,1)} custom-call(bf16[8,72,1024]{2,1,0:T(8,128)(2,1)} %bitcast.61), custom_call_target="tpu_custom_call" | custom-call | tf_op jit(solution)/shard_map/pallas_call | solution.py:160
  133.7 0.1 copy.23
  133.7 0.0 copy-done.3
  133.7 0.2 select_reduce_fusion
  133.9 0.0 all-gather.2.cloned.1.call-done
  134.0 6.7 %fusion.1 = f32[576,1792]{1,0:T(8,128)} fusion(bf16[576,1024]{1,0:T(8,128)(2,1)} %bitcast.58, bf16[1,1024,5376]{2,1,0:T(8,128)(2,1)} %all-gather.2.cloned.1.call-done), kind=kOutput, calls=%fused_computation.4 | convolution fusion | flops 2113929216 | bytes 8978432 | tf_op jit(solution)/shard_map/esd,edf->esf/dot_general | solution.py:309
  140.7 10.3 %fusion.3 = bf16[576,1024]{1,0:T(8,128)(2,1)} fusion(bf16[1,1024,5376]{2,1,0:T(8,128)(2,1)} %all-gather.2.cloned.1.call-done, f32[576,1792]{1,0:T(8,128)} %fusion.1, bf16[576,1024]{1,0:T(8,128)(2,1)} %bitcast.59), kind=kOutput, calls=%fused_computation.8 | convolution fusion | flops 4234641408 | bytes 13828096 | tf_op jit(solution)/shard_map/esf,edf->esd/dot_general | solution.py:311
  151.0 14.3 %shard_map.134 = bf16[8,72,1024]{2,1,0:T(8,128)(2,1)} custom-call(bf16[8,72,1024]{2,1,0:T(8,128)(2,1)} %bitcast.60), custom_call_target="tpu_custom_call" | custom-call | tf_op jit(solution)/shard_map/pallas_call | solution.py:160
  165.3 3.1 %fusion.5 = bf16[1,192,1024]{2,1,0:T(8,128)(2,1)} fusion(f32[192,576]{1,0:T(8,128)S(1)} %select_reduce_fusion, bf16[576,1024]{1,0:T(8,128)(2,1)} %bitcast.57, bf16[192,1024]{1,0:T(8,128)(2,1)S(1)} %get-tuple-element.3), kind=kOutput, calls=%fused_computation.11 | convolution fusion | flops 1359544320 | bytes 2408448 | tf_op jit(solution)/shard_map/dot_general | solution.py:326
  (6 shorter events, 0.1 us)
Async XLA Ops:
  7.2 82.7 %copy-start = (bf16[1024,1024]{1,0:T(8,128)(2,1)S(1)}, bf16[1024,1024]{1,0:T(8,128)(2,1)}, u32[]{:S(2)}) copy-start(bf16[1024,1024]{1,0:T(8,128)(2,1)} %param.17) | copy-start | bytes 6291460
  7.2 126.8 %all-gather.2.cloned.1.call-start = ((), (), s32[]{:S(2)}) async-start(), calls=%async_computation | async-start | bytes 11354112 | tf_op jit(solution)/shard_map/all_gather | solution.py:302
  66.5 23.3 %copy-start.1 = (bf16[1,192,1024]{2,1,0:T(8,128)(2,1)S(1)}, bf16[1,192,1024]{2,1,0:T(8,128)(2,1)}, u32[]{:S(2)}) copy-start(bf16[1,192,1024]{2,1,0:T(8,128)(2,1)} %param.12) | copy-start | bytes 1179652
  67.8 24.4 %copy-start.2 = (f32[1024]{0:T(1024)S(1)}, f32[1024]{0:T(1024)}, u32[]{:S(2)}) copy-start(f32[1024]{0:T(1024)} %param.18) | copy-start | bytes 12292
  92.4 41.3 %copy-start.3 = (f32[1,192,2]{1,2,0:T(2,128)S(1)}, f32[1,192,2]{1,2,0:T(2,128)}, u32[]{:S(2)}) copy-start(f32[1,192,2]{1,2,0:T(2,128)} %param.23) | copy-start | bytes 4612
Sparse Core Ops, SparseCore 0:
  10.8 118.6 all-gather.1

commit v7 on v6

--- a/solution.py
+++ b/solution.py
@@ -198,13 +198,14 @@
         raw = lax.dot_general(
             query, key, (((1,), (1,)), ((), ())), preferred_element_type=jnp.float32
         )
-        return raw * scale, allowed_block(j)
+        return raw * scale
 
     def first_pass(j, carry):
         @pl.when(flag_ref[j] > 0)
         def _():
+            allowed = allowed_block(j)
             for h in range(heads):
-                s, allowed = scores(j, h)
+                s = scores(j, h)
                 top_ref[h] = jnp.maximum(top_ref[h], jnp.where(allowed, s, -1e30))
         return carry
 
@@ -216,8 +217,9 @@
         @pl.when(flag_ref[j] > 0)
         def _():
             rows = pl.ds(pl.multiple_of(j * KEY_BLOCK, KEY_BLOCK), KEY_BLOCK)
+            allowed = allowed_block(j)
             for h in range(heads):
-                s, allowed = scores(j, h)
+                s = scores(j, h)
                 weights = jnp.where(allowed, jnp.exp(s - top_ref[h]), 0.0)
                 sum_ref[h] += weights
                 value = kv_ref[rows, pl.ds(value_at + (h // groups) * head_size, head_size)]

time: 176 us -> 189 us (1.074)
  waiting for transfers between devices: 0.04 us -> 19.5 us
  Pallas kernels: 125 us -> 119 us
    all_gather x1, waiting for transfers between devices: 0.02 us -> 19.5 us  [shards(): lax.all_gather(jnp.concatenate([gate_weight, up_weight, down_weight], axi...]
    pallas_call x1, Pallas kernels: 22 us -> 18.8 us  [block_attention(): pl.pallas_call(functools.partial(attention_kernel, groups, head_size), ou...]
    pallas_call x2, Pallas kernels: 50.7 us -> 47.8 us  [exchange_exp(): pl.pallas_call(functools.partial(exchange_kernel, n_exp), out_shape=jax.S...]
  transfers between devices with their start and end apart: 1 -> 1, of which waited for: 0 -> 1; matrix products, arithmetic and copies ran while one was open for 8% -> 7% of each run, Pallas kernels for 63% -> 52%
where the time goes in v7:
time: 189 us
  Pallas kernels  119 us (63%)
  matrix products  25.4 us (13%)
  waiting for transfers between devices  19.5 us (10%)
  between operations  14.2 us (8%)
  other arithmetic  6.37 us (3%)
  local copies, waits for them, and re-layouts  3.89 us (2%)
    pallas_call x1, Pallas kernels, gather_ctx_kernel(): pl.pallas_call(functools.partial(gather_kernel, n_z), out_shape=jax.Shape...  52.6 us
    pallas_call x2, Pallas kernels, exchange_exp(): pl.pallas_call(functools.partial(exchange_kernel, n_exp), out_shape=jax.S...  47.8 us
    all_gather x1, waiting for transfers between devices, shards(): lax.all_gather(jnp.concatenate([gate_weight, up_weight, down_weight], axi...  19.5 us
    pallas_call x1, Pallas kernels, block_attention(): pl.pallas_call(functools.partial(attention_kernel, groups, head_size), ou...  18.8 us
    dot_general x1, matrix products, shards(): jnp.einsum('esf,edf->esd', hidden, down_piece, preferred_element_type=jnp...  10.3 us
    dot_general x1, matrix products, shards(): jnp.einsum('esd,edf->esf', arrived, up_piece, preferred_element_type=jnp....  6.74 us
  transfers between devices with their start and end apart: 1, of which 1 were waited for; matrix products, arithmetic and copies ran while one was open for 7% of the time, Pallas kernels for 52%

profile of v7, /device:TPU:1, one launch (start us, length us, event | category | flops | bytes accessed | tf_op | source)
XLA Modules:
  0.0 188.6 jit_solution(2556374675250066520)
XLA Ops:
  7.2 0.0 copy-start
  7.2 0.0 all-gather.2.cloned.1.call-start
  7.2 1.9 %pad_maximum_fusion = bf16[1,32,5376]{2,1,0:T(8,128)(2,1)} fusion(bf16[1,32,1792]{2,1,0:T(8,128)(2,1)} %param.21, bf16[1,32,1792]{2,1,0:T(8,128)(2,1)} %param.20, bf16[1,32,1792]{2,1,0:T(8,128)(2,1)} %param.19), kind=kLoop, calls=%fused_computation.24 | loop fusion | flops 1032192 | bytes 688128 | tf_op jit(solution)/shard_map/concatenate | solution.py:305
  9.1 0.0 all-gather.2.cloned.1.call-update
  9.1 0.8 copy.20
  10.0 0.1 eq.56
  10.1 0.1 eq.52
  10.3 0.9 reduce-window.6
  11.1 0.2 slice_reduce_fusion
  11.4 0.8 fusion.16
  12.2 0.1 reduce_max.14
  12.3 1.6 pad_maximum_fusion.1.shard_ref
  13.9 52.6 %shard_map.131 = bf16[32,192,512]{2,1,0:T(8,128)(2,1)} custom-call(bf16[192,512]{1,0:T(8,128)(2,1)} %pad_maximum_fusion.1.shard_ref), custom_call_target="tpu_custom_call" | custom-call | tf_op jit(solution)/shard_map/pallas_call | solution.py:109
  66.5 0.0 copy-start.1
  66.5 0.6 reduce_max.18.flag_ref
  67.2 0.6 broadcast_in_dim.32
  67.8 0.0 copy-start.2
  67.8 18.8 %shard_map.132 = bf16[192,1024]{1,0:T(8,128)(2,1)} custom-call(s32[48]{0:T(128)} %reduce_max.18.flag_ref, bf16[192,1024]{1,0:T(8,128)(2,1)} %bitcast.63, bf16[6144,512]{1,0:T(8,128)(2,1)} %bitcast.56, bf16[192,192]{1,0:T(8,128)(2,1)} %bitcast.62), custom_call_target="tpu_custom_call" | custom-call | tf_op jit(solution)/shard_map/pallas_call | solution.py:247
  86.7 0.0 copy-done
  86.7 0.0 copy-done.1
  86.7 2.4 %fusion.6 = (f32[192]{0:T(256)S(1)}, bf16[192,1024]{1,0:T(8,128)(2,1)S(1)}, bf16[1,192,1024]{2,1,0:T(8,128)(2,1)}) fusion(bf16[1,192,1024]{2,1,0:T(8,128)(2,1)S(1)} %copy-done.1, bf16[192,1024]{1,0:T(8,128)(2,1)} %shard_map.132, bf16[1024,1024]{1,0:T(8,128)(2,1)S(1)} %copy-done), kind=kOutput, calls=%fused_computation.17 | convolution fusion | flops 404029248 | bytes 3670784 | tf_op jit(solution)/shard_map/dot_general | solution.py:284
  89.0 0.0 copy-done.2
  89.0 0.2 fusion.8
  89.2 0.0 copy-start.3
  89.2 0.4 broadcast_in_dim.37
  89.6 1.2 reshape.104
  90.8 0.1 fusion.12
  90.9 0.1 reduce_sum.30
  91.1 2.9 %convolution_convert_fusion = bf16[576,1024]{1,0:T(8,128)(2,1)} fusion(bf16[384,1024]{1,0:T(8,128)(2,1)} %reshape.104, s32[384]{0:T(512)S(1)} %multiply_add_fusion), kind=kOutput, calls=%fused_computation.7 | convolution fusion | flops 453795840 | bytes 1967616 | tf_op jit(solution)/shard_map/dot_general | solution.py:298
  94.0 27.2 %shard_map.133 = bf16[8,72,1024]{2,1,0:T(8,128)(2,1)} custom-call(bf16[8,72,1024]{2,1,0:T(8,128)(2,1)} %bitcast.61), custom_call_target="tpu_custom_call" | custom-call | tf_op jit(solution)/shard_map/pallas_call | solution.py:160
  121.2 0.1 copy.23
  121.3 0.0 copy-done.3
  121.3 0.2 select_reduce_fusion
  121.5 19.5 %all-gather.2.cloned.1.call-done = bf16[1,1024,5376]{2,1,0:T(8,128)(2,1)} async-done(((bf16[1,32,5376]{2,1,0:T(8,128)(2,1)}), bf16[1,1024,5376]{2,1,0:T(8,128)(2,1)}) %all-gather.2.cloned.1.call-update) | async-done | bytes 11010064 | tf_op jit(solution)/shard_map/all_gather | solution.py:304
  141.0 6.7 %fusion.1 = f32[576,1792]{1,0:T(8,128)} fusion(bf16[576,1024]{1,0:T(8,128)(2,1)} %bitcast.58, bf16[1,1024,5376]{2,1,0:T(8,128)(2,1)} %all-gather.2.cloned.1.call-done), kind=kOutput, calls=%fused_computation.4 | convolution fusion | flops 2113929216 | bytes 8978432 | tf_op jit(solution)/shard_map/esd,edf->esf/dot_general | solution.py:311
  147.7 10.3 %fusion.3 = bf16[576,1024]{1,0:T(8,128)(2,1)} fusion(bf16[1,1024,5376]{2,1,0:T(8,128)(2,1)} %all-gather.2.cloned.1.call-done, f32[576,1792]{1,0:T(8,128)} %fusion.1, bf16[576,1024]{1,0:T(8,128)(2,1)} %bitcast.59), kind=kOutput, calls=%fused_computation.8 | convolution fusion | flops 4234641408 | bytes 13828096 | tf_op jit(solution)/shard_map/esf,edf->esd/dot_general | solution.py:313
  158.0 20.6 %shard_map.134 = bf16[8,72,1024]{2,1,0:T(8,128)(2,1)} custom-call(bf16[8,72,1024]{2,1,0:T(8,128)(2,1)} %bitcast.60), custom_call_target="tpu_custom_call" | custom-call | tf_op jit(solution)/shard_map/pallas_call | solution.py:160
  178.6 3.1 %fusion.5 = bf16[1,192,1024]{2,1,0:T(8,128)(2,1)} fusion(f32[192,576]{1,0:T(8,128)S(1)} %select_reduce_fusion, bf16[576,1024]{1,0:T(8,128)(2,1)} %bitcast.57, bf16[192,1024]{1,0:T(8,128)(2,1)S(1)} %get-tuple-element.3), kind=kOutput, calls=%fused_computation.11 | convolution fusion | flops 1359544320 | bytes 2408448 | tf_op jit(solution)/shard_map/dot_general | solution.py:328
  (6 shorter events, 0.1 us)
Async XLA Ops:
  7.2 79.5 %copy-start = (bf16[1024,1024]{1,0:T(8,128)(2,1)S(1)}, bf16[1024,1024]{1,0:T(8,128)(2,1)}, u32[]{:S(2)}) copy-start(bf16[1024,1024]{1,0:T(8,128)(2,1)} %param.17) | copy-start | bytes 6291460
  7.2 133.8 %all-gather.2.cloned.1.call-start = ((), (), s32[]{:S(2)}) async-start(), calls=%async_computation | async-start | bytes 11354112 | tf_op jit(solution)/shard_map/all_gather | solution.py:304
  66.5 20.1 %copy-start.1 = (bf16[1,192,1024]{2,1,0:T(8,128)(2,1)S(1)}, bf16[1,192,1024]{2,1,0:T(8,128)(2,1)}, u32[]{:S(2)}) copy-start(bf16[1,192,1024]{2,1,0:T(8,128)(2,1)} %param.12) | copy-start | bytes 1179652
  67.8 21.2 %copy-start.2 = (f32[1024]{0:T(1024)S(1)}, f32[1024]{0:T(1024)}, u32[]{:S(2)}) copy-start(f32[1024]{0:T(1024)} %param.18) | copy-start | bytes 12292
  89.2 32.1 %copy-start.3 = (f32[1,192,2]{1,2,0:T(2,128)S(1)}, f32[1,192,2]{1,2,0:T(2,128)}, u32[]{:S(2)}) copy-start(f32[1,192,2]{1,2,0:T(2,128)} %param.23) | copy-start | bytes 4612
Sparse Core Ops, SparseCore 0:
  10.8 130.1 all-gather.1

commit v8 on v7

--- a/solution.py
+++ b/solution.py
@@ -301,20 +301,37 @@
     )
     arrived = exchange_exp(outgoing, 1).reshape(1, EXPERTS * CAP, D)
     ff = gate_weight.shape[-1]
-    weight_piece = lax.all_gather(
-        jnp.concatenate([gate_weight, up_weight, down_weight], axis=-1), CTX_AXES, axis=1, tiled=True
-    )
-    gate_piece = weight_piece[..., :ff]
-    up_piece = weight_piece[..., ff : 2 * ff]
-    down_piece = weight_piece[..., 2 * ff :]
-    gate_sum = jnp.einsum("esd,edf->esf", arrived, gate_piece, preferred_element_type=jnp.float32)
-    up_sum = jnp.einsum("esd,edf->esf", arrived, up_piece, preferred_element_type=jnp.float32)
+    half = ff // 2
+    core = lax.axis_index("core")
+    swap = [(0, 1), (1, 0)]
+
+    def halves(part):
+        columns = slice(part * half, (part + 1) * half)
+        return jnp.concatenate([w[0][:, columns] for w in (gate_weight, up_weight, down_weight)], axis=-1)
+
+    own_half = jnp.where(core == 0, halves(0), halves(1))
+    other_half = jnp.where(core == 0, halves(1), halves(0))
+    from_sibling = lax.ppermute(other_half, "core", swap)
+    chip_rows = jnp.where(
+        core == 0,
+        jnp.concatenate([own_half, from_sibling], axis=0),
+        jnp.concatenate([from_sibling, own_half], axis=0),
+    )
+    weight_piece = lax.all_gather(chip_rows, CTX_AXES[:2], axis=0, tiled=True)
+    gate_piece = weight_piece[:, :half]
+    up_piece = weight_piece[:, half : 2 * half]
+    down_piece = weight_piece[:, 2 * half :]
+    own_tokens = arrived[0]
+    both_tokens = jnp.concatenate([own_tokens, lax.ppermute(own_tokens, "core", swap)], axis=0)
+    gate_sum = jnp.dot(both_tokens, gate_piece, preferred_element_type=jnp.float32)
+    up_sum = jnp.dot(both_tokens, up_piece, preferred_element_type=jnp.float32)
     hidden = (jax.nn.silu(gate_sum) * up_sum).astype(jnp.bfloat16)
-    expert_rows = jnp.einsum(
-        "esf,edf->esd",
-        hidden,
-        down_piece,
-        preferred_element_type=jnp.float32,
+    partial = lax.dot_general(
+        hidden, down_piece, (((1,), (1,)), ((), ())), preferred_element_type=jnp.float32
+    )
+    slot_rows = own_tokens.shape[0]
+    expert_rows = (
+        partial[:slot_rows] + lax.ppermute(partial[slot_rows:], "core", swap)
     ).astype(jnp.bfloat16)
     returned = exchange_exp(expert_rows.reshape(EXPERTS, CAP, D), 2)
     combine = jnp.sum(

time: 189 us -> 200 us (1.058)
  starting transfers between devices: 0.04 us -> 7.71 us
  Pallas kernels: 119 us -> 114 us
  local copies, waits for them, and re-layouts: 3.89 us -> 8.49 us
    ppermute x0 -> x3, waiting for transfers between devices: none -> 8.27 us  [the longest x1 4.06 us: shards(): lax.ppermute(partial[slot_rows:], 'core', swap)]
    ppermute x0 -> x3, starting transfers between devices: none -> 7.68 us  [the longest x1 4.07 us: shards(): lax.ppermute(partial[slot_rows:], 'core', swap)]
    all_gather x1, waiting for transfers between devices: 19.5 us -> 12.4 us  [shards(): weight_piece = lax.all_gather(chip_rows, CTX_AXES[:2], axis=0, tiled=True)]
    pallas_call x2, Pallas kernels: 47.8 us -> 41.5 us  [exchange_exp(): pl.pallas_call(functools.partial(exchange_kernel, n_exp), out_shape=jax.S...]
    slice x1 -> x4, local copies, waits for them, and re-layouts: 0.22 us -> 5.5 us  [the longest x1 3.36 us: shards(): partial[slot_rows:]]
    convert_element_type x0 -> x1, other arithmetic: none -> 3.76 us  [shards(): expert_rows = (partial[:slot_rows] + lax.ppermute(partial[slot_rows:], 'c...]
    pallas_call x1, Pallas kernels: 18.8 us -> 22.5 us  [block_attention(): pl.pallas_call(functools.partial(attention_kernel, groups, head_size), ou...]
    pallas_call x1, Pallas kernels: 52.6 us -> 50.4 us  [gather_ctx_kernel(): pl.pallas_call(functools.partial(gather_kernel, n_z), out_shape=jax.Shape...]
  transfers between devices with their start and end apart: 1 -> 4, of which waited for: 1 -> 4; matrix products, arithmetic and copies ran while one was open for 7% -> 6% of each run, Pallas kernels for 52% -> 47%
where the time goes in v8:
time: 200 us; the launch traced here: 199 us
  Pallas kernels  114 us (57%)
  matrix products  26.4 us (13%)
  waiting for transfers between devices  20.7 us (10%)
  between operations  14.2 us (7%)
  local copies, waits for them, and re-layouts  8.49 us (4%)
  starting transfers between devices  7.71 us (4%)
  other arithmetic  7.4 us (4%)
    pallas_call x1, Pallas kernels, gather_ctx_kernel(): pl.pallas_call(functools.partial(gather_kernel, n_z), out_shape=jax.Shape...  50.4 us
    pallas_call x2, Pallas kernels, exchange_exp(): pl.pallas_call(functools.partial(exchange_kernel, n_exp), out_shape=jax.S...  41.5 us
    pallas_call x1, Pallas kernels, block_attention(): pl.pallas_call(functools.partial(attention_kernel, groups, head_size), ou...  22.5 us
    all_gather x1, waiting for transfers between devices, shards(): weight_piece = lax.all_gather(chip_rows, CTX_AXES[:2], axis=0, tiled=True)  12.4 us
    dot_general x1, matrix products, shards(): lax.dot_general(hidden, down_piece, (((1,), (1,)), ((), ())), preferred_e...  11.2 us
    dot_general x1, matrix products, shards(): jnp.dot(both_tokens, gate_piece, preferred_element_type=jnp.float32)  6.77 us
    ppermute x1, starting transfers between devices, shards(): lax.ppermute(partial[slot_rows:], 'core', swap)  4.07 us
    ppermute x1, waiting for transfers between devices, shards(): lax.ppermute(partial[slot_rows:], 'core', swap)  4.06 us
  transfers between devices with their start and end apart: 4, of which 4 were waited for; matrix products, arithmetic and copies ran while one was open for 6% of the time, Pallas kernels for 47%

profile of v8, /device:TPU:1, one launch (start us, length us, event | category | flops | bytes accessed | tf_op | source)
XLA Modules:
  0.0 199.3 jit_solution(2343249533694422941)
XLA Ops:
  7.2 0.0 copy-start
  7.2 0.0 copy-start.7
  7.2 0.0 copy-start.4
  7.2 0.0 copy-start.3
  7.2 0.0 copy-start.2
  7.2 0.0 all-gather.2.cloned.1.call-start
  7.3 1.0 fusion.28
  8.3 0.9 fusion.26
  9.2 0.1 broadcast_select_fusion.1
  9.3 3.3 %collective-permute-start.1 = (bf16[32,2688]{1,0:T(8,128)(2,1)S(1)}, bf16[32,2688]{1,0:T(8,128)(2,1)S(1)}, u32[]{:S(2)}, u32[]{:S(2)}) collective-permute-start(bf16[32,2688]{1,0:T(8,128)(2,1)S(1)} %get-tuple-element.6), channel_id=1, source_target_pairs={{0,8},{8,0},{1,9},{9,1},{2,10},{10,2},{3,11},{11,3},{4,12},{12,4},... | collective-permute-start | bytes 516104 | tf_op jit(solution)/shard_map/ppermute | solution.py:314
  12.6 1.0 collective-permute-done.1
  13.7 0.8 maximum_select_fusion
  14.5 0.0 all-gather.2.cloned.1.call-update
  14.5 0.0 copy-done.7
  14.5 0.1 copy.20
  14.6 0.1 eq.61
  14.8 0.1 eq.57
  14.9 0.9 reduce-window.6
  15.8 0.2 slice_reduce_fusion
  16.1 0.0 copy-done.4
  16.1 0.1 reduce_max.14
  16.2 0.7 pad_maximum_fusion.4.shard_ref
  16.9 50.4 %shard_map.131 = bf16[32,192,512]{2,1,0:T(8,128)(2,1)} custom-call(bf16[192,512]{1,0:T(8,128)(2,1)} %pad_maximum_fusion.4.shard_ref), custom_call_target="tpu_custom_call" | custom-call | tf_op jit(solution)/shard_map/pallas_call | solution.py:109
  67.3 0.7 reduce_max.18.flag_ref
  68.0 0.6 broadcast_in_dim.32
  68.6 22.5 %shard_map.132 = bf16[192,1024]{1,0:T(8,128)(2,1)} custom-call(s32[48]{0:T(128)} %reduce_max.18.flag_ref, bf16[192,1024]{1,0:T(8,128)(2,1)} %bitcast.48, bf16[6144,512]{1,0:T(8,128)(2,1)} %bitcast.40, bf16[192,192]{1,0:T(8,128)(2,1)} %bitcast.47), custom_call_target="tpu_custom_call" | custom-call | tf_op jit(solution)/shard_map/pallas_call | solution.py:247
  91.1 0.0 copy-done.1
  91.1 2.4 %fusion.13 = (f32[192]{0:T(256)S(1)}, bf16[192,1024]{1,0:T(8,128)(2,1)S(1)}, bf16[1,192,1024]{2,1,0:T(8,128)(2,1)}) fusion(bf16[1,192,1024]{2,1,0:T(8,128)(2,1)S(1)} %copy-done.1, bf16[192,1024]{1,0:T(8,128)(2,1)} %shard_map.132, bf16[1024,1024]{1,0:T(8,128)(2,1)S(1)} %copy-done), kind=kOutput, calls=%fused_computation.19 | convolution fusion | flops 404029248 | bytes 3670784 | tf_op jit(solution)/shard_map/dot_general | solution.py:284
  93.5 0.2 fusion.15
  93.7 0.4 broadcast_in_dim.37
  94.1 1.2 reshape.74
  95.3 0.1 fusion.19
  95.4 3.0 %convolution_convert_fusion = bf16[576,1024]{1,0:T(8,128)(2,1)} fusion(bf16[384,1024]{1,0:T(8,128)(2,1)} %reshape.74, s32[384]{0:T(512)S(1)} %multiply_add_fusion), kind=kOutput, calls=%fused_computation.10 | convolution fusion | flops 453795840 | bytes 1967616 | tf_op jit(solution)/shard_map/dot_general | solution.py:298
  98.3 20.6 %shard_map.133 = bf16[8,72,1024]{2,1,0:T(8,128)(2,1)} custom-call(bf16[8,72,1024]{2,1,0:T(8,128)(2,1)} %bitcast.46), custom_call_target="tpu_custom_call" | custom-call | tf_op jit(solution)/shard_map/pallas_call | solution.py:160
  118.9 0.3 collective-permute-start
  119.2 3.2 %collective-permute-done = bf16[576,1024]{1,0:T(8,128)(2,1)} collective-permute-done((bf16[576,1024]{1,0:T(8,128)(2,1)}, bf16[576,1024]{1,0:T(8,128)(2,1)}, u32[]{:S(2)}, u32[]{:S(2)}) %collective-permute-start) | collective-permute-done | bytes 1179680 | tf_op jit(solution)/shard_map/ppermute | solution.py:325
  122.4 12.4 %all-gather.2.cloned.1.call-done = bf16[1024,2688]{1,0:T(8,128)(2,1)} async-done(((bf16[64,2688]{1,0:T(8,128)(2,1)}), bf16[1024,2688]{1,0:T(8,128)(2,1)}) %all-gather.2.cloned.1.call-update) | async-done | bytes 5505040 | tf_op jit(solution)/shard_map/all_gather | solution.py:320
  134.8 6.8 %fusion.9 = f32[1152,896]{1,0:T(8,128)} fusion(bf16[1024,2688]{1,0:T(8,128)(2,1)} %all-gather.2.cloned.1.call-done, bf16[576,1024]{1,0:T(8,128)(2,1)} %collective-permute-done, bf16[576,1024]{1,0:T(8,128)(2,1)} %bitcast.44), kind=kOutput, calls=%fused_computation.8 | convolution fusion | flops 2118647808 | bytes 8323072 | tf_op jit(solution)/shard_map/dot_general | solution.py:326
  141.5 11.2 %fusion.1 = f32[1152,1024]{1,0:T(8,128)} fusion(f32[1152,896]{1,0:T(8,128)} %fusion.9, bf16[1024,2688]{1,0:T(8,128)(2,1)} %all-gather.2.cloned.1.call-done, bf16[576,1024]{1,0:T(8,128)(2,1)} %collective-permute-done, bf16[576,1024]{1,0:T(8,128)(2,1)} %bitcast.45), kind=kOutput, calls=%fused_computation.4 | convolution fusion | flops 4238770176 | bytes 14876672 | tf_op jit(solution)/shard_map/dot_general | solution.py:329
  152.7 3.4 %slice.69 = f32[576,1024]{1,0:T(8,128)} slice(f32[1152,1024]{1,0:T(8,128)} %fusion.1), slice={[576:1152], [0:1024]} | slice | bytes 4718592 | tf_op jit(solution)/shard_map/slice | solution.py:334
  156.1 4.1 %collective-permute-start.2 = (f32[576,1024]{1,0:T(8,128)}, f32[576,1024]{1,0:T(8,128)}, u32[]{:S(2)}, u32[]{:S(2)}) collective-permute-start(f32[576,1024]{1,0:T(8,128)} %slice.69), channel_id=1, source_target_pairs={{0,8},{8,0},{1,9},{9,1},{2,10},{10,2},{3,11},{11,3},{4,12},{12,4},... | collective-permute-start | bytes 7077896 | tf_op jit(solution)/shard_map/ppermute | solution.py:334
  160.2 0.1 reduce_sum.30
  160.3 0.1 copy.23
  160.4 0.2 select_reduce_fusion
  160.6 4.1 %collective-permute-done.2 = f32[576,1024]{1,0:T(8,128)} collective-permute-done((f32[576,1024]{1,0:T(8,128)}, f32[576,1024]{1,0:T(8,128)}, u32[]{:S(2)}, u32[]{:S(2)}) %collective-permute-start.2) | collective-permute-done | bytes 2359328 | tf_op jit(solution)/shard_map/ppermute | solution.py:334
  164.7 3.8 %fusion = bf16[576,1024]{1,0:T(8,128)(2,1)} fusion(f32[576,1024]{1,0:T(8,128)} %collective-permute-done.2, f32[1152,1024]{1,0:T(8,128)} %fusion.1), kind=kLoop, calls=%fused_computation.2 | loop fusion | flops 1179648 | bytes 5898240 | tf_op jit(solution)/shard_map/convert_element_type | solution.py:335
  168.4 20.9 %shard_map.134 = bf16[8,72,1024]{2,1,0:T(8,128)(2,1)} custom-call(bf16[8,72,1024]{2,1,0:T(8,128)(2,1)} %bitcast.42), custom_call_target="tpu_custom_call" | custom-call | tf_op jit(solution)/shard_map/pallas_call | solution.py:160
  189.4 3.1 %fusion.12 = bf16[1,192,1024]{2,1,0:T(8,128)(2,1)} fusion(f32[192,576]{1,0:T(8,128)S(1)} %select_reduce_fusion, bf16[576,1024]{1,0:T(8,128)(2,1)} %bitcast.41, bf16[192,1024]{1,0:T(8,128)(2,1)S(1)} %get-tuple-element.3), kind=kOutput, calls=%fused_computation.13 | convolution fusion | flops 1359544320 | bytes 2408448 | tf_op jit(solution)/shard_map/dot_general | solution.py:345
  (15 shorter events, 0.1 us)
Async XLA Ops:
  7.2 84.0 %copy-start = (bf16[1024,1024]{1,0:T(8,128)(2,1)S(1)}, bf16[1024,1024]{1,0:T(8,128)(2,1)}, u32[]{:S(2)}) copy-start(bf16[1024,1024]{1,0:T(8,128)(2,1)} %param.17) | copy-start | bytes 6291460
  7.2 7.3 %copy-start.7 = (s32[1,192,2]{1,2,0:T(2,128)S(1)}, s32[1,192,2]{1,2,0:T(2,128)}, u32[]{:S(2)}) copy-start(s32[1,192,2]{1,2,0:T(2,128)} %param.22) | copy-start | bytes 4612
  7.2 8.9 %copy-start.4 = (s32[1,6,192]{2,0,1:T(1,128)S(1)}, s32[1,6,192]{2,0,1:T(1,128)}, u32[]{:S(2)}) copy-start(s32[1,6,192]{2,0,1:T(1,128)} %param.16) | copy-start | bytes 13828
  7.2 9.0 %copy-start.3 = (bf16[1,192,256]{2,1,0:T(8,128)(2,1)S(1)}, bf16[1,192,256]{2,1,0:T(8,128)(2,1)}, u32[]{:S(2)}) copy-start(bf16[1,192,256]{2,1,0:T(8,128)(2,1)} %param.14) | copy-start | bytes 294916
  7.2 9.0 %copy-start.2 = (bf16[1,192,256]{2,1,0:T(8,128)(2,1)S(1)}, bf16[1,192,256]{2,1,0:T(8,128)(2,1)}, u32[]{:S(2)}) copy-start(bf16[1,192,256]{2,1,0:T(8,128)(2,1)} %param.15) | copy-start | bytes 294916
  7.2 127.6 %all-gather.2.cloned.1.call-start = ((), (), s32[]{:S(2)}) async-start(), calls=%async_computation | async-start | bytes 5849088 | tf_op jit(solution)/shard_map/all_gather | solution.py:320
  9.3 4.4 %collective-permute-start.1 = (bf16[32,2688]{1,0:T(8,128)(2,1)S(1)}, bf16[32,2688]{1,0:T(8,128)(2,1)S(1)}, u32[]{:S(2)}, u32[]{:S(2)}) collective-permute-start(bf16[32,2688]{1,0:T(8,128)(2,1)S(1)} %get-tuple-element.6), channel_id=1, source_target_pairs={{0,8},{8,0},{1,9},{9,1},{2,10},{10,2},{3,11},{11,3},{4,12},{12,4},... | collective-permute-start | bytes 516104 | tf_op jit(solution)/shard_map/ppermute | solution.py:314
  68.6 22.5 %copy-start.1 = (bf16[1,192,1024]{2,1,0:T(8,128)(2,1)S(1)}, bf16[1,192,1024]{2,1,0:T(8,128)(2,1)}, u32[]{:S(2)}) copy-start(bf16[1,192,1024]{2,1,0:T(8,128)(2,1)} %param.12) | copy-start | bytes 1179652
  91.1 2.4 %copy-start.5 = (f32[1024]{0:T(1024)S(1)}, f32[1024]{0:T(1024)}, u32[]{:S(2)}) copy-start(f32[1024]{0:T(1024)} %param.18) | copy-start | bytes 12292
  118.9 3.5 %collective-permute-start = (bf16[576,1024]{1,0:T(8,128)(2,1)}, bf16[576,1024]{1,0:T(8,128)(2,1)}, u32[]{:S(2)}, u32[]{:S(2)}) collective-permute-start(bf16[576,1024]{1,0:T(8,128)(2,1)} %bitcast.43), channel_id=1, source_target_pairs={{0,8},{8,0},{1,9},{9,1},{2,10},{10,2},{3,11},{11,3},{4,12},{12,4},... | collective-permute-start | bytes 3538952 | tf_op jit(solution)/shard_map/ppermute | solution.py:325
  152.7 7.7 %copy-start.6 = (f32[1,192,2]{1,2,0:T(2,128)S(1)}, f32[1,192,2]{1,2,0:T(2,128)}, u32[]{:S(2)}) copy-start(f32[1,192,2]{1,2,0:T(2,128)} %param.23) | copy-start | bytes 4612
  156.1 8.6 %collective-permute-start.2 = (f32[576,1024]{1,0:T(8,128)}, f32[576,1024]{1,0:T(8,128)}, u32[]{:S(2)}, u32[]{:S(2)}) collective-permute-start(f32[576,1024]{1,0:T(8,128)} %slice.69), channel_id=1, source_target_pairs={{0,8},{8,0},{1,9},{9,1},{2,10},{10,2},{3,11},{11,3},{4,12},{12,4},... | collective-permute-start | bytes 7077896 | tf_op jit(solution)/shard_map/ppermute | solution.py:334
Sparse Core Ops, SparseCore 0:
  14.6 120.1 all-gather.1

commit v9 on v7

--- a/solution.py
+++ b/solution.py
@@ -103,7 +103,7 @@
         copy.wait_send()
 
 
-def gather_ctx_kernel(block):
+def gather_ctx_kernel(block, collective_id=0):
     n_z = lax.axis_size("z")
     n_all = n_z * 4
     return pl.pallas_call(
@@ -116,7 +116,7 @@
             pltpu.SemaphoreType.DMA((4, n_all)),
             pltpu.SemaphoreType.DMA((n_all,)),
         ],
-        compiler_params=pltpu.CompilerParams(collective_id=0, has_side_effects=True),
+        compiler_params=pltpu.CompilerParams(collective_id=collective_id, has_side_effects=True),
     )(block)
 
 
@@ -301,9 +301,8 @@
     )
     arrived = exchange_exp(outgoing, 1).reshape(1, EXPERTS * CAP, D)
     ff = gate_weight.shape[-1]
-    weight_piece = lax.all_gather(
-        jnp.concatenate([gate_weight, up_weight, down_weight], axis=-1), CTX_AXES, axis=1, tiled=True
-    )
+    weight_local = jnp.concatenate([gate_weight[0], up_weight[0], down_weight[0]], axis=-1)
+    weight_piece = gather_ctx_kernel(weight_local, 3).reshape(1, -1, weight_local.shape[-1])
     gate_piece = weight_piece[..., :ff]
     up_piece = weight_piece[..., ff : 2 * ff]
     down_piece = weight_piece[..., 2 * ff :]

time: 189 us -> 223 us (1.18)
  Pallas kernels: 119 us -> 187 us
  waiting for transfers between devices: 19.5 us -> 0 us
  between operations: 14.2 us -> 0.8 us
    pallas_call x1 -> x2, Pallas kernels: 52.6 us -> 126 us  [gather_ctx_kernel(): pl.pallas_call(functools.partial(gather_kernel, n_z), out_shape=jax.Shape...]
    all_gather x1 -> x0, waiting for transfers between devices: 19.5 us -> none  [shards(): lax.all_gather(jnp.concatenate([gate_weight, up_weight, down_weight], axi...]
    pallas_call x2, Pallas kernels: 47.8 us -> 35.4 us  [exchange_exp(): pl.pallas_call(functools.partial(exchange_kernel, n_exp), out_shape=jax.S...]
    pallas_call x1, Pallas kernels: 18.8 us -> 25.3 us  [block_attention(): pl.pallas_call(functools.partial(attention_kernel, groups, head_size), ou...]
  transfers between devices with their start and end apart: 1 -> 0, of which waited for: 1 -> 0; matrix products, arithmetic and copies ran while one was open for 7% -> 0% of each run, Pallas kernels for 52% -> 0%
where the time goes in v9:
time: 223 us; the launch traced here: 222 us
  Pallas kernels  187 us (84%)
  matrix products  25.5 us (11%)
  other arithmetic  5.2 us (2%)
  local copies, waits for them, and re-layouts  4.07 us (2%)
    pallas_call x2, Pallas kernels, gather_ctx_kernel(): pl.pallas_call(functools.partial(gather_kernel, n_z), out_shape=jax.Shape...  126 us
    pallas_call x2, Pallas kernels, exchange_exp(): pl.pallas_call(functools.partial(exchange_kernel, n_exp), out_shape=jax.S...  35.4 us
    pallas_call x1, Pallas kernels, block_attention(): pl.pallas_call(functools.partial(attention_kernel, groups, head_size), ou...  25.3 us
    dot_general x1, matrix products, shards(): jnp.einsum('esf,edf->esd', hidden, down_piece, preferred_element_type=jnp...  10.3 us
    dot_general x1, matrix products, shards(): jnp.einsum('esd,edf->esf', arrived, up_piece, preferred_element_type=jnp....  6.74 us

profile of v9, /device:TPU:1, one launch (start us, length us, event | category | flops | bytes accessed | tf_op | source)
XLA Modules:
  0.0 222.2 jit_solution(13667776053493741370)
XLA Ops:
  0.6 0.0 copy-start
  0.6 0.9 copy.20
  1.6 0.1 eq.56
  1.8 0.9 reduce-window.6
  2.6 0.2 slice_reduce_fusion
  2.9 0.1 eq.52
  3.0 0.1 fusion.12
  3.1 0.8 fusion.16
  3.9 0.7 broadcast_in_dim.32
  4.6 0.1 reduce_max.14
  4.7 0.6 reduce_max.18.flag_ref
  5.3 1.6 pad_maximum_fusion.1.shard_ref
  6.9 48.9 %shard_map.131 = bf16[32,192,512]{2,1,0:T(8,128)(2,1)} custom-call(bf16[192,512]{1,0:T(8,128)(2,1)} %pad_maximum_fusion.1.shard_ref), custom_call_target="tpu_custom_call" | custom-call | tf_op jit(solution)/shard_map/pallas_call | solution.py:109
  55.9 0.0 copy-start.1
  55.9 0.0 copy-start.5
  55.9 25.3 %shard_map.132 = bf16[192,1024]{1,0:T(8,128)(2,1)} custom-call(s32[48]{0:T(128)} %reduce_max.18.flag_ref, bf16[192,1024]{1,0:T(8,128)(2,1)} %bitcast.69, bf16[6144,512]{1,0:T(8,128)(2,1)} %bitcast.60, bf16[192,192]{1,0:T(8,128)(2,1)} %bitcast.68), custom_call_target="tpu_custom_call" | custom-call | tf_op jit(solution)/shard_map/pallas_call | solution.py:247
  81.2 0.0 copy-done
  81.2 0.0 copy-done.1
  81.2 2.4 %fusion.6 = (f32[192]{0:T(256)S(1)}, bf16[192,1024]{1,0:T(8,128)(2,1)S(1)}, bf16[1,192,1024]{2,1,0:T(8,128)(2,1)}) fusion(bf16[1,192,1024]{2,1,0:T(8,128)(2,1)S(1)} %copy-done.1, bf16[192,1024]{1,0:T(8,128)(2,1)} %shard_map.132, bf16[1024,1024]{1,0:T(8,128)(2,1)S(1)} %copy-done), kind=kOutput, calls=%fused_computation.17 | convolution fusion | flops 404029248 | bytes 3670784 | tf_op jit(solution)/shard_map/dot_general | solution.py:284
  83.6 0.0 copy-done.5
  83.6 0.2 fusion.8
  83.8 0.0 copy-start.2
  83.8 0.4 broadcast_in_dim.37
  84.2 1.2 reshape.107
  85.4 0.0 copy-start.3
  85.4 0.0 copy-start.4
  85.4 3.0 %convolution_convert_fusion = bf16[576,1024]{1,0:T(8,128)(2,1)} fusion(bf16[384,1024]{1,0:T(8,128)(2,1)} %reshape.107, s32[384]{0:T(512)S(1)} %multiply_add_fusion), kind=kOutput, calls=%fused_computation.7 | convolution fusion | flops 453795840 | bytes 1967616 | tf_op jit(solution)/shard_map/dot_general | solution.py:298
  88.4 16.2 %shard_map.133 = bf16[8,72,1024]{2,1,0:T(8,128)(2,1)} custom-call(bf16[8,72,1024]{2,1,0:T(8,128)(2,1)} %bitcast.67), custom_call_target="tpu_custom_call" | custom-call | tf_op jit(solution)/shard_map/pallas_call | solution.py:160
  104.7 0.0 copy-done.2
  104.7 0.0 copy-done.3
  104.7 0.0 copy-done.4
  104.7 0.8 pad_maximum_fusion.shard_ref
  105.4 77.1 %shard_map.134 = bf16[32,32,5376]{2,1,0:T(8,128)(2,1)} custom-call(bf16[32,5376]{1,0:T(8,128)(2,1)} %pad_maximum_fusion.shard_ref), custom_call_target="tpu_custom_call" | custom-call | tf_op jit(solution)/shard_map/pallas_call | solution.py:109
  182.5 6.7 %fusion.1 = f32[576,1792]{1,0:T(8,128)} fusion(bf16[576,1024]{1,0:T(8,128)(2,1)} %bitcast.64, bf16[1,1024,5376]{2,1,0:T(8,128)(2,1)} %bitcast.61), kind=kOutput, calls=%fused_computation.4 | convolution fusion | flops 2113929216 | bytes 8978432 | tf_op jit(solution)/shard_map/esd,edf->esf/dot_general | solution.py:310
  189.3 0.0 copy-start.6
  189.3 10.3 %fusion.3 = bf16[576,1024]{1,0:T(8,128)(2,1)} fusion(bf16[1,1024,5376]{2,1,0:T(8,128)(2,1)} %bitcast.62, f32[576,1792]{1,0:T(8,128)} %fusion.1, bf16[576,1024]{1,0:T(8,128)(2,1)} %bitcast.65), kind=kOutput, calls=%fused_computation.8 | convolution fusion | flops 4234641408 | bytes 13828096 | tf_op jit(solution)/shard_map/esf,edf->esd/dot_general | solution.py:312
  199.5 19.1 %shard_map.135 = bf16[8,72,1024]{2,1,0:T(8,128)(2,1)} custom-call(bf16[8,72,1024]{2,1,0:T(8,128)(2,1)} %bitcast.66), custom_call_target="tpu_custom_call" | custom-call | tf_op jit(solution)/shard_map/pallas_call | solution.py:160
  218.7 0.1 reduce_sum.30
  218.8 0.1 copy.23
  218.9 0.0 copy-done.6
  218.9 0.2 select_reduce_fusion
  219.1 3.1 %fusion.5 = bf16[1,192,1024]{2,1,0:T(8,128)(2,1)} fusion(f32[192,576]{1,0:T(8,128)S(1)} %select_reduce_fusion, bf16[576,1024]{1,0:T(8,128)(2,1)} %bitcast.63, bf16[192,1024]{1,0:T(8,128)(2,1)S(1)} %get-tuple-element.3), kind=kOutput, calls=%fused_computation.11 | convolution fusion | flops 1359544320 | bytes 2408448 | tf_op jit(solution)/shard_map/dot_general | solution.py:327
  (6 shorter events, 0.1 us)
Async XLA Ops:
  0.6 80.6 %copy-start = (bf16[1024,1024]{1,0:T(8,128)(2,1)S(1)}, bf16[1024,1024]{1,0:T(8,128)(2,1)}, u32[]{:S(2)}) copy-start(bf16[1024,1024]{1,0:T(8,128)(2,1)} %param.17) | copy-start | bytes 6291460
  55.9 25.4 %copy-start.1 = (bf16[1,192,1024]{2,1,0:T(8,128)(2,1)S(1)}, bf16[1,192,1024]{2,1,0:T(8,128)(2,1)}, u32[]{:S(2)}) copy-start(bf16[1,192,1024]{2,1,0:T(8,128)(2,1)} %param.12) | copy-start | bytes 1179652
  55.9 27.7 %copy-start.5 = (f32[1024]{0:T(1024)S(1)}, f32[1024]{0:T(1024)}, u32[]{:S(2)}) copy-start(f32[1024]{0:T(1024)} %param.18) | copy-start | bytes 12292
  83.8 20.9 %copy-start.2 = (bf16[1,32,1792]{2,1,0:T(8,128)(2,1)S(1)}, bf16[1,32,1792]{2,1,0:T(8,128)(2,1)}, u32[]{:S(2)}) copy-start(bf16[1,32,1792]{2,1,0:T(8,128)(2,1)} %param.21) | copy-start | bytes 344068
  85.4 19.2 %copy-start.3 = (bf16[1,32,1792]{2,1,0:T(8,128)(2,1)S(1)}, bf16[1,32,1792]{2,1,0:T(8,128)(2,1)}, u32[]{:S(2)}) copy-start(bf16[1,32,1792]{2,1,0:T(8,128)(2,1)} %param.20) | copy-start | bytes 344068
  85.4 19.2 %copy-start.4 = (bf16[1,32,1792]{2,1,0:T(8,128)(2,1)S(1)}, bf16[1,32,1792]{2,1,0:T(8,128)(2,1)}, u32[]{:S(2)}) copy-start(bf16[1,32,1792]{2,1,0:T(8,128)(2,1)} %param.19) | copy-start | bytes 344068
  189.3 29.6 %copy-start.6 = (f32[1,192,2]{1,2,0:T(2,128)S(1)}, f32[1,192,2]{1,2,0:T(2,128)}, u32[]{:S(2)}) copy-start(f32[1,192,2]{1,2,0:T(2,128)} %param.23) | copy-start | bytes 4612

commit v10 on v8

--- a/solution.py
+++ b/solution.py
@@ -317,7 +317,14 @@
         jnp.concatenate([own_half, from_sibling], axis=0),
         jnp.concatenate([from_sibling, own_half], axis=0),
     )
-    weight_piece = lax.all_gather(chip_rows, CTX_AXES[:2], axis=0, tiled=True)
+    y_hi = lax.axis_index("yh")
+    from_partner = lax.ppermute(chip_rows, "yh", swap)
+    slice_rows = jnp.where(
+        y_hi == 0,
+        jnp.concatenate([chip_rows, from_partner], axis=0),
+        jnp.concatenate([from_partner, chip_rows], axis=0),
+    )
+    weight_piece = lax.all_gather(slice_rows, "z", axis=0, tiled=True)
     gate_piece = weight_piece[:, :half]
     up_piece = weight_piece[:, half : 2 * half]
     down_piece = weight_piece[:, 2 * half :]

time: 200 us -> 196 us (0.980)
  the two profiles are of different devices: /device:TPU:1 before, /device:TPU:48 now
where the time goes in v10:
time: 196 us; the launch traced here: 195 us
  Pallas kernels  117 us (60%)
  matrix products  26.4 us (13%)
  waiting for transfers between devices  20 us (10%)
  between operations  14.2 us (7%)
  local copies, waits for them, and re-layouts  8.48 us (4%)
  other arithmetic  7.63 us (4%)
    pallas_call x2, Pallas kernels, exchange_exp(): pl.pallas_call(functools.partial(exchange_kernel, n_exp), out_shape=jax.S...  51.8 us
    pallas_call x1, Pallas kernels, gather_ctx_kernel(): pl.pallas_call(functools.partial(gather_kernel, n_z), out_shape=jax.Shape...  50.1 us
    pallas_call x1, Pallas kernels, block_attention(): pl.pallas_call(functools.partial(attention_kernel, groups, head_size), ou...  15.5 us
    ppermute x1, waiting for transfers between devices, shards(): from_partner = lax.ppermute(chip_rows, 'yh', swap)  11.3 us
    dot_general x1, matrix products, shards(): lax.dot_general(hidden, down_piece, (((1,), (1,)), ((), ())), preferred_e...  11.2 us
    dot_general x1, matrix products, shards(): jnp.dot(both_tokens, gate_piece, preferred_element_type=jnp.float32)  6.76 us
    ppermute x1, waiting for transfers between devices, shards(): lax.ppermute(partial[slot_rows:], 'core', swap)  4.28 us
  transfers between devices with their start and end apart: 5, of which 4 were waited for; matrix products, arithmetic and copies ran while one was open for 6% of the time, Pallas kernels for 50%

profile of v10, /device:TPU:48, one launch (start us, length us, event | category | flops | bytes accessed | tf_op | source)
XLA Modules:
  0.0 195.3 jit_solution(15145155121074729499)
XLA Ops:
  7.2 0.0 copy-start
  7.2 0.0 copy-start.7
  7.2 0.0 all-gather.2.cloned.1.call-start
  7.3 1.0 fusion.28
  8.3 0.9 fusion.26
  9.2 0.1 broadcast_select_fusion.1
  9.3 0.1 collective-permute-start.1
  9.4 1.4 collective-permute-done.1
  10.8 0.1 maximum_select_fusion.1
  10.8 0.4 collective-permute-start.2
  11.3 11.3 %collective-permute-done.2 = bf16[64,2688]{1,0:T(8,128)(2,1)S(1)} collective-permute-done((bf16[64,2688]{1,0:T(8,128)(2,1)S(1)}, bf16[64,2688]{1,0:T(8,128)(2,1)S(1)}, u32[]{:S(2)}, u32[]{:S(2)}) %collective-permute-start.2) | collective-permute-done | bytes 344096 | tf_op jit(solution)/shard_map/ppermute | solution.py:321
  22.5 1.0 maximum_select_fusion
  23.5 0.0 all-gather.2.cloned.1.call-update
  23.6 0.1 copy.20
  23.7 0.1 eq.64
  23.8 0.1 eq.60
  24.0 0.9 reduce-window.6
  24.9 0.2 slice_reduce_fusion
  25.1 0.0 copy-done.4
  25.2 0.1 reduce_max.14
  25.3 0.0 copy-done.3
  25.3 0.0 copy-done.2
  25.3 0.7 pad_maximum_fusion.4.shard_ref
  26.0 50.1 %shard_map.131 = bf16[32,192,512]{2,1,0:T(8,128)(2,1)} custom-call(bf16[192,512]{1,0:T(8,128)(2,1)} %pad_maximum_fusion.4.shard_ref), custom_call_target="tpu_custom_call" | custom-call | tf_op jit(solution)/shard_map/pallas_call | solution.py:109
  76.1 0.6 reduce_max.18.flag_ref
  76.7 0.6 broadcast_in_dim.32
  77.4 15.5 %shard_map.132 = bf16[192,1024]{1,0:T(8,128)(2,1)} custom-call(s32[48]{0:T(128)} %reduce_max.18.flag_ref, bf16[192,1024]{1,0:T(8,128)(2,1)} %bitcast.48, bf16[6144,512]{1,0:T(8,128)(2,1)} %bitcast.40, bf16[192,192]{1,0:T(8,128)(2,1)} %bitcast.47), custom_call_target="tpu_custom_call" | custom-call | tf_op jit(solution)/shard_map/pallas_call | solution.py:247
  92.9 0.0 copy-done
  92.9 2.4 %fusion.13 = (f32[192]{0:T(256)S(1)}, bf16[192,1024]{1,0:T(8,128)(2,1)S(1)}, bf16[1,192,1024]{2,1,0:T(8,128)(2,1)}) fusion(bf16[1,192,1024]{2,1,0:T(8,128)(2,1)S(1)} %copy-done.1, bf16[192,1024]{1,0:T(8,128)(2,1)} %shard_map.132, bf16[1024,1024]{1,0:T(8,128)(2,1)S(1)} %copy-done), kind=kOutput, calls=%fused_computation.19 | convolution fusion | flops 404029248 | bytes 3670784 | tf_op jit(solution)/shard_map/dot_general | solution.py:284
  95.3 0.2 fusion.15
  95.4 0.4 broadcast_in_dim.37
  95.8 1.2 reshape.74
  97.0 0.1 fusion.19
  97.1 3.0 %convolution_convert_fusion = bf16[576,1024]{1,0:T(8,128)(2,1)} fusion(bf16[384,1024]{1,0:T(8,128)(2,1)} %reshape.74, s32[384]{0:T(512)S(1)} %multiply_add_fusion), kind=kOutput, calls=%fused_computation.10 | convolution fusion | flops 453795840 | bytes 1967616 | tf_op jit(solution)/shard_map/dot_general | solution.py:298
  100.1 32.8 %shard_map.133 = bf16[8,72,1024]{2,1,0:T(8,128)(2,1)} custom-call(bf16[8,72,1024]{2,1,0:T(8,128)(2,1)} %bitcast.46), custom_call_target="tpu_custom_call" | custom-call | tf_op jit(solution)/shard_map/pallas_call | solution.py:160
  132.9 0.4 collective-permute-start
  133.3 3.1 %collective-permute-done = bf16[576,1024]{1,0:T(8,128)(2,1)} collective-permute-done((bf16[576,1024]{1,0:T(8,128)(2,1)}, bf16[576,1024]{1,0:T(8,128)(2,1)}, u32[]{:S(2)}, u32[]{:S(2)}) %collective-permute-start) | collective-permute-done | bytes 1179680 | tf_op jit(solution)/shard_map/ppermute | solution.py:332
  136.4 6.8 %fusion.9 = f32[1152,896]{1,0:T(8,128)} fusion(bf16[1024,2688]{1,0:T(8,128)(2,1)} %all-gather.2.cloned.1.call-done, bf16[576,1024]{1,0:T(8,128)(2,1)} %collective-permute-done, bf16[576,1024]{1,0:T(8,128)(2,1)} %bitcast.44), kind=kOutput, calls=%fused_computation.8 | convolution fusion | flops 2118647808 | bytes 8323072 | tf_op jit(solution)/shard_map/dot_general | solution.py:333
  143.1 11.2 %fusion.1 = f32[1152,1024]{1,0:T(8,128)} fusion(f32[1152,896]{1,0:T(8,128)} %fusion.9, bf16[1024,2688]{1,0:T(8,128)(2,1)} %all-gather.2.cloned.1.call-done, bf16[576,1024]{1,0:T(8,128)(2,1)} %collective-permute-done, bf16[576,1024]{1,0:T(8,128)(2,1)} %bitcast.45), kind=kOutput, calls=%fused_computation.4 | convolution fusion | flops 4238770176 | bytes 14876672 | tf_op jit(solution)/shard_map/dot_general | solution.py:336
  154.3 3.4 %slice.69 = f32[576,1024]{1,0:T(8,128)} slice(f32[1152,1024]{1,0:T(8,128)} %fusion.1), slice={[576:1152], [0:1024]} | slice | bytes 4718592 | tf_op jit(solution)/shard_map/slice | solution.py:341
  157.7 0.1 collective-permute-start.3
  157.8 0.1 reduce_sum.30
  158.0 0.1 copy.23
  158.1 0.2 select_reduce_fusion
  158.3 4.3 %collective-permute-done.3 = f32[576,1024]{1,0:T(8,128)} collective-permute-done((f32[576,1024]{1,0:T(8,128)}, f32[576,1024]{1,0:T(8,128)}, u32[]{:S(2)}, u32[]{:S(2)}) %collective-permute-start.3) | collective-permute-done | bytes 2359328 | tf_op jit(solution)/shard_map/ppermute | solution.py:341
  162.5 3.8 %fusion = bf16[576,1024]{1,0:T(8,128)(2,1)} fusion(f32[576,1024]{1,0:T(8,128)} %collective-permute-done.3, f32[1152,1024]{1,0:T(8,128)} %fusion.1), kind=kLoop, calls=%fused_computation.2 | loop fusion | flops 1179648 | bytes 5898240 | tf_op jit(solution)/shard_map/convert_element_type | solution.py:342
  166.3 19.0 %shard_map.134 = bf16[8,72,1024]{2,1,0:T(8,128)(2,1)} custom-call(bf16[8,72,1024]{2,1,0:T(8,128)(2,1)} %bitcast.42), custom_call_target="tpu_custom_call" | custom-call | tf_op jit(solution)/shard_map/pallas_call | solution.py:160
  185.3 3.1 %fusion.12 = bf16[1,192,1024]{2,1,0:T(8,128)(2,1)} fusion(f32[192,576]{1,0:T(8,128)S(1)} %select_reduce_fusion, bf16[576,1024]{1,0:T(8,128)(2,1)} %bitcast.41, bf16[192,1024]{1,0:T(8,128)(2,1)S(1)} %get-tuple-element.3), kind=kOutput, calls=%fused_computation.13 | convolution fusion | flops 1359544320 | bytes 2408448 | tf_op jit(solution)/shard_map/dot_general | solution.py:352
  (18 shorter events, 0.1 us)
Async XLA Ops:
  7.2 85.7 %copy-start = (bf16[1024,1024]{1,0:T(8,128)(2,1)S(1)}, bf16[1024,1024]{1,0:T(8,128)(2,1)}, u32[]{:S(2)}) copy-start(bf16[1024,1024]{1,0:T(8,128)(2,1)} %param.17) | copy-start | bytes 6291460
  7.2 16.4 %copy-start.7 = (s32[1,192,2]{1,2,0:T(2,128)S(1)}, s32[1,192,2]{1,2,0:T(2,128)}, u32[]{:S(2)}) copy-start(s32[1,192,2]{1,2,0:T(2,128)} %param.22) | copy-start | bytes 4612
  7.2 17.9 %copy-start.4 = (s32[1,6,192]{2,0,1:T(1,128)S(1)}, s32[1,6,192]{2,0,1:T(1,128)}, u32[]{:S(2)}) copy-start(s32[1,6,192]{2,0,1:T(1,128)} %param.16) | copy-start | bytes 13828
  7.2 18.1 %copy-start.3 = (bf16[1,192,256]{2,1,0:T(8,128)(2,1)S(1)}, bf16[1,192,256]{2,1,0:T(8,128)(2,1)}, u32[]{:S(2)}) copy-start(bf16[1,192,256]{2,1,0:T(8,128)(2,1)} %param.14) | copy-start | bytes 294916
  7.2 18.1 %copy-start.2 = (bf16[1,192,256]{2,1,0:T(8,128)(2,1)S(1)}, bf16[1,192,256]{2,1,0:T(8,128)(2,1)}, u32[]{:S(2)}) copy-start(bf16[1,192,256]{2,1,0:T(8,128)(2,1)} %param.15) | copy-start | bytes 294916
  7.2 129.1 %all-gather.2.cloned.1.call-start = ((), (), s32[]{:S(2)}) async-start(), calls=%async_computation | async-start | bytes 6193152 | tf_op jit(solution)/shard_map/all_gather | solution.py:327
  9.3 1.5 collective-permute-start.1
  10.8 11.7 %collective-permute-start.2 = (bf16[64,2688]{1,0:T(8,128)(2,1)S(1)}, bf16[64,2688]{1,0:T(8,128)(2,1)S(1)}, u32[]{:S(2)}, u32[]{:S(2)}) collective-permute-start(bf16[64,2688]{1,0:T(8,128)(2,1)S(1)} %maximum_select_fusion.1), channel_id=1, source_target_pairs={{0,16},{16,0},{1,17},{17,1},{2,18},{18,2},{3,19},{19,3},{4,20},{20... | collective-permute-start | bytes 1032200 | tf_op jit(solution)/shard_map/ppermute | solution.py:321
  77.4 15.5 %copy-start.1 = (bf16[1,192,1024]{2,1,0:T(8,128)(2,1)S(1)}, bf16[1,192,1024]{2,1,0:T(8,128)(2,1)}, u32[]{:S(2)}) copy-start(bf16[1,192,1024]{2,1,0:T(8,128)(2,1)} %param.12) | copy-start | bytes 1179652
  92.9 2.4 %copy-start.5 = (f32[1024]{0:T(1024)S(1)}, f32[1024]{0:T(1024)}, u32[]{:S(2)}) copy-start(f32[1024]{0:T(1024)} %param.18) | copy-start | bytes 12292
  132.9 3.5 %collective-permute-start = (bf16[576,1024]{1,0:T(8,128)(2,1)}, bf16[576,1024]{1,0:T(8,128)(2,1)}, u32[]{:S(2)}, u32[]{:S(2)}) collective-permute-start(bf16[576,1024]{1,0:T(8,128)(2,1)} %bitcast.43), channel_id=1, source_target_pairs={{0,8},{8,0},{1,9},{9,1},{2,10},{10,2},{3,11},{11,3},{4,12},{12,4},... | collective-permute-start | bytes 3538952 | tf_op jit(solution)/shard_map/ppermute | solution.py:332
  154.3 3.7 %copy-start.6 = (f32[1,192,2]{1,2,0:T(2,128)S(1)}, f32[1,192,2]{1,2,0:T(2,128)}, u32[]{:S(2)}) copy-start(f32[1,192,2]{1,2,0:T(2,128)} %param.23) | copy-start | bytes 4612
  157.7 4.9 %collective-permute-start.3 = (f32[576,1024]{1,0:T(8,128)}, f32[576,1024]{1,0:T(8,128)}, u32[]{:S(2)}, u32[]{:S(2)}) collective-permute-start(f32[576,1024]{1,0:T(8,128)} %slice.69), channel_id=1, source_target_pairs={{0,8},{8,0},{1,9},{9,1},{2,10},{10,2},{3,11},{11,3},{4,12},{12,4},... | collective-permute-start | bytes 7077896 | tf_op jit(solution)/shard_map/ppermute | solution.py:341
Sparse Core Ops, SparseCore 0:
  23.7 78.9 all-gather.1

commit v11 on v6

--- a/solution.py
+++ b/solution.py
@@ -305,19 +305,33 @@
     gate_piece = weight_piece[..., :ff]
     up_piece = weight_piece[..., ff : 2 * ff]
     down_piece = weight_piece[..., 2 * ff :]
-    gate_sum = jnp.einsum("esd,edf->esf", arrived, gate_piece, preferred_element_type=jnp.float32)
-    up_sum = jnp.einsum("esd,edf->esf", arrived, up_piece, preferred_element_type=jnp.float32)
-    hidden = (jax.nn.silu(gate_sum) * up_sum).astype(jnp.bfloat16)
-    expert_rows = jnp.einsum(
-        "esf,edf->esd",
-        hidden,
-        down_piece,
-        preferred_element_type=jnp.float32,
-    ).astype(jnp.bfloat16)
-    returned = exchange_exp(expert_rows.reshape(EXPERTS, CAP, D), 2)
+    me = lax.axis_index("exp")
+    tokens_rot = jnp.roll(arrived.reshape(EXPERTS, CAP, D), -me, axis=0)
+
+    def run_rows(chunk_tokens):
+        flat = chunk_tokens.reshape(-1, D)
+        gate_sum = jnp.dot(flat, gate_piece[0], preferred_element_type=jnp.float32)
+        up_sum = jnp.dot(flat, up_piece[0], preferred_element_type=jnp.float32)
+        hidden = (jax.nn.silu(gate_sum) * up_sum).astype(jnp.bfloat16)
+        rows = lax.dot_general(
+            hidden, down_piece[0], (((1,), (1,)), ((), ())), preferred_element_type=jnp.float32
+        )
+        return rows.astype(jnp.bfloat16).reshape(-1, CAP, D)
+
+    split = EXPERTS // 2
+    first_rows = run_rows(tokens_rot[:split])
+    second_rows = run_rows(tokens_rot[split:])
+    received = [first_rows[0]]
+    for offset in range(1, EXPERTS):
+        chunk = first_rows[offset] if offset < split else second_rows[offset - split]
+        received.append(
+            lax.ppermute(chunk, "exp", [(i, (i + offset) % EXPERTS) for i in range(EXPERTS)])
+        )
+    returned = jnp.stack(received)
+    target_rot = lax.rem(me - id_row + EXPERTS, EXPERTS) * CAP + slot_index
     combine = jnp.sum(
         jnp.where(
-            jnp.arange(EXPERTS * CAP, dtype=jnp.int32)[None, None, :] == target.reshape(row_count, TOP)[:, :, None],
+            jnp.arange(EXPERTS * CAP, dtype=jnp.int32)[None, None, :] == target_rot.reshape(row_count, TOP)[:, :, None],
             gate_probs[0][:, :, None],
             0.0,
         ),

time: 176 us -> 186 us (1.057)
  Pallas kernels: 125 us -> 93.9 us
  waiting for transfers between devices: 0.04 us -> 18 us
  starting transfers between devices: 0.04 us -> 8.18 us
  local copies, waits for them, and re-layouts: 3.89 us -> 9.85 us
  matrix products: 25.4 us -> 31.1 us
    pallas_call x2 -> x1, Pallas kernels: 50.7 us -> 20.1 us  [exchange_exp(): pl.pallas_call(functools.partial(exchange_kernel, n_exp), out_shape=jax.S...]
    all_gather x1, waiting for transfers between devices: 0.02 us -> 10.2 us  [shards(): lax.all_gather(jnp.concatenate([gate_weight, up_weight, down_weight], axi...]
    ppermute x0 -> x7, starting transfers between devices: none -> 8.14 us  [shards(): lax.ppermute(chunk, 'exp', [(i, (i + offset) % EXPERTS) for i in range(EX...]
    ppermute x0 -> x7, waiting for transfers between devices: none -> 7.83 us  [shards(): lax.ppermute(chunk, 'exp', [(i, (i + offset) % EXPERTS) for i in range(EX...]
    dot_general x2 -> x4, matrix products: 17 us -> 24 us  [the longest x2 14.3 us: run_rows(): lax.dot_general(hidden, down_piece[0], (((1,), (1,)), ((), ())), preferre...]
    slice x1 -> x4, local copies, waits for them, and re-layouts: 0.22 us -> 4.26 us  [the longest x1 1.82 us: shards(): second_rows[offset - split]]
    unnamed x10 -> x19, local copies, waits for them, and re-layouts: 0.82 us -> 2.72 us
  transfers between devices with their start and end apart: 1 -> 8, of which waited for: 0 -> 6; matrix products, arithmetic and copies ran while one was open for 8% -> 17% of each run, Pallas kernels for 63% -> 51%
where the time goes in v11:
time: 186 us; the launch traced here: 183 us
  Pallas kernels  93.9 us (50%)
  matrix products  31.1 us (17%)
  waiting for transfers between devices  18 us (10%)
  between operations  14.3 us (8%)
  local copies, waits for them, and re-layouts  9.85 us (5%)
  starting transfers between devices  8.18 us (4%)
  other arithmetic  8.09 us (4%)
    pallas_call x1, Pallas kernels, gather_ctx_kernel(): pl.pallas_call(functools.partial(gather_kernel, n_z), out_shape=jax.Shape...  52.6 us
    pallas_call x1, Pallas kernels, block_attention(): pl.pallas_call(functools.partial(attention_kernel, groups, head_size), ou...  21.2 us
    pallas_call x1, Pallas kernels, exchange_exp(): pl.pallas_call(functools.partial(exchange_kernel, n_exp), out_shape=jax.S...  20.1 us
    dot_general x2, matrix products, run_rows(): lax.dot_general(hidden, down_piece[0], (((1,), (1,)), ((), ())), preferre...  14.3 us
    all_gather x1, waiting for transfers between devices, shards(): lax.all_gather(jnp.concatenate([gate_weight, up_weight, down_weight], axi...  10.2 us
    dot_general x2, matrix products, run_rows(): gate_sum = jnp.dot(flat, gate_piece[0], preferred_element_type=jnp.float32)  9.71 us
    ppermute x7, starting transfers between devices, shards(): lax.ppermute(chunk, 'exp', [(i, (i + offset) % EXPERTS) for i in range(EX...  8.14 us
    ppermute x7, waiting for transfers between devices, shards(): lax.ppermute(chunk, 'exp', [(i, (i + offset) % EXPERTS) for i in range(EX...  7.83 us
  transfers between devices with their start and end apart: 8, of which 6 were waited for; matrix products, arithmetic and copies ran while one was open for 17% of the time, Pallas kernels for 51%

profile of v11, /device:TPU:1, one launch (start us, length us, event | category | flops | bytes accessed | tf_op | source)
XLA Modules:
  0.0 183.5 jit_solution(6921488298699551629)
XLA Ops:
  7.2 0.0 all-gather.2.cloned.1.call-start
  7.2 1.9 %pad_maximum_fusion = bf16[1,32,5376]{2,1,0:T(8,128)(2,1)} fusion(bf16[1,32,1792]{2,1,0:T(8,128)(2,1)} %param.21, bf16[1,32,1792]{2,1,0:T(8,128)(2,1)} %param.20, bf16[1,32,1792]{2,1,0:T(8,128)(2,1)} %param.19), kind=kLoop, calls=%fused_computation.36 | loop fusion | flops 1032192 | bytes 688128 | tf_op jit(solution)/shard_map/concatenate | solution.py:303
  9.1 0.0 all-gather.2.cloned.1.call-update
  9.2 0.8 copy.26
  10.0 0.1 eq.59
  10.1 0.1 eq.55
  10.3 0.8 fusion.35
  11.1 0.1 reduce_max.14
  11.2 1.6 pad_maximum_fusion.1.shard_ref
  12.8 52.6 %shard_map.131 = bf16[32,192,512]{2,1,0:T(8,128)(2,1)} custom-call(bf16[192,512]{1,0:T(8,128)(2,1)} %pad_maximum_fusion.1.shard_ref), custom_call_target="tpu_custom_call" | custom-call | tf_op jit(solution)/shard_map/pallas_call | solution.py:109
  65.4 0.6 reduce_max.18.flag_ref
  66.1 0.6 broadcast_in_dim.32
  66.7 21.2 %shard_map.132 = bf16[192,1024]{1,0:T(8,128)(2,1)} custom-call(s32[48]{0:T(128)} %reduce_max.18.flag_ref, bf16[192,1024]{1,0:T(8,128)(2,1)} %bitcast.99, bf16[6144,512]{1,0:T(8,128)(2,1)} %bitcast.91, bf16[192,192]{1,0:T(8,128)(2,1)} %bitcast.98), custom_call_target="tpu_custom_call" | custom-call | tf_op jit(solution)/shard_map/pallas_call | solution.py:245
  88.0 2.4 %fusion.17 = (f32[192]{0:T(256)S(1)}, bf16[192,1024]{1,0:T(8,128)(2,1)S(1)}, bf16[1,192,1024]{2,1,0:T(8,128)(2,1)}) fusion(bf16[1,192,1024]{2,1,0:T(8,128)(2,1)S(1)} %copy-done.1, bf16[192,1024]{1,0:T(8,128)(2,1)} %shard_map.132, bf16[1024,1024]{1,0:T(8,128)(2,1)S(1)} %copy-done), kind=kOutput, calls=%fused_computation.29 | convolution fusion | flops 404029248 | bytes 3670784 | tf_op jit(solution)/shard_map/dot_general | solution.py:282
  90.3 0.2 fusion.19
  90.5 0.4 broadcast_in_dim.37
  90.9 1.2 reshape.104
  92.1 0.8 reduce-window.6
  93.0 0.2 slice_reduce_fusion
  93.2 0.1 fusion.24
  93.3 0.1 reduce_sum.30
  93.5 2.9 %convolution_convert_fusion = bf16[576,1024]{1,0:T(8,128)(2,1)} fusion(bf16[384,1024]{1,0:T(8,128)(2,1)} %reshape.104, s32[384]{0:T(512)S(1)} %multiply_add_fusion), kind=kOutput, calls=%fused_computation.15 | convolution fusion | flops 453795840 | bytes 1967616 | tf_op jit(solution)/shard_map/dot_general | solution.py:296
  96.5 20.1 %shard_map.133 = bf16[8,72,1024]{2,1,0:T(8,128)(2,1)} custom-call(bf16[8,72,1024]{2,1,0:T(8,128)(2,1)} %bitcast.93), custom_call_target="tpu_custom_call" | custom-call | tf_op jit(solution)/shard_map/pallas_call | solution.py:160
  116.6 0.1 copy.28
  116.7 0.2 select_reduce_fusion
  116.9 1.8 fusion.14
  118.6 1.1 fusion.32
  119.8 10.2 %all-gather.2.cloned.1.call-done = bf16[1,1024,5376]{2,1,0:T(8,128)(2,1)} async-done(((bf16[1,32,5376]{2,1,0:T(8,128)(2,1)}), bf16[1,1024,5376]{2,1,0:T(8,128)(2,1)}) %all-gather.2.cloned.1.call-update) | async-done | bytes 11010064 | tf_op jit(solution)/shard_map/all_gather | solution.py:302
  130.0 4.9 %fusion = f32[288,1792]{1,0:T(8,128)} fusion(bf16[288,1024]{1,0:T(8,128)(2,1)} %bitcast.96, bf16[1,1024,5376]{2,1,0:T(8,128)(2,1)} %all-gather.2.cloned.1.call-done), kind=kOutput, calls=%fused_computation.3 | convolution fusion | flops 1056964608 | bytes 6324224 | tf_op jit(solution)/shard_map/dot_general | solution.py:313
  134.9 7.1 %fusion.11 = bf16[288,1024]{1,0:T(8,128)(2,1)} fusion(bf16[1,1024,5376]{2,1,0:T(8,128)(2,1)} %all-gather.2.cloned.1.call-done, bf16[288,1024]{1,0:T(8,128)(2,1)} %bitcast.97, f32[288,1792]{1,0:T(8,128)} %fusion), kind=kOutput, calls=%fused_computation.17 | convolution fusion | flops 2117320704 | bytes 10584064 | tf_op jit(solution)/shard_map/dot_general | solution.py:316
  142.0 1.8 fusion.33
  143.8 0.4 collective-permute-start.3
  144.2 4.8 %fusion.1 = f32[288,1792]{1,0:T(8,128)} fusion(bf16[288,1024]{1,0:T(8,128)(2,1)} %bitcast.94, bf16[1,1024,5376]{2,1,0:T(8,128)(2,1)} %all-gather.2.cloned.1.call-done), kind=kOutput, calls=%fused_computation.4 | convolution fusion | flops 1056964608 | bytes 6324224 | tf_op jit(solution)/shard_map/dot_general | solution.py:313
  149.0 7.1 %fusion.10 = bf16[288,1024]{1,0:T(8,128)(2,1)} fusion(bf16[1,1024,5376]{2,1,0:T(8,128)(2,1)} %all-gather.2.cloned.1.call-done, bf16[288,1024]{1,0:T(8,128)(2,1)} %bitcast.95, f32[288,1792]{1,0:T(8,128)} %fusion.1), kind=kOutput, calls=%fused_computation.16 | convolution fusion | flops 2117320704 | bytes 10584064 | tf_op jit(solution)/shard_map/dot_general | solution.py:316
  156.1 1.1 fusion.34
  157.2 1.2 collective-permute-start
  158.5 2.4 %collective-permute-start.1 = (bf16[72,1024]{1,0:T(8,128)(2,1)S(1)}, bf16[72,1024]{1,0:T(8,128)(2,1)S(1)}, u32[]{:S(2)}, u32[]{:S(2)}) collective-permute-start(bf16[72,1024]{1,0:T(8,128)(2,1)S(1)} %get-tuple-element.12), channel_id=1, source_target_pairs={{0,2},{1,3},{2,4},{3,5},{4,6},{5,7},{6,0},{7,1},{8,10},{9,11},{10,... | collective-permute-start | bytes 442376 | tf_op jit(solution)/shard_map/ppermute | solution.py:328
  160.9 2.0 %collective-permute-start.2 = (bf16[72,1024]{1,0:T(8,128)(2,1)S(1)}, bf16[72,1024]{1,0:T(8,128)(2,1)S(1)}, u32[]{:S(2)}, u32[]{:S(2)}) collective-permute-start(bf16[72,1024]{1,0:T(8,128)(2,1)S(1)} %get-tuple-element.11), channel_id=1, source_target_pairs={{0,3},{1,4},{2,5},{3,6},{4,7},{5,0},{6,1},{7,2},{8,11},{9,12},{10,... | collective-permute-start | bytes 442376 | tf_op jit(solution)/shard_map/ppermute | solution.py:328
  162.9 0.3 collective-permute-start.4
  163.2 0.9 fusion.22
  164.2 0.1 collective-permute-done
  164.3 1.7 collective-permute-start.5
  166.0 3.4 %collective-permute-done.1 = bf16[72,1024]{1,0:T(8,128)(2,1)S(1)} collective-permute-done((bf16[72,1024]{1,0:T(8,128)(2,1)S(1)}, bf16[72,1024]{1,0:T(8,128)(2,1)S(1)}, u32[]{:S(2)}, u32[]{:S(2)}) %collective-permute-start.1) | collective-permute-done | bytes 147488 | tf_op jit(solution)/shard_map/ppermute | solution.py:328
  169.4 0.9 bitcast_dynamic-update-slice_fusion.3
  170.4 0.9 collective-permute-done.4
  171.3 2.5 %collective-permute-done.5 = bf16[72,1024]{1,0:T(8,128)(2,1)S(1)} collective-permute-done((bf16[72,1024]{1,0:T(8,128)(2,1)S(1)}, bf16[72,1024]{1,0:T(8,128)(2,1)S(1)}, u32[]{:S(2)}, u32[]{:S(2)}) %collective-permute-start.5) | collective-permute-done | bytes 147488 | tf_op jit(solution)/shard_map/ppermute | solution.py:328
  173.8 1.0 collective-permute-done.6
  174.8 1.8 fusion.13
  (25 shorter events, 0.2 us)
Async XLA Ops:
  7.2 80.8 %copy-start = (bf16[1024,1024]{1,0:T(8,128)(2,1)S(1)}, bf16[1024,1024]{1,0:T(8,128)(2,1)}, u32[]{:S(2)}) copy-start(bf16[1024,1024]{1,0:T(8,128)(2,1)} %param.17) | copy-start | bytes 6291460
  7.2 122.8 %all-gather.2.cloned.1.call-start = ((), (), s32[]{:S(2)}) async-start(), calls=%async_computation | async-start | bytes 11354112 | tf_op jit(solution)/shard_map/all_gather | solution.py:302
  66.7 21.2 %copy-start.1 = (bf16[1,192,1024]{2,1,0:T(8,128)(2,1)S(1)}, bf16[1,192,1024]{2,1,0:T(8,128)(2,1)}, u32[]{:S(2)}) copy-start(bf16[1,192,1024]{2,1,0:T(8,128)(2,1)} %param.12) | copy-start | bytes 1179652
  88.0 2.4 %copy-start.3 = (f32[1024]{0:T(1024)S(1)}, f32[1024]{0:T(1024)}, u32[]{:S(2)}) copy-start(f32[1024]{0:T(1024)} %param.18) | copy-start | bytes 12292
  93.5 23.2 %copy-start.2 = (s32[1,192,2]{1,2,0:T(2,128)S(1)}, s32[1,192,2]{1,2,0:T(2,128)}, u32[]{:S(2)}) copy-start(s32[1,192,2]{1,2,0:T(2,128)} %param.22) | copy-start | bytes 4612
  93.5 23.2 %copy-start.4 = (f32[1,192,2]{1,2,0:T(2,128)S(1)}, f32[1,192,2]{1,2,0:T(2,128)}, u32[]{:S(2)}) copy-start(f32[1,192,2]{1,2,0:T(2,128)} %param.23) | copy-start | bytes 4612
  143.8 25.6 %collective-permute-start.3 = (bf16[72,1024]{1,0:T(8,128)(2,1)}, bf16[72,1024]{1,0:T(8,128)(2,1)}, u32[]{:S(2)}, u32[]{:S(2)}) collective-permute-start(bf16[72,1024]{1,0:T(8,128)(2,1)} %get-tuple-element.10), channel_id=1, source_target_pairs={{0,4},{1,5},{2,6},{3,7},{4,0},{5,1},{6,2},{7,3},{8,12},{9,13},{10,... | collective-permute-start | bytes 442376 | tf_op jit(solution)/shard_map/ppermute | solution.py:328
  157.2 7.1 %collective-permute-start = (bf16[72,1024]{1,0:T(8,128)(2,1)S(1)}, bf16[72,1024]{1,0:T(8,128)(2,1)S(1)}, u32[]{:S(2)}, u32[]{:S(2)}) collective-permute-start(bf16[72,1024]{1,0:T(8,128)(2,1)S(1)} %get-tuple-element.13), channel_id=1, source_target_pairs={{0,1},{1,2},{2,3},{3,4},{4,5},{5,6},{6,7},{7,0},{8,9},{9,10},{10,1... | collective-permute-start | bytes 442376 | tf_op jit(solution)/shard_map/ppermute | solution.py:328
  158.5 10.9 %collective-permute-start.1 = (bf16[72,1024]{1,0:T(8,128)(2,1)S(1)}, bf16[72,1024]{1,0:T(8,128)(2,1)S(1)}, u32[]{:S(2)}, u32[]{:S(2)}) collective-permute-start(bf16[72,1024]{1,0:T(8,128)(2,1)S(1)} %get-tuple-element.12), channel_id=1, source_target_pairs={{0,2},{1,3},{2,4},{3,5},{4,6},{5,7},{6,0},{7,1},{8,10},{9,11},{10,... | collective-permute-start | bytes 442376 | tf_op jit(solution)/shard_map/ppermute | solution.py:328
  160.9 8.5 %collective-permute-start.2 = (bf16[72,1024]{1,0:T(8,128)(2,1)S(1)}, bf16[72,1024]{1,0:T(8,128)(2,1)S(1)}, u32[]{:S(2)}, u32[]{:S(2)}) collective-permute-start(bf16[72,1024]{1,0:T(8,128)(2,1)S(1)} %get-tuple-element.11), channel_id=1, source_target_pairs={{0,3},{1,4},{2,5},{3,6},{4,7},{5,0},{6,1},{7,2},{8,11},{9,12},{10,... | collective-permute-start | bytes 442376 | tf_op jit(solution)/shard_map/ppermute | solution.py:328
  162.9 8.3 %collective-permute-start.4 = (bf16[72,1024]{1,0:T(8,128)(2,1)S(1)}, bf16[72,1024]{1,0:T(8,128)(2,1)S(1)}, u32[]{:S(2)}, u32[]{:S(2)}) collective-permute-start(bf16[72,1024]{1,0:T(8,128)(2,1)S(1)} %get-tuple-element.9), channel_id=1, source_target_pairs={{0,5},{1,6},{2,7},{3,0},{4,1},{5,2},{6,3},{7,4},{8,13},{9,14},{10,... | collective-permute-start | bytes 442376 | tf_op jit(solution)/shard_map/ppermute | solution.py:328
  164.3 9.5 %collective-permute-start.5 = (bf16[72,1024]{1,0:T(8,128)(2,1)S(1)}, bf16[72,1024]{1,0:T(8,128)(2,1)S(1)}, u32[]{:S(2)}, u32[]{:S(2)}) collective-permute-start(bf16[72,1024]{1,0:T(8,128)(2,1)S(1)} %get-tuple-element.8), channel_id=1, source_target_pairs={{0,6},{1,7},{2,0},{3,1},{4,2},{5,3},{6,4},{7,5},{8,14},{9,15},{10,... | collective-permute-start | bytes 442376 | tf_op jit(solution)/shard_map/ppermute | solution.py:328
  169.4 5.4 %collective-permute-start.6 = (bf16[72,1024]{1,0:T(8,128)(2,1)S(1)}, bf16[72,1024]{1,0:T(8,128)(2,1)S(1)}, u32[]{:S(2)}, u32[]{:S(2)}) collective-permute-start(bf16[72,1024]{1,0:T(8,128)(2,1)S(1)} %get-tuple-element.7), channel_id=1, source_target_pairs={{0,7},{1,0},{2,1},{3,2},{4,3},{5,4},{6,5},{7,6},{8,15},{9,8},{10,9... | collective-permute-start | bytes 442376 | tf_op jit(solution)/shard_map/ppermute | solution.py:328
Sparse Core Ops, SparseCore 0:
  10.8 119.1 all-gather.1

commit v12 on v6

--- a/solution.py
+++ b/solution.py
@@ -305,8 +305,9 @@
     gate_piece = weight_piece[..., :ff]
     up_piece = weight_piece[..., ff : 2 * ff]
     down_piece = weight_piece[..., 2 * ff :]
-    gate_sum = jnp.einsum("esd,edf->esf", arrived, gate_piece, preferred_element_type=jnp.float32)
-    up_sum = jnp.einsum("esd,edf->esf", arrived, up_piece, preferred_element_type=jnp.float32)
+    both_sums = jnp.dot(arrived[0], weight_piece[0, :, : 2 * ff], preferred_element_type=jnp.float32)
+    gate_sum = both_sums[None, :, :ff]
+    up_sum = both_sums[None, :, ff:]
     hidden = (jax.nn.silu(gate_sum) * up_sum).astype(jnp.bfloat16)
     expert_rows = jnp.einsum(
         "esf,edf->esd",

time: 176 us -> 172 us (0.977)
  matrix products: 25.4 us -> 21 us
    pallas_call x2, Pallas kernels: 50.7 us -> 40.6 us  [exchange_exp(): pl.pallas_call(functools.partial(exchange_kernel, n_exp), out_shape=jax.S...]
    pallas_call x1, Pallas kernels: 22 us -> 31.6 us  [block_attention(): pl.pallas_call(functools.partial(attention_kernel, groups, head_size), ou...]
    dot_general x1, matrix products: 10.3 us -> 5.47 us  [shards(): jnp.einsum('esf,edf->esd', hidden, down_piece, preferred_element_type=jnp...]
  transfers between devices with their start and end apart: 1 -> 1, of which waited for: 0 -> 0; matrix products, arithmetic and copies ran while one was open for 8% -> 8% of each run, Pallas kernels for 63% -> 64%
where the time goes in v12:
time: 172 us; the launch traced here: 170 us
  Pallas kernels  125 us (73%)
  matrix products  21 us (12%)
  between operations  14.2 us (8%)
  other arithmetic  6.37 us (4%)
  local copies, waits for them, and re-layouts  3.89 us (2%)
    pallas_call x1, Pallas kernels, gather_ctx_kernel(): pl.pallas_call(functools.partial(gather_kernel, n_z), out_shape=jax.Shape...  52.6 us
    pallas_call x2, Pallas kernels, exchange_exp(): pl.pallas_call(functools.partial(exchange_kernel, n_exp), out_shape=jax.S...  40.6 us
    pallas_call x1, Pallas kernels, block_attention(): pl.pallas_call(functools.partial(attention_kernel, groups, head_size), ou...  31.6 us
    dot_general x1, matrix products, shards(): jnp.dot(arrived[0], weight_piece[0, :, :2 * ff], preferred_element_type=j...  7.08 us
    dot_general x1, matrix products, shards(): jnp.einsum('esf,edf->esd', hidden, down_piece, preferred_element_type=jnp...  5.47 us
  transfers between devices with their start and end apart: 1, of which 0 were waited for; matrix products, arithmetic and copies ran while one was open for 8% of the time, Pallas kernels for 64%

profile of v12, /device:TPU:1, one launch (start us, length us, event | category | flops | bytes accessed | tf_op | source)
XLA Modules:
  0.0 170.3 jit_solution(10652132724707261922)
XLA Ops:
  7.2 0.0 copy-start
  7.2 0.0 all-gather.2.cloned.1.call-start
  7.2 1.9 %pad_maximum_fusion = bf16[1,32,5376]{2,1,0:T(8,128)(2,1)} fusion(bf16[1,32,1792]{2,1,0:T(8,128)(2,1)} %param.21, bf16[1,32,1792]{2,1,0:T(8,128)(2,1)} %param.20, bf16[1,32,1792]{2,1,0:T(8,128)(2,1)} %param.19), kind=kLoop, calls=%fused_computation.23 | loop fusion | flops 1032192 | bytes 688128 | tf_op jit(solution)/shard_map/concatenate | solution.py:303
  9.1 0.0 all-gather.2.cloned.1.call-update
  9.1 0.8 copy.20
  10.0 0.1 eq.56
  10.1 0.1 eq.52
  10.3 0.9 reduce-window.6
  11.1 0.2 slice_reduce_fusion
  11.4 0.8 fusion.19
  12.2 0.1 reduce_max.14
  12.3 1.6 pad_maximum_fusion.1.shard_ref
  13.9 52.6 %shard_map.131 = bf16[32,192,512]{2,1,0:T(8,128)(2,1)} custom-call(bf16[192,512]{1,0:T(8,128)(2,1)} %pad_maximum_fusion.1.shard_ref), custom_call_target="tpu_custom_call" | custom-call | tf_op jit(solution)/shard_map/pallas_call | solution.py:109
  66.5 0.0 copy-start.1
  66.5 0.6 reduce_max.18.flag_ref
  67.2 0.6 broadcast_in_dim.34
  67.8 0.0 copy-start.2
  67.8 31.6 %shard_map.132 = bf16[192,1024]{1,0:T(8,128)(2,1)} custom-call(s32[48]{0:T(128)} %reduce_max.18.flag_ref, bf16[192,1024]{1,0:T(8,128)(2,1)} %bitcast.52, bf16[6144,512]{1,0:T(8,128)(2,1)} %bitcast.46, bf16[192,192]{1,0:T(8,128)(2,1)} %bitcast.51), custom_call_target="tpu_custom_call" | custom-call | tf_op jit(solution)/shard_map/pallas_call | solution.py:245
  99.4 0.0 copy-done
  99.4 0.0 copy-done.1
  99.4 2.4 %fusion.9 = (f32[192]{0:T(256)S(1)}, bf16[192,1024]{1,0:T(8,128)(2,1)S(1)}, bf16[1,192,1024]{2,1,0:T(8,128)(2,1)}) fusion(bf16[1,192,1024]{2,1,0:T(8,128)(2,1)S(1)} %copy-done.1, bf16[192,1024]{1,0:T(8,128)(2,1)} %shard_map.132, bf16[1024,1024]{1,0:T(8,128)(2,1)S(1)} %copy-done), kind=kOutput, calls=%fused_computation.16 | convolution fusion | flops 404029248 | bytes 3670784 | tf_op jit(solution)/shard_map/dot_general | solution.py:282
  101.8 0.0 copy-done.2
  101.8 0.2 fusion.11
  102.0 0.0 copy-start.3
  102.0 0.4 broadcast_in_dim.39
  102.4 1.2 reshape.89
  103.6 0.1 fusion.15
  103.7 0.1 reduce_sum.30
  103.9 2.9 %convolution_convert_fusion = bf16[576,1024]{1,0:T(8,128)(2,1)} fusion(bf16[384,1024]{1,0:T(8,128)(2,1)} %reshape.89, s32[384]{0:T(512)S(1)} %multiply_add_fusion), kind=kOutput, calls=%fused_computation.6 | convolution fusion | flops 453795840 | bytes 1967616 | tf_op jit(solution)/shard_map/dot_general | solution.py:296
  106.8 24.1 %shard_map.133 = bf16[8,72,1024]{2,1,0:T(8,128)(2,1)} custom-call(bf16[8,72,1024]{2,1,0:T(8,128)(2,1)} %bitcast.49), custom_call_target="tpu_custom_call" | custom-call | tf_op jit(solution)/shard_map/pallas_call | solution.py:160
  130.9 0.1 copy.23
  131.0 0.0 copy-done.3
  131.0 0.2 select_reduce_fusion
  131.2 0.0 all-gather.2.cloned.1.call-done
  131.2 7.1 %fusion = f32[576,3584]{1,0:T(8,128)S(1)} fusion(bf16[576,1024]{1,0:T(8,128)(2,1)} %bitcast.48, bf16[1,1024,5376]{2,1,0:T(8,128)(2,1)} %all-gather.2.cloned.1.call-done), kind=kOutput, calls=%fused_computation.1 | convolution fusion | flops 4227858432 | bytes 16777216 | tf_op jit(solution)/shard_map/dot_general | solution.py:308
  138.3 5.5 %fusion.4 = bf16[576,1024]{1,0:T(8,128)(2,1)} fusion(bf16[1,1024,5376]{2,1,0:T(8,128)(2,1)} %all-gather.2.cloned.1.call-done, f32[576,3584]{1,0:T(8,128)S(1)} %fusion), kind=kOutput, calls=%fused_computation.7 | convolution fusion | flops 2120712192 | bytes 13107200 | tf_op jit(solution)/shard_map/esf,edf->esd/dot_general | solution.py:312
  143.8 16.5 %shard_map.134 = bf16[8,72,1024]{2,1,0:T(8,128)(2,1)} custom-call(bf16[8,72,1024]{2,1,0:T(8,128)(2,1)} %bitcast.50), custom_call_target="tpu_custom_call" | custom-call | tf_op jit(solution)/shard_map/pallas_call | solution.py:160
  160.3 3.1 %fusion.8 = bf16[1,192,1024]{2,1,0:T(8,128)(2,1)} fusion(f32[192,576]{1,0:T(8,128)S(1)} %select_reduce_fusion, bf16[576,1024]{1,0:T(8,128)(2,1)} %bitcast.47, bf16[192,1024]{1,0:T(8,128)(2,1)S(1)} %get-tuple-element.3), kind=kOutput, calls=%fused_computation.10 | convolution fusion | flops 1359544320 | bytes 2408448 | tf_op jit(solution)/shard_map/dot_general | solution.py:327
  (6 shorter events, 0.1 us)
Async XLA Ops:
  7.2 92.3 %copy-start = (bf16[1024,1024]{1,0:T(8,128)(2,1)S(1)}, bf16[1024,1024]{1,0:T(8,128)(2,1)}, u32[]{:S(2)}) copy-start(bf16[1024,1024]{1,0:T(8,128)(2,1)} %param.17) | copy-start | bytes 6291460
  7.2 124.1 %all-gather.2.cloned.1.call-start = ((), (), s32[]{:S(2)}) async-start(), calls=%async_computation | async-start | bytes 11354112 | tf_op jit(solution)/shard_map/all_gather | solution.py:302
  66.5 32.9 %copy-start.1 = (bf16[1,192,1024]{2,1,0:T(8,128)(2,1)S(1)}, bf16[1,192,1024]{2,1,0:T(8,128)(2,1)}, u32[]{:S(2)}) copy-start(bf16[1,192,1024]{2,1,0:T(8,128)(2,1)} %param.12) | copy-start | bytes 1179652
  67.8 34.0 %copy-start.2 = (f32[1024]{0:T(1024)S(1)}, f32[1024]{0:T(1024)}, u32[]{:S(2)}) copy-start(f32[1024]{0:T(1024)} %param.18) | copy-start | bytes 12292
  102.0 29.0 %copy-start.3 = (f32[1,192,2]{1,2,0:T(2,128)S(1)}, f32[1,192,2]{1,2,0:T(2,128)}, u32[]{:S(2)}) copy-start(f32[1,192,2]{1,2,0:T(2,128)} %param.23) | copy-start | bytes 4612
Sparse Core Ops, SparseCore 0:
  10.8 118.7 all-gather.1

commit v13 on v12

--- a/solution.py
+++ b/solution.py
@@ -324,12 +324,13 @@
         ),
         axis=1,
     )
-    mixture = jnp.dot(
-        combine,
-        returned.reshape(EXPERTS * CAP, D).astype(jnp.float32),
-        precision=lax.Precision.HIGHEST,
-        preferred_element_type=jnp.float32,
-    )
+    returned_rows = returned.reshape(EXPERTS * CAP, D)
+    mixture = jnp.zeros((row_count, D), jnp.float32)
+    remainder = combine
+    for _ in range(3):
+        part = remainder.astype(jnp.bfloat16)
+        remainder = remainder - part.astype(jnp.float32)
+        mixture = mixture + jnp.dot(part, returned_rows, preferred_element_type=jnp.float32)
     layer_out = (residual.astype(jnp.float32) + mixture).astype(jnp.bfloat16)
     return (attention_out[None], layer_out[None])
 

time: 172 us -> 174 us (1.012)
  waiting for transfers between devices: 0.04 us -> 8.98 us
  Pallas kernels: 125 us -> 118 us
    all_gather x1, waiting for transfers between devices: 0.02 us -> 8.97 us  [shards(): lax.all_gather(jnp.concatenate([gate_weight, up_weight, down_weight], axi...]
    pallas_call x1, Pallas kernels: 31.6 us -> 25.1 us  [block_attention(): pl.pallas_call(functools.partial(attention_kernel, groups, head_size), ou...]
    dot_general x1 -> x3, matrix products: 3.11 us -> 3.55 us  [shards(): jnp.dot(part, returned_rows, preferred_element_type=jnp.float32)]
  transfers between devices with their start and end apart: 1 -> 1, of which waited for: 0 -> 1; matrix products, arithmetic and copies ran while one was open for 8% -> 8% of each run, Pallas kernels for 64% -> 57%
where the time goes in v13:
time: 174 us; the launch traced here: 173 us
  Pallas kernels  118 us (68%)
  matrix products  21.4 us (12%)
  between operations  14.2 us (8%)
  waiting for transfers between devices  8.98 us (5%)
  other arithmetic  6.34 us (4%)
  local copies, waits for them, and re-layouts  3.9 us (2%)
    pallas_call x1, Pallas kernels, gather_ctx_kernel(): pl.pallas_call(functools.partial(gather_kernel, n_z), out_shape=jax.Shape...  52.6 us
    pallas_call x2, Pallas kernels, exchange_exp(): pl.pallas_call(functools.partial(exchange_kernel, n_exp), out_shape=jax.S...  39.9 us
    pallas_call x1, Pallas kernels, block_attention(): pl.pallas_call(functools.partial(attention_kernel, groups, head_size), ou...  25.1 us
    all_gather x1, waiting for transfers between devices, shards(): lax.all_gather(jnp.concatenate([gate_weight, up_weight, down_weight], axi...  8.97 us
    dot_general x1, matrix products, shards(): jnp.dot(arrived[0], weight_piece[0, :, :2 * ff], preferred_element_type=j...  7.07 us
    dot_general x1, matrix products, shards(): jnp.einsum('esf,edf->esd', hidden, down_piece, preferred_element_type=jnp...  5.48 us
    dot_general x3, matrix products, shards(): jnp.dot(part, returned_rows, preferred_element_type=jnp.float32)  3.55 us
  transfers between devices with their start and end apart: 1, of which 1 were waited for; matrix products, arithmetic and copies ran while one was open for 8% of the time, Pallas kernels for 57%

profile of v13, /device:TPU:1, one launch (start us, length us, event | category | flops | bytes accessed | tf_op | source)
XLA Modules:
  0.0 172.5 jit_solution(17192036865661098362)
XLA Ops:
  7.2 0.0 copy-start
  7.2 0.0 all-gather.2.cloned.1.call-start
  7.2 1.9 %pad_maximum_fusion = bf16[1,32,5376]{2,1,0:T(8,128)(2,1)} fusion(bf16[1,32,1792]{2,1,0:T(8,128)(2,1)} %param.21, bf16[1,32,1792]{2,1,0:T(8,128)(2,1)} %param.20, bf16[1,32,1792]{2,1,0:T(8,128)(2,1)} %param.19), kind=kLoop, calls=%fused_computation.27 | loop fusion | flops 1032192 | bytes 688128 | tf_op jit(solution)/shard_map/concatenate | solution.py:303
  9.1 0.0 all-gather.2.cloned.1.call-update
  9.1 0.8 copy.20
  10.0 0.1 eq.56
  10.1 0.1 eq.52
  10.2 0.8 fusion.24
  11.0 0.1 reduce_max.14
  11.1 1.6 pad_maximum_fusion.1.shard_ref
  12.8 52.6 %shard_map.131 = bf16[32,192,512]{2,1,0:T(8,128)(2,1)} custom-call(bf16[192,512]{1,0:T(8,128)(2,1)} %pad_maximum_fusion.1.shard_ref), custom_call_target="tpu_custom_call" | custom-call | tf_op jit(solution)/shard_map/pallas_call | solution.py:109
  65.4 0.6 reduce_max.18.flag_ref
  66.0 0.6 broadcast_in_dim.34
  66.7 0.0 copy-start.2
  66.7 25.1 %shard_map.132 = bf16[192,1024]{1,0:T(8,128)(2,1)} custom-call(s32[48]{0:T(128)} %reduce_max.18.flag_ref, bf16[192,1024]{1,0:T(8,128)(2,1)} %bitcast.55, bf16[6144,512]{1,0:T(8,128)(2,1)} %bitcast.47, bf16[192,192]{1,0:T(8,128)(2,1)} %bitcast.54), custom_call_target="tpu_custom_call" | custom-call | tf_op jit(solution)/shard_map/pallas_call | solution.py:245
  91.8 0.0 copy-done
  91.8 0.0 copy-done.2
  91.8 0.0 copy-start.3
  91.8 2.4 %fusion.10 = (f32[192]{0:T(256)S(1)}, bf16[192,1024]{1,0:T(8,128)(2,1)S(1)}, bf16[1,192,1024]{2,1,0:T(8,128)(2,1)}) fusion(bf16[1,192,1024]{2,1,0:T(8,128)(2,1)S(1)} %copy-done.2, bf16[192,1024]{1,0:T(8,128)(2,1)} %shard_map.132, bf16[1024,1024]{1,0:T(8,128)(2,1)S(1)} %copy-done), kind=kOutput, calls=%fused_computation.18 | convolution fusion | flops 404029248 | bytes 3670784 | tf_op jit(solution)/shard_map/dot_general | solution.py:282
  94.2 0.0 copy-done.3
  94.2 0.2 fusion.12
  94.4 0.4 broadcast_in_dim.39
  94.8 1.2 reshape.89
  96.0 0.8 reduce-window.6
  96.9 0.2 slice_reduce_fusion
  97.1 0.1 fusion.20
  97.2 0.1 reduce_sum.30
  97.4 0.0 copy-start.4
  97.4 2.9 %convolution_convert_fusion = bf16[576,1024]{1,0:T(8,128)(2,1)} fusion(bf16[384,1024]{1,0:T(8,128)(2,1)} %reshape.89, s32[384]{0:T(512)S(1)} %multiply_add_fusion), kind=kOutput, calls=%fused_computation.6 | convolution fusion | flops 453795840 | bytes 1967616 | tf_op jit(solution)/shard_map/dot_general | solution.py:296
  100.3 20.3 %shard_map.133 = bf16[8,72,1024]{2,1,0:T(8,128)(2,1)} custom-call(bf16[8,72,1024]{2,1,0:T(8,128)(2,1)} %bitcast.52), custom_call_target="tpu_custom_call" | custom-call | tf_op jit(solution)/shard_map/pallas_call | solution.py:160
  120.7 0.1 copy.23
  120.7 0.0 copy-done.4
  120.7 0.2 select_reduce_fusion
  120.9 9.0 %all-gather.2.cloned.1.call-done = bf16[1,1024,5376]{2,1,0:T(8,128)(2,1)} async-done(((bf16[1,32,5376]{2,1,0:T(8,128)(2,1)}), bf16[1,1024,5376]{2,1,0:T(8,128)(2,1)}) %all-gather.2.cloned.1.call-update) | async-done | bytes 11010064 | tf_op jit(solution)/shard_map/all_gather | solution.py:302
  129.9 7.1 %fusion = f32[576,3584]{1,0:T(8,128)S(1)} fusion(bf16[576,1024]{1,0:T(8,128)(2,1)} %bitcast.51, bf16[1,1024,5376]{2,1,0:T(8,128)(2,1)} %all-gather.2.cloned.1.call-done), kind=kOutput, calls=%fused_computation.1 | convolution fusion | flops 4227858432 | bytes 16777216 | tf_op jit(solution)/shard_map/dot_general | solution.py:308
  137.0 5.5 %fusion.4 = bf16[576,1024]{1,0:T(8,128)(2,1)} fusion(bf16[1,1024,5376]{2,1,0:T(8,128)(2,1)} %all-gather.2.cloned.1.call-done, f32[576,3584]{1,0:T(8,128)S(1)} %fusion), kind=kOutput, calls=%fused_computation.7 | convolution fusion | flops 2120712192 | bytes 13107200 | tf_op jit(solution)/shard_map/esf,edf->esd/dot_general | solution.py:312
  142.5 19.6 %shard_map.134 = bf16[8,72,1024]{2,1,0:T(8,128)(2,1)} custom-call(bf16[8,72,1024]{2,1,0:T(8,128)(2,1)} %bitcast.53), custom_call_target="tpu_custom_call" | custom-call | tf_op jit(solution)/shard_map/pallas_call | solution.py:160
  162.1 0.0 copy-start.1
  162.1 1.8 %fusion.16 = f32[192,1024]{1,0:T(8,128)S(1)} fusion(bf16[576,1024]{1,0:T(8,128)(2,1)} %bitcast.48, f32[192,576]{1,0:T(8,128)S(1)} %select_reduce_fusion), kind=kOutput, calls=%fused_computation.29 | convolution fusion | flops 226603008 | bytes 2408448 | tf_op jit(solution)/shard_map/dot_general | solution.py:333
  164.0 0.0 copy-done.1
  164.0 0.5 convolution_add_fusion.1
  164.5 1.2 fusion.9
  (6 shorter events, 0.1 us)
Async XLA Ops:
  7.2 84.7 %copy-start = (bf16[1024,1024]{1,0:T(8,128)(2,1)S(1)}, bf16[1024,1024]{1,0:T(8,128)(2,1)}, u32[]{:S(2)}) copy-start(bf16[1024,1024]{1,0:T(8,128)(2,1)} %param.17) | copy-start | bytes 6291460
  7.2 122.7 %all-gather.2.cloned.1.call-start = ((), (), s32[]{:S(2)}) async-start(), calls=%async_computation | async-start | bytes 11354112 | tf_op jit(solution)/shard_map/all_gather | solution.py:302
  66.7 25.1 %copy-start.2 = (bf16[1,192,1024]{2,1,0:T(8,128)(2,1)S(1)}, bf16[1,192,1024]{2,1,0:T(8,128)(2,1)}, u32[]{:S(2)}) copy-start(bf16[1,192,1024]{2,1,0:T(8,128)(2,1)} %param.12) | copy-start | bytes 1179652
  91.8 2.4 %copy-start.3 = (f32[1024]{0:T(1024)S(1)}, f32[1024]{0:T(1024)}, u32[]{:S(2)}) copy-start(f32[1024]{0:T(1024)} %param.18) | copy-start | bytes 12292
  97.4 23.4 %copy-start.4 = (f32[1,192,2]{1,2,0:T(2,128)S(1)}, f32[1,192,2]{1,2,0:T(2,128)}, u32[]{:S(2)}) copy-start(f32[1,192,2]{1,2,0:T(2,128)} %param.23) | copy-start | bytes 4612
  162.1 1.9 %copy-start.1 = (bf16[8,72,1024]{2,1,0:T(8,128)(2,1)S(1)}, bf16[8,72,1024]{2,1,0:T(8,128)(2,1)}, u32[]{:S(2)}) copy-start(bf16[8,72,1024]{2,1,0:T(8,128)(2,1)} %shard_map.134) | copy-start | bytes 3538948
Sparse Core Ops, SparseCore 0:
  10.8 119.0 all-gather.1

commit v14 on v12

--- a/solution.py
+++ b/solution.py
@@ -120,36 +120,93 @@
     )(block)
 
 
-def exchange_kernel(n_exp, chunk_ref, out_ref, local_sem, send_sem, recv_sem):
+RELAY_ROWS = 32
+
+
+def exchange_kernel(n_exp, chunk_ref, out_ref, relay_buf, local_sem, send_sem, recv_sem, relay_send, relay_in, fwd_send, relay_recv):
     me = lax.axis_index("exp")
     z = lax.axis_index("z")
     yh = lax.axis_index("yh")
     core = lax.axis_index("core")
-
-    def peer(offset):
-        return lax.rem(me + offset, n_exp)
+    n_x = n_exp // 2
+    x = me % n_x
+    row = me // n_x
+    rows = chunk_ref.shape[1]
+    near = pl.ds(0, RELAY_ROWS)
+    far = pl.ds(RELAY_ROWS, rows - RELAY_ROWS)
+
+    def device(r, xx):
+        return (z, yh, core, r * n_x + lax.rem(xx + 2 * n_x, n_x))
 
     barrier = pltpu.get_barrier_semaphore()
     for offset in range(1, n_exp):
-        pl.semaphore_signal(barrier, 1, device_id=(z, yh, core, peer(offset)), device_id_type=MESH)
+        pl.semaphore_signal(barrier, 1, device_id=(z, yh, core, lax.rem(me + offset, n_exp)), device_id_type=MESH)
     pl.semaphore_wait(barrier, n_exp - 1)
     own = pltpu.make_async_copy(chunk_ref.at[me], out_ref.at[me], local_sem)
     own.start()
     sends = []
-    for offset in range(1, n_exp):
-        target = peer(offset)
+    relay_at = device(row, x - 1)
+    for r_off in range(2):
+        target_row = lax.rem(row + r_off, 2)
+        for dx in range(n_x):
+            if r_off == 0 and dx == 0:
+                continue
+            target = device(target_row, x + dx)
+            target_index = target[3]
+            slot = r_off * n_x + dx
+            if dx == n_x // 2:
+                copy = pltpu.make_async_remote_copy(
+                    chunk_ref.at[target_index, far], out_ref.at[me, far], send_sem.at[slot], recv_sem.at[me],
+                    device_id=target, device_id_type=MESH,
+                )
+                copy.start()
+                sends.append(copy)
+                copy = pltpu.make_async_remote_copy(
+                    chunk_ref.at[target_index, near], relay_buf.at[r_off], relay_send.at[r_off], relay_in.at[r_off],
+                    device_id=relay_at, device_id_type=MESH,
+                )
+                copy.start()
+                sends.append(copy)
+            else:
+                copy = pltpu.make_async_remote_copy(
+                    chunk_ref.at[target_index], out_ref.at[me], send_sem.at[slot], recv_sem.at[me],
+                    device_id=target, device_id_type=MESH,
+                )
+                copy.start()
+                sends.append(copy)
+    relayed_source = device(row, x + 1)[3]
+    for r_off in range(2):
+        pltpu.make_async_remote_copy(
+            relay_buf.at[r_off], relay_buf.at[r_off], relay_send.at[r_off], relay_in.at[r_off],
+            device_id=relay_at, device_id_type=MESH,
+        ).wait_recv()
+        target = device(lax.rem(row + r_off, 2), x - 1)
         copy = pltpu.make_async_remote_copy(
-            chunk_ref.at[target], out_ref.at[me], send_sem.at[offset], recv_sem.at[me],
-            device_id=(z, yh, core, target), device_id_type=MESH,
+            relay_buf.at[r_off], out_ref.at[relayed_source, near], fwd_send.at[r_off], relay_recv.at[relayed_source],
+            device_id=target, device_id_type=MESH,
         )
         copy.start()
         sends.append(copy)
-    for offset in range(1, n_exp):
-        source = peer(n_exp - offset)
-        pltpu.make_async_remote_copy(
-            out_ref.at[source], out_ref.at[source], send_sem.at[offset], recv_sem.at[source],
-            device_id=(z, yh, core, source), device_id_type=MESH,
-        ).wait_recv()
+    for r_off in range(2):
+        source_row = lax.rem(row + r_off, 2)
+        for dx in range(n_x):
+            if r_off == 0 and dx == 0:
+                continue
+            source = device(source_row, x + dx)[3]
+            if dx == n_x // 2:
+                pltpu.make_async_remote_copy(
+                    out_ref.at[source, far], out_ref.at[source, far], send_sem.at[0], recv_sem.at[source],
+                    device_id=relay_at, device_id_type=MESH,
+                ).wait_recv()
+                pltpu.make_async_remote_copy(
+                    out_ref.at[source, near], out_ref.at[source, near], send_sem.at[0], relay_recv.at[source],
+                    device_id=relay_at, device_id_type=MESH,
+                ).wait_recv()
+            else:
+                pltpu.make_async_remote_copy(
+                    out_ref.at[source], out_ref.at[source], send_sem.at[0], recv_sem.at[source],
+                    device_id=relay_at, device_id_type=MESH,
+                ).wait_recv()
     own.wait()
     for copy in sends:
         copy.wait_send()
@@ -163,8 +220,13 @@
         in_specs=[pl.BlockSpec(memory_space=pl.ANY)],
         out_specs=pl.BlockSpec(memory_space=pl.ANY),
         scratch_shapes=[
+            pltpu.VMEM((2, RELAY_ROWS) + chunks.shape[2:], chunks.dtype),
             pltpu.SemaphoreType.DMA(()),
             pltpu.SemaphoreType.DMA((n_exp,)),
+            pltpu.SemaphoreType.DMA((n_exp,)),
+            pltpu.SemaphoreType.DMA((2,)),
+            pltpu.SemaphoreType.DMA((2,)),
+            pltpu.SemaphoreType.DMA((2,)),
             pltpu.SemaphoreType.DMA((n_exp,)),
         ],
         compiler_params=pltpu.CompilerParams(collective_id=collective_id, has_side_effects=True),

time: 172 us -> 174 us (1.012)
  waiting for transfers between devices: 0.04 us -> 2.32 us
    pallas_call x1, Pallas kernels: 31.6 us -> 35.5 us  [block_attention(): pl.pallas_call(functools.partial(attention_kernel, groups, head_size), ou...]
    pallas_call x2, Pallas kernels: 40.6 us -> 37.6 us  [exchange_exp(): pl.pallas_call(functools.partial(exchange_kernel, n_exp), out_shape=jax.S...]
    all_gather x1, waiting for transfers between devices: 0.02 us -> 2.3 us  [shards(): lax.all_gather(jnp.concatenate([gate_weight, up_weight, down_weight], axi...]
  transfers between devices with their start and end apart: 1 -> 1, of which waited for: 0 -> 1; matrix products, arithmetic and copies ran while one was open for 8% -> 8% of each run, Pallas kernels for 64% -> 60%
where the time goes in v14:
time: 174 us
  Pallas kernels  126 us (72%)
  matrix products  21.1 us (12%)
  between operations  14.2 us (8%)
  other arithmetic  6.35 us (4%)
  local copies, waits for them, and re-layouts  3.9 us (2%)
  waiting for transfers between devices  2.32 us (1%)
    pallas_call x1, Pallas kernels, gather_ctx_kernel(): pl.pallas_call(functools.partial(gather_kernel, n_z), out_shape=jax.Shape...  52.6 us
    pallas_call x2, Pallas kernels, exchange_exp(): pl.pallas_call(functools.partial(exchange_kernel, n_exp), out_shape=jax.S...  37.6 us
    pallas_call x1, Pallas kernels, block_attention(): pl.pallas_call(functools.partial(attention_kernel, groups, head_size), ou...  35.5 us
    dot_general x1, matrix products, shards(): jnp.dot(arrived[0], weight_piece[0, :, :2 * ff], preferred_element_type=j...  7.07 us
    dot_general x1, matrix products, shards(): jnp.einsum('esf,edf->esd', hidden, down_piece, preferred_element_type=jnp...  5.48 us
  transfers between devices with their start and end apart: 1, of which 1 were waited for; matrix products, arithmetic and copies ran while one was open for 8% of the time, Pallas kernels for 60%

profile of v14, /device:TPU:1, one launch (start us, length us, event | category | flops | bytes accessed | tf_op | source)
XLA Modules:
  0.0 173.5 jit_solution(18388896337058018245)
XLA Ops:
  7.2 0.0 copy-start
  7.2 0.0 all-gather.2.cloned.1.call-start
  7.2 1.9 %pad_maximum_fusion = bf16[1,32,5376]{2,1,0:T(8,128)(2,1)} fusion(bf16[1,32,1792]{2,1,0:T(8,128)(2,1)} %param.21, bf16[1,32,1792]{2,1,0:T(8,128)(2,1)} %param.20, bf16[1,32,1792]{2,1,0:T(8,128)(2,1)} %param.19), kind=kLoop, calls=%fused_computation.23 | loop fusion | flops 1032192 | bytes 688128 | tf_op jit(solution)/shard_map/concatenate | solution.py:365
  9.1 0.0 all-gather.2.cloned.1.call-update
  9.1 0.8 copy.20
  10.0 0.1 eq.56
  10.1 0.1 eq.52
  10.3 0.9 reduce-window.6
  11.1 0.2 slice_reduce_fusion
  11.4 0.8 fusion.19
  12.2 0.1 reduce_max.14
  12.3 1.6 pad_maximum_fusion.1.shard_ref
  13.9 52.6 %shard_map.131 = bf16[32,192,512]{2,1,0:T(8,128)(2,1)} custom-call(bf16[192,512]{1,0:T(8,128)(2,1)} %pad_maximum_fusion.1.shard_ref), custom_call_target="tpu_custom_call" | custom-call | tf_op jit(solution)/shard_map/pallas_call | solution.py:109
  66.5 0.0 copy-start.1
  66.5 0.6 reduce_max.18.flag_ref
  67.2 0.6 broadcast_in_dim.34
  67.8 0.0 copy-start.2
  67.8 35.5 %shard_map.132 = bf16[192,1024]{1,0:T(8,128)(2,1)} custom-call(s32[48]{0:T(128)} %reduce_max.18.flag_ref, bf16[192,1024]{1,0:T(8,128)(2,1)} %bitcast.52, bf16[6144,512]{1,0:T(8,128)(2,1)} %bitcast.46, bf16[192,192]{1,0:T(8,128)(2,1)} %bitcast.51), custom_call_target="tpu_custom_call" | custom-call | tf_op jit(solution)/shard_map/pallas_call | solution.py:307
  103.3 0.0 copy-done
  103.3 0.0 copy-done.1
  103.3 2.5 %fusion.9 = (f32[192]{0:T(256)S(1)}, bf16[192,1024]{1,0:T(8,128)(2,1)S(1)}, bf16[1,192,1024]{2,1,0:T(8,128)(2,1)}) fusion(bf16[1,192,1024]{2,1,0:T(8,128)(2,1)S(1)} %copy-done.1, bf16[192,1024]{1,0:T(8,128)(2,1)} %shard_map.132, bf16[1024,1024]{1,0:T(8,128)(2,1)S(1)} %copy-done), kind=kOutput, calls=%fused_computation.16 | convolution fusion | flops 404029248 | bytes 3670784 | tf_op jit(solution)/shard_map/dot_general | solution.py:344
  105.8 0.0 copy-done.2
  105.8 0.2 fusion.11
  106.0 0.0 copy-start.3
  106.0 0.4 broadcast_in_dim.39
  106.4 1.2 reshape.89
  107.6 0.1 fusion.15
  107.7 0.1 reduce_sum.30
  107.8 3.0 %convolution_convert_fusion = bf16[576,1024]{1,0:T(8,128)(2,1)} fusion(bf16[384,1024]{1,0:T(8,128)(2,1)} %reshape.89, s32[384]{0:T(512)S(1)} %multiply_add_fusion), kind=kOutput, calls=%fused_computation.6 | convolution fusion | flops 453795840 | bytes 1967616 | tf_op jit(solution)/shard_map/dot_general | solution.py:358
  110.8 16.1 %shard_map.133 = bf16[8,72,1024]{2,1,0:T(8,128)(2,1)} custom-call(bf16[8,72,1024]{2,1,0:T(8,128)(2,1)} %bitcast.49), custom_call_target="tpu_custom_call" | custom-call | tf_op jit(solution)/shard_map/pallas_call | solution.py:217
  126.9 0.1 copy.23
  127.0 0.0 copy-done.3
  127.0 0.2 select_reduce_fusion
  127.2 2.3 %all-gather.2.cloned.1.call-done = bf16[1,1024,5376]{2,1,0:T(8,128)(2,1)} async-done(((bf16[1,32,5376]{2,1,0:T(8,128)(2,1)}), bf16[1,1024,5376]{2,1,0:T(8,128)(2,1)}) %all-gather.2.cloned.1.call-update) | async-done | bytes 11010064 | tf_op jit(solution)/shard_map/all_gather | solution.py:364
  129.5 7.1 %fusion = f32[576,3584]{1,0:T(8,128)S(1)} fusion(bf16[576,1024]{1,0:T(8,128)(2,1)} %bitcast.48, bf16[1,1024,5376]{2,1,0:T(8,128)(2,1)} %all-gather.2.cloned.1.call-done), kind=kOutput, calls=%fused_computation.1 | convolution fusion | flops 4227858432 | bytes 16777216 | tf_op jit(solution)/shard_map/dot_general | solution.py:370
  136.6 5.5 %fusion.4 = bf16[576,1024]{1,0:T(8,128)(2,1)} fusion(bf16[1,1024,5376]{2,1,0:T(8,128)(2,1)} %all-gather.2.cloned.1.call-done, f32[576,3584]{1,0:T(8,128)S(1)} %fusion), kind=kOutput, calls=%fused_computation.7 | convolution fusion | flops 2120712192 | bytes 13107200 | tf_op jit(solution)/shard_map/esf,edf->esd/dot_general | solution.py:374
  142.1 21.5 %shard_map.134 = bf16[8,72,1024]{2,1,0:T(8,128)(2,1)} custom-call(bf16[8,72,1024]{2,1,0:T(8,128)(2,1)} %bitcast.50), custom_call_target="tpu_custom_call" | custom-call | tf_op jit(solution)/shard_map/pallas_call | solution.py:217
  163.6 3.1 %fusion.8 = bf16[1,192,1024]{2,1,0:T(8,128)(2,1)} fusion(f32[192,576]{1,0:T(8,128)S(1)} %select_reduce_fusion, bf16[576,1024]{1,0:T(8,128)(2,1)} %bitcast.47, bf16[192,1024]{1,0:T(8,128)(2,1)S(1)} %get-tuple-element.3), kind=kOutput, calls=%fused_computation.10 | convolution fusion | flops 1359544320 | bytes 2408448 | tf_op jit(solution)/shard_map/dot_general | solution.py:389
  (6 shorter events, 0.1 us)
Async XLA Ops:
  7.2 96.2 %copy-start = (bf16[1024,1024]{1,0:T(8,128)(2,1)S(1)}, bf16[1024,1024]{1,0:T(8,128)(2,1)}, u32[]{:S(2)}) copy-start(bf16[1024,1024]{1,0:T(8,128)(2,1)} %param.17) | copy-start | bytes 6291460
  7.2 122.3 %all-gather.2.cloned.1.call-start = ((), (), s32[]{:S(2)}) async-start(), calls=%async_computation | async-start | bytes 11354112 | tf_op jit(solution)/shard_map/all_gather | solution.py:364
  66.5 36.8 %copy-start.1 = (bf16[1,192,1024]{2,1,0:T(8,128)(2,1)S(1)}, bf16[1,192,1024]{2,1,0:T(8,128)(2,1)}, u32[]{:S(2)}) copy-start(bf16[1,192,1024]{2,1,0:T(8,128)(2,1)} %param.12) | copy-start | bytes 1179652
  67.8 38.0 %copy-start.2 = (f32[1024]{0:T(1024)S(1)}, f32[1024]{0:T(1024)}, u32[]{:S(2)}) copy-start(f32[1024]{0:T(1024)} %param.18) | copy-start | bytes 12292
  106.0 21.0 %copy-start.3 = (f32[1,192,2]{1,2,0:T(2,128)S(1)}, f32[1,192,2]{1,2,0:T(2,128)}, u32[]{:S(2)}) copy-start(f32[1,192,2]{1,2,0:T(2,128)} %param.23) | copy-start | bytes 4612
Sparse Core Ops, SparseCore 0:
  10.8 118.6 all-gather.1

commit v15 on v12

--- a/solution.py
+++ b/solution.py
@@ -327,7 +327,7 @@
     mixture = jnp.dot(
         combine,
         returned.reshape(EXPERTS * CAP, D).astype(jnp.float32),
-        precision=lax.Precision.HIGHEST,
+        precision=lax.Precision.HIGH,
         preferred_element_type=jnp.float32,
     )
     layer_out = (residual.astype(jnp.float32) + mixture).astype(jnp.bfloat16)

time: 172 us -> 172 us (level)
  waiting for transfers between devices: 0.04 us -> 6.54 us
  Pallas kernels: 125 us -> 120 us
    all_gather x1, waiting for transfers between devices: 0.02 us -> 6.53 us  [shards(): lax.all_gather(jnp.concatenate([gate_weight, up_weight, down_weight], axi...]
    pallas_call x1, Pallas kernels: 31.6 us -> 25.7 us  [block_attention(): pl.pallas_call(functools.partial(attention_kernel, groups, head_size), ou...]
  transfers between devices with their start and end apart: 1 -> 1, of which waited for: 0 -> 1; matrix products, arithmetic and copies ran while one was open for 8% -> 8% of each run, Pallas kernels for 64% -> 58%
where the time goes in v15:
time: 172 us; the launch traced here: 171 us
  Pallas kernels  120 us (70%)
  matrix products  20.6 us (12%)
  between operations  14.2 us (8%)
  waiting for transfers between devices  6.54 us (4%)
  other arithmetic  6.37 us (4%)
  local copies, waits for them, and re-layouts  3.89 us (2%)
    pallas_call x1, Pallas kernels, gather_ctx_kernel(): pl.pallas_call(functools.partial(gather_kernel, n_z), out_shape=jax.Shape...  52.6 us
    pallas_call x2, Pallas kernels, exchange_exp(): pl.pallas_call(functools.partial(exchange_kernel, n_exp), out_shape=jax.S...  41.4 us
    pallas_call x1, Pallas kernels, block_attention(): pl.pallas_call(functools.partial(attention_kernel, groups, head_size), ou...  25.7 us
    dot_general x1, matrix products, shards(): jnp.dot(arrived[0], weight_piece[0, :, :2 * ff], preferred_element_type=j...  7.07 us
    all_gather x1, waiting for transfers between devices, shards(): lax.all_gather(jnp.concatenate([gate_weight, up_weight, down_weight], axi...  6.53 us
    dot_general x1, matrix products, shards(): jnp.einsum('esf,edf->esd', hidden, down_piece, preferred_element_type=jnp...  5.48 us
  transfers between devices with their start and end apart: 1, of which 1 were waited for; matrix products, arithmetic and copies ran while one was open for 8% of the time, Pallas kernels for 58%

profile of v15, /device:TPU:1, one launch (start us, length us, event | category | flops | bytes accessed | tf_op | source)
XLA Modules:
  0.0 171.4 jit_solution(12486105378781727444)
XLA Ops:
  7.2 0.0 copy-start
  7.2 0.0 all-gather.2.cloned.1.call-start
  7.2 1.9 %pad_maximum_fusion = bf16[1,32,5376]{2,1,0:T(8,128)(2,1)} fusion(bf16[1,32,1792]{2,1,0:T(8,128)(2,1)} %param.21, bf16[1,32,1792]{2,1,0:T(8,128)(2,1)} %param.20, bf16[1,32,1792]{2,1,0:T(8,128)(2,1)} %param.19), kind=kLoop, calls=%fused_computation.23 | loop fusion | flops 1032192 | bytes 688128 | tf_op jit(solution)/shard_map/concatenate | solution.py:303
  9.1 0.0 all-gather.2.cloned.1.call-update
  9.1 0.8 copy.20
  10.0 0.1 eq.56
  10.1 0.1 eq.52
  10.3 0.9 reduce-window.6
  11.1 0.2 slice_reduce_fusion
  11.4 0.8 fusion.19
  12.2 0.1 reduce_max.14
  12.3 1.6 pad_maximum_fusion.1.shard_ref
  13.9 52.6 %shard_map.131 = bf16[32,192,512]{2,1,0:T(8,128)(2,1)} custom-call(bf16[192,512]{1,0:T(8,128)(2,1)} %pad_maximum_fusion.1.shard_ref), custom_call_target="tpu_custom_call" | custom-call | tf_op jit(solution)/shard_map/pallas_call | solution.py:109
  66.5 0.0 copy-start.1
  66.5 0.6 reduce_max.18.flag_ref
  67.2 0.6 broadcast_in_dim.34
  67.8 0.0 copy-start.2
  67.8 25.7 %shard_map.132 = bf16[192,1024]{1,0:T(8,128)(2,1)} custom-call(s32[48]{0:T(128)} %reduce_max.18.flag_ref, bf16[192,1024]{1,0:T(8,128)(2,1)} %bitcast.52, bf16[6144,512]{1,0:T(8,128)(2,1)} %bitcast.46, bf16[192,192]{1,0:T(8,128)(2,1)} %bitcast.51), custom_call_target="tpu_custom_call" | custom-call | tf_op jit(solution)/shard_map/pallas_call | solution.py:245
  93.6 0.0 copy-done
  93.6 0.0 copy-done.1
  93.6 2.4 %fusion.9 = (f32[192]{0:T(256)S(1)}, bf16[192,1024]{1,0:T(8,128)(2,1)S(1)}, bf16[1,192,1024]{2,1,0:T(8,128)(2,1)}) fusion(bf16[1,192,1024]{2,1,0:T(8,128)(2,1)S(1)} %copy-done.1, bf16[192,1024]{1,0:T(8,128)(2,1)} %shard_map.132, bf16[1024,1024]{1,0:T(8,128)(2,1)S(1)} %copy-done), kind=kOutput, calls=%fused_computation.16 | convolution fusion | flops 404029248 | bytes 3670784 | tf_op jit(solution)/shard_map/dot_general | solution.py:282
  96.0 0.0 copy-done.2
  96.0 0.2 fusion.11
  96.1 0.0 copy-start.3
  96.1 0.4 broadcast_in_dim.39
  96.6 1.2 reshape.89
  97.8 0.1 fusion.15
  97.8 0.1 reduce_sum.30
  98.0 2.9 %convolution_convert_fusion = bf16[576,1024]{1,0:T(8,128)(2,1)} fusion(bf16[384,1024]{1,0:T(8,128)(2,1)} %reshape.89, s32[384]{0:T(512)S(1)} %multiply_add_fusion), kind=kOutput, calls=%fused_computation.6 | convolution fusion | flops 453795840 | bytes 1967616 | tf_op jit(solution)/shard_map/dot_general | solution.py:296
  100.9 21.8 %shard_map.133 = bf16[8,72,1024]{2,1,0:T(8,128)(2,1)} custom-call(bf16[8,72,1024]{2,1,0:T(8,128)(2,1)} %bitcast.49), custom_call_target="tpu_custom_call" | custom-call | tf_op jit(solution)/shard_map/pallas_call | solution.py:160
  122.8 0.1 copy.23
  122.9 0.0 copy-done.3
  122.9 0.2 select_reduce_fusion
  123.1 6.5 %all-gather.2.cloned.1.call-done = bf16[1,1024,5376]{2,1,0:T(8,128)(2,1)} async-done(((bf16[1,32,5376]{2,1,0:T(8,128)(2,1)}), bf16[1,1024,5376]{2,1,0:T(8,128)(2,1)}) %all-gather.2.cloned.1.call-update) | async-done | bytes 11010064 | tf_op jit(solution)/shard_map/all_gather | solution.py:302
  129.6 7.1 %fusion = f32[576,3584]{1,0:T(8,128)S(1)} fusion(bf16[576,1024]{1,0:T(8,128)(2,1)} %bitcast.48, bf16[1,1024,5376]{2,1,0:T(8,128)(2,1)} %all-gather.2.cloned.1.call-done), kind=kOutput, calls=%fused_computation.1 | convolution fusion | flops 4227858432 | bytes 16777216 | tf_op jit(solution)/shard_map/dot_general | solution.py:308
  136.7 5.5 %fusion.4 = bf16[576,1024]{1,0:T(8,128)(2,1)} fusion(bf16[1,1024,5376]{2,1,0:T(8,128)(2,1)} %all-gather.2.cloned.1.call-done, f32[576,3584]{1,0:T(8,128)S(1)} %fusion), kind=kOutput, calls=%fused_computation.7 | convolution fusion | flops 2120712192 | bytes 13107200 | tf_op jit(solution)/shard_map/esf,edf->esd/dot_general | solution.py:312
  142.2 19.6 %shard_map.134 = bf16[8,72,1024]{2,1,0:T(8,128)(2,1)} custom-call(bf16[8,72,1024]{2,1,0:T(8,128)(2,1)} %bitcast.50), custom_call_target="tpu_custom_call" | custom-call | tf_op jit(solution)/shard_map/pallas_call | solution.py:160
  161.7 2.8 %fusion.8 = bf16[1,192,1024]{2,1,0:T(8,128)(2,1)} fusion(f32[192,576]{1,0:T(8,128)S(1)} %select_reduce_fusion, bf16[576,1024]{1,0:T(8,128)(2,1)} %bitcast.47, bf16[192,1024]{1,0:T(8,128)(2,1)S(1)} %get-tuple-element.3), kind=kOutput, calls=%fused_computation.10 | convolution fusion | flops 680067072 | bytes 2408448 | tf_op jit(solution)/shard_map/dot_general | solution.py:327
  (6 shorter events, 0.1 us)
Async XLA Ops:
  7.2 86.4 %copy-start = (bf16[1024,1024]{1,0:T(8,128)(2,1)S(1)}, bf16[1024,1024]{1,0:T(8,128)(2,1)}, u32[]{:S(2)}) copy-start(bf16[1024,1024]{1,0:T(8,128)(2,1)} %param.17) | copy-start | bytes 6291460
  7.2 122.4 %all-gather.2.cloned.1.call-start = ((), (), s32[]{:S(2)}) async-start(), calls=%async_computation | async-start | bytes 11354112 | tf_op jit(solution)/shard_map/all_gather | solution.py:302
  66.5 27.0 %copy-start.1 = (bf16[1,192,1024]{2,1,0:T(8,128)(2,1)S(1)}, bf16[1,192,1024]{2,1,0:T(8,128)(2,1)}, u32[]{:S(2)}) copy-start(bf16[1,192,1024]{2,1,0:T(8,128)(2,1)} %param.12) | copy-start | bytes 1179652
  67.8 28.1 %copy-start.2 = (f32[1024]{0:T(1024)S(1)}, f32[1024]{0:T(1024)}, u32[]{:S(2)}) copy-start(f32[1024]{0:T(1024)} %param.18) | copy-start | bytes 12292
  96.1 26.7 %copy-start.3 = (f32[1,192,2]{1,2,0:T(2,128)S(1)}, f32[1,192,2]{1,2,0:T(2,128)}, u32[]{:S(2)}) copy-start(f32[1,192,2]{1,2,0:T(2,128)} %param.23) | copy-start | bytes 4612
Sparse Core Ops, SparseCore 0:
  10.8 118.7 all-gather.1

commit v16 on v12

--- a/solution.py
+++ b/solution.py
@@ -120,7 +120,7 @@
     )(block)
 
 
-def exchange_kernel(n_exp, chunk_ref, out_ref, local_sem, send_sem, recv_sem):
+def exchange_kernel(n_exp, chunk_ref, out_ref, send_sem, recv_sem):
     me = lax.axis_index("exp")
     z = lax.axis_index("z")
     yh = lax.axis_index("yh")
@@ -133,8 +133,6 @@
     for offset in range(1, n_exp):
         pl.semaphore_signal(barrier, 1, device_id=(z, yh, core, peer(offset)), device_id_type=MESH)
     pl.semaphore_wait(barrier, n_exp - 1)
-    own = pltpu.make_async_copy(chunk_ref.at[me], out_ref.at[me], local_sem)
-    own.start()
     sends = []
     for offset in range(1, n_exp):
         target = peer(offset)
@@ -150,25 +148,25 @@
             out_ref.at[source], out_ref.at[source], send_sem.at[offset], recv_sem.at[source],
             device_id=(z, yh, core, source), device_id_type=MESH,
         ).wait_recv()
-    own.wait()
     for copy in sends:
         copy.wait_send()
 
 
 def exchange_exp(chunks, collective_id):
     n_exp = chunks.shape[0]
-    return pl.pallas_call(
+    exchanged = pl.pallas_call(
         functools.partial(exchange_kernel, n_exp),
         out_shape=jax.ShapeDtypeStruct(chunks.shape, chunks.dtype),
         in_specs=[pl.BlockSpec(memory_space=pl.ANY)],
         out_specs=pl.BlockSpec(memory_space=pl.ANY),
         scratch_shapes=[
-            pltpu.SemaphoreType.DMA(()),
             pltpu.SemaphoreType.DMA((n_exp,)),
             pltpu.SemaphoreType.DMA((n_exp,)),
         ],
         compiler_params=pltpu.CompilerParams(collective_id=collective_id, has_side_effects=True),
     )(chunks)
+    me = lax.axis_index("exp")
+    return lax.dynamic_update_slice(exchanged, lax.dynamic_slice_in_dim(chunks, me, 1, 0), (me, 0, 0))
 
 
 KEY_BLOCK = 128

time: 172 us -> 177 us (1.029)
  the two profiles are of different devices: /device:TPU:1 before, /device:TPU:96 now
where the time goes in v16:
time: 177 us; the launch traced here: 176 us
  Pallas kernels  128 us (72%)
  matrix products  21 us (12%)
  between operations  14.2 us (8%)
  local copies, waits for them, and re-layouts  7.05 us (4%)
  other arithmetic  6.35 us (4%)
    pallas_call x2, Pallas kernels, exchange_exp(): pl.pallas_call(functools.partial(exchange_kernel, n_exp), out_shape=jax.S...  51.4 us
    pallas_call x1, Pallas kernels, gather_ctx_kernel(): pl.pallas_call(functools.partial(gather_kernel, n_z), out_shape=jax.Shape...  47.4 us
    pallas_call x1, Pallas kernels, block_attention(): pl.pallas_call(functools.partial(attention_kernel, groups, head_size), ou...  29 us
    dot_general x1, matrix products, shards(): jnp.dot(arrived[0], weight_piece[0, :, :2 * ff], preferred_element_type=j...  7.08 us
    dot_general x1, matrix products, shards(): jnp.einsum('esf,edf->esd', hidden, down_piece, preferred_element_type=jnp...  5.48 us
  transfers between devices with their start and end apart: 1, of which 0 were waited for; matrix products, arithmetic and copies ran while one was open for 9% of the time, Pallas kernels for 59%

profile of v16, /device:TPU:96, one launch (start us, length us, event | category | flops | bytes accessed | tf_op | source)
XLA Modules:
  0.0 176.4 jit_solution(14583646511204312122)
XLA Ops:
  7.2 0.0 copy-start
  7.2 0.0 all-gather.2.cloned.1.call-start
  7.2 1.9 %pad_maximum_fusion = bf16[1,32,5376]{2,1,0:T(8,128)(2,1)} fusion(bf16[1,32,1792]{2,1,0:T(8,128)(2,1)} %param.21, bf16[1,32,1792]{2,1,0:T(8,128)(2,1)} %param.20, bf16[1,32,1792]{2,1,0:T(8,128)(2,1)} %param.19), kind=kLoop, calls=%fused_computation.23 | loop fusion | flops 1032192 | bytes 688128 | tf_op jit(solution)/shard_map/concatenate | solution.py:301
  9.1 0.0 all-gather.2.cloned.1.call-update
  9.1 0.8 copy.20
  10.0 0.1 eq.56
  10.1 0.1 eq.52
  10.3 0.9 reduce-window.6
  11.1 0.2 slice_reduce_fusion
  11.4 0.8 fusion.19
  12.2 0.1 reduce_max.14
  12.3 1.6 pad_maximum_fusion.1.shard_ref
  13.9 47.4 %shard_map.131 = bf16[32,192,512]{2,1,0:T(8,128)(2,1)} custom-call(bf16[192,512]{1,0:T(8,128)(2,1)} %pad_maximum_fusion.1.shard_ref), custom_call_target="tpu_custom_call" | custom-call | tf_op jit(solution)/shard_map/pallas_call | solution.py:109
  61.3 0.6 reduce_max.18.flag_ref
  61.9 0.6 broadcast_in_dim.34
  62.6 0.0 copy-start.1
  62.6 29.0 %shard_map.132 = bf16[192,1024]{1,0:T(8,128)(2,1)} custom-call(s32[48]{0:T(128)} %reduce_max.18.flag_ref, bf16[192,1024]{1,0:T(8,128)(2,1)} %bitcast.54, bf16[6144,512]{1,0:T(8,128)(2,1)} %bitcast.46, bf16[192,192]{1,0:T(8,128)(2,1)} %bitcast.53), custom_call_target="tpu_custom_call" | custom-call | tf_op jit(solution)/shard_map/pallas_call | solution.py:243
  91.6 0.0 copy-done
  91.6 0.0 copy-done.1
  91.6 0.0 copy-start.2
  91.6 2.4 %fusion.9 = (f32[192]{0:T(256)S(1)}, bf16[192,1024]{1,0:T(8,128)(2,1)S(1)}, bf16[1,192,1024]{2,1,0:T(8,128)(2,1)}) fusion(bf16[1,192,1024]{2,1,0:T(8,128)(2,1)S(1)} %copy-done.1, bf16[192,1024]{1,0:T(8,128)(2,1)} %shard_map.132, bf16[1024,1024]{1,0:T(8,128)(2,1)S(1)} %copy-done), kind=kOutput, calls=%fused_computation.16 | convolution fusion | flops 404029248 | bytes 3670784 | tf_op jit(solution)/shard_map/dot_general | solution.py:280
  94.0 0.0 copy-done.2
  94.0 0.2 fusion.11
  94.2 0.4 broadcast_in_dim.39
  94.6 1.2 reshape.89
  95.8 0.1 fusion.15
  95.9 0.1 reduce_sum.30
  96.0 0.0 copy-start.3
  96.1 2.9 %convolution_convert_fusion = bf16[576,1024]{1,0:T(8,128)(2,1)} fusion(bf16[384,1024]{1,0:T(8,128)(2,1)} %reshape.89, s32[384]{0:T(512)S(1)} %multiply_add_fusion), kind=kOutput, calls=%fused_computation.6 | convolution fusion | flops 453795840 | bytes 1967616 | tf_op jit(solution)/shard_map/dot_general | solution.py:294
  99.0 28.4 %shard_map.133 = bf16[8,72,1024]{2,1,0:T(8,128)(2,1)} custom-call(bf16[8,72,1024]{2,1,0:T(8,128)(2,1)} %bitcast.48), custom_call_target="tpu_custom_call" | custom-call | tf_op jit(solution)/shard_map/pallas_call | solution.py:157
  127.4 0.1 copy.23
  127.5 1.6 dynamic-slice_dynamic-update-slice_fusion.1
  129.0 0.0 copy-done.3
  129.0 0.2 select_reduce_fusion
  129.2 0.0 all-gather.2.cloned.1.call-done
  129.3 7.1 %fusion = f32[576,3584]{1,0:T(8,128)S(1)} fusion(bf16[576,1024]{1,0:T(8,128)(2,1)} %bitcast.52, bf16[1,1024,5376]{2,1,0:T(8,128)(2,1)} %all-gather.2.cloned.1.call-done), kind=kOutput, calls=%fused_computation.1 | convolution fusion | flops 4227858432 | bytes 16777216 | tf_op jit(solution)/shard_map/dot_general | solution.py:306
  136.3 5.5 %fusion.4 = bf16[576,1024]{1,0:T(8,128)(2,1)} fusion(bf16[1,1024,5376]{2,1,0:T(8,128)(2,1)} %all-gather.2.cloned.1.call-done, f32[576,3584]{1,0:T(8,128)S(1)} %fusion), kind=kOutput, calls=%fused_computation.7 | convolution fusion | flops 2120712192 | bytes 13107200 | tf_op jit(solution)/shard_map/esf,edf->esd/dot_general | solution.py:310
  141.8 23.0 %shard_map.134 = bf16[8,72,1024]{2,1,0:T(8,128)(2,1)} custom-call(bf16[8,72,1024]{2,1,0:T(8,128)(2,1)} %bitcast.50), custom_call_target="tpu_custom_call" | custom-call | tf_op jit(solution)/shard_map/pallas_call | solution.py:157
  164.9 1.6 dynamic-slice_dynamic-update-slice_fusion
  166.5 3.1 %fusion.8 = bf16[1,192,1024]{2,1,0:T(8,128)(2,1)} fusion(f32[192,576]{1,0:T(8,128)S(1)} %select_reduce_fusion, bf16[576,1024]{1,0:T(8,128)(2,1)} %bitcast.47, bf16[192,1024]{1,0:T(8,128)(2,1)S(1)} %get-tuple-element.3), kind=kOutput, calls=%fused_computation.10 | convolution fusion | flops 1359544320 | bytes 2408448 | tf_op jit(solution)/shard_map/dot_general | solution.py:325
  (6 shorter events, 0.1 us)
Async XLA Ops:
  7.2 84.5 %copy-start = (bf16[1024,1024]{1,0:T(8,128)(2,1)S(1)}, bf16[1024,1024]{1,0:T(8,128)(2,1)}, u32[]{:S(2)}) copy-start(bf16[1024,1024]{1,0:T(8,128)(2,1)} %param.17) | copy-start | bytes 6291460
  7.2 122.1 %all-gather.2.cloned.1.call-start = ((), (), s32[]{:S(2)}) async-start(), calls=%async_computation | async-start | bytes 11354112 | tf_op jit(solution)/shard_map/all_gather | solution.py:300
  62.6 29.0 %copy-start.1 = (bf16[1,192,1024]{2,1,0:T(8,128)(2,1)S(1)}, bf16[1,192,1024]{2,1,0:T(8,128)(2,1)}, u32[]{:S(2)}) copy-start(bf16[1,192,1024]{2,1,0:T(8,128)(2,1)} %param.12) | copy-start | bytes 1179652
  91.6 2.4 %copy-start.2 = (f32[1024]{0:T(1024)S(1)}, f32[1024]{0:T(1024)}, u32[]{:S(2)}) copy-start(f32[1024]{0:T(1024)} %param.18) | copy-start | bytes 12292
  96.0 33.0 %copy-start.3 = (f32[1,192,2]{1,2,0:T(2,128)S(1)}, f32[1,192,2]{1,2,0:T(2,128)}, u32[]{:S(2)}) copy-start(f32[1,192,2]{1,2,0:T(2,128)} %param.23) | copy-start | bytes 4612
Sparse Core Ops, SparseCore 0:
  10.8 115.6 all-gather.1

commit v17 on v12

--- a/solution.py
+++ b/solution.py
@@ -160,7 +160,7 @@
     return pl.pallas_call(
         functools.partial(exchange_kernel, n_exp),
         out_shape=jax.ShapeDtypeStruct(chunks.shape, chunks.dtype),
-        in_specs=[pl.BlockSpec(memory_space=pl.ANY)],
+        in_specs=[pl.BlockSpec(memory_space=pltpu.VMEM)],
         out_specs=pl.BlockSpec(memory_space=pl.ANY),
         scratch_shapes=[
             pltpu.SemaphoreType.DMA(()),

time: 172 us -> 173 us (level)
  waiting for transfers between devices: 0.04 us -> 2.8 us
    pallas_call x1, Pallas kernels: 31.6 us -> 27.7 us  [block_attention(): pl.pallas_call(functools.partial(attention_kernel, groups, head_size), ou...]
    pallas_call x2, Pallas kernels: 40.6 us -> 44.2 us  [exchange_exp(): pl.pallas_call(functools.partial(exchange_kernel, n_exp), out_shape=jax.S...]
    all_gather x1, waiting for transfers between devices: 0.02 us -> 2.78 us  [shards(): lax.all_gather(jnp.concatenate([gate_weight, up_weight, down_weight], axi...]
  transfers between devices with their start and end apart: 1 -> 1, of which waited for: 0 -> 1; matrix products, arithmetic and copies ran while one was open for 8% -> 8% of each run, Pallas kernels for 64% -> 60%
where the time goes in v17:
time: 173 us
  Pallas kernels  124 us (72%)
  matrix products  20.9 us (12%)
  between operations  14.2 us (8%)
  other arithmetic  6.36 us (4%)
  local copies, waits for them, and re-layouts  3.9 us (2%)
  waiting for transfers between devices  2.8 us (2%)
    pallas_call x1, Pallas kernels, gather_ctx_kernel(): pl.pallas_call(functools.partial(gather_kernel, n_z), out_shape=jax.Shape...  52.6 us
    pallas_call x2, Pallas kernels, exchange_exp(): pl.pallas_call(functools.partial(exchange_kernel, n_exp), out_shape=jax.S...  44.2 us
    pallas_call x1, Pallas kernels, block_attention(): pl.pallas_call(functools.partial(attention_kernel, groups, head_size), ou...  27.7 us
    dot_general x1, matrix products, shards(): jnp.dot(arrived[0], weight_piece[0, :, :2 * ff], preferred_element_type=j...  7.07 us
    dot_general x1, matrix products, shards(): jnp.einsum('esf,edf->esd', hidden, down_piece, preferred_element_type=jnp...  5.47 us
  transfers between devices with their start and end apart: 1, of which 1 were waited for; matrix products, arithmetic and copies ran while one was open for 8% of the time, Pallas kernels for 60%

profile of v17, /device:TPU:1, one launch (start us, length us, event | category | flops | bytes accessed | tf_op | source)
XLA Modules:
  0.0 172.7 jit_solution(2720137726202334435)
XLA Ops:
  7.2 0.0 copy-start
  7.2 0.0 all-gather.2.cloned.1.call-start
  7.2 1.9 %pad_maximum_fusion = bf16[1,32,5376]{2,1,0:T(8,128)(2,1)} fusion(bf16[1,32,1792]{2,1,0:T(8,128)(2,1)} %param.21, bf16[1,32,1792]{2,1,0:T(8,128)(2,1)} %param.20, bf16[1,32,1792]{2,1,0:T(8,128)(2,1)} %param.19), kind=kLoop, calls=%fused_computation.23 | loop fusion | flops 1032192 | bytes 688128 | tf_op jit(solution)/shard_map/concatenate | solution.py:303
  9.1 0.0 all-gather.2.cloned.1.call-update
  9.1 0.8 copy.20
  10.0 0.1 eq.56
  10.1 0.1 eq.52
  10.3 0.9 reduce-window.6
  11.1 0.2 slice_reduce_fusion
  11.4 0.8 fusion.19
  12.2 0.1 reduce_max.14
  12.3 1.6 pad_maximum_fusion.1.shard_ref
  13.9 52.6 %shard_map.131 = bf16[32,192,512]{2,1,0:T(8,128)(2,1)} custom-call(bf16[192,512]{1,0:T(8,128)(2,1)} %pad_maximum_fusion.1.shard_ref), custom_call_target="tpu_custom_call" | custom-call | tf_op jit(solution)/shard_map/pallas_call | solution.py:109
  66.5 0.0 copy-start.1
  66.5 0.6 reduce_max.18.flag_ref
  67.2 0.6 broadcast_in_dim.34
  67.8 0.0 copy-start.2
  67.8 27.7 %shard_map.132 = bf16[192,1024]{1,0:T(8,128)(2,1)} custom-call(s32[48]{0:T(128)} %reduce_max.18.flag_ref, bf16[192,1024]{1,0:T(8,128)(2,1)} %bitcast.52, bf16[6144,512]{1,0:T(8,128)(2,1)} %bitcast.46, bf16[192,192]{1,0:T(8,128)(2,1)} %bitcast.51), custom_call_target="tpu_custom_call" | custom-call | tf_op jit(solution)/shard_map/pallas_call | solution.py:245
  95.5 0.0 copy-done
  95.5 0.0 copy-done.1
  95.5 2.4 %fusion.9 = (f32[192]{0:T(256)S(1)}, bf16[192,1024]{1,0:T(8,128)(2,1)S(1)}, bf16[1,192,1024]{2,1,0:T(8,128)(2,1)}) fusion(bf16[1,192,1024]{2,1,0:T(8,128)(2,1)S(1)} %copy-done.1, bf16[192,1024]{1,0:T(8,128)(2,1)} %shard_map.132, bf16[1024,1024]{1,0:T(8,128)(2,1)S(1)} %copy-done), kind=kOutput, calls=%fused_computation.16 | convolution fusion | flops 404029248 | bytes 3670784 | tf_op jit(solution)/shard_map/dot_general | solution.py:282
  97.9 0.0 copy-done.2
  97.9 0.2 fusion.11
  98.1 0.0 copy-start.3
  98.1 0.4 broadcast_in_dim.39
  98.5 1.2 reshape.89
  99.7 0.1 fusion.15
  99.8 0.1 reduce_sum.30
  100.0 2.9 %convolution_convert_fusion = bf16[576,1024]{1,0:T(8,128)(2,1)} fusion(bf16[384,1024]{1,0:T(8,128)(2,1)} %reshape.89, s32[384]{0:T(512)S(1)} %multiply_add_fusion), kind=kOutput, calls=%fused_computation.6 | convolution fusion | flops 453795840 | bytes 1967616 | tf_op jit(solution)/shard_map/dot_general | solution.py:296
  102.9 23.6 %shard_map.133 = bf16[8,72,1024]{2,1,0:T(8,128)(2,1)} custom-call(bf16[8,72,1024]{2,1,0:T(8,128)(2,1)} %bitcast.49), custom_call_target="tpu_custom_call" | custom-call | tf_op jit(solution)/shard_map/pallas_call | solution.py:160
  126.5 0.1 copy.23
  126.6 0.0 copy-done.3
  126.6 0.2 select_reduce_fusion
  126.8 2.8 %all-gather.2.cloned.1.call-done = bf16[1,1024,5376]{2,1,0:T(8,128)(2,1)} async-done(((bf16[1,32,5376]{2,1,0:T(8,128)(2,1)}), bf16[1,1024,5376]{2,1,0:T(8,128)(2,1)}) %all-gather.2.cloned.1.call-update) | async-done | bytes 11010064 | tf_op jit(solution)/shard_map/all_gather | solution.py:302
  129.6 7.1 %fusion = f32[576,3584]{1,0:T(8,128)S(1)} fusion(bf16[576,1024]{1,0:T(8,128)(2,1)} %bitcast.48, bf16[1,1024,5376]{2,1,0:T(8,128)(2,1)} %all-gather.2.cloned.1.call-done), kind=kOutput, calls=%fused_computation.1 | convolution fusion | flops 4227858432 | bytes 16777216 | tf_op jit(solution)/shard_map/dot_general | solution.py:308
  136.7 5.5 %fusion.4 = bf16[576,1024]{1,0:T(8,128)(2,1)} fusion(bf16[1,1024,5376]{2,1,0:T(8,128)(2,1)} %all-gather.2.cloned.1.call-done, f32[576,3584]{1,0:T(8,128)S(1)} %fusion), kind=kOutput, calls=%fused_computation.7 | convolution fusion | flops 2120712192 | bytes 13107200 | tf_op jit(solution)/shard_map/esf,edf->esd/dot_general | solution.py:312
  142.2 20.6 %shard_map.134 = bf16[8,72,1024]{2,1,0:T(8,128)(2,1)} custom-call(bf16[8,72,1024]{2,1,0:T(8,128)(2,1)} %bitcast.50), custom_call_target="tpu_custom_call" | custom-call | tf_op jit(solution)/shard_map/pallas_call | solution.py:160
  162.7 3.1 %fusion.8 = bf16[1,192,1024]{2,1,0:T(8,128)(2,1)} fusion(f32[192,576]{1,0:T(8,128)S(1)} %select_reduce_fusion, bf16[576,1024]{1,0:T(8,128)(2,1)} %bitcast.47, bf16[192,1024]{1,0:T(8,128)(2,1)S(1)} %get-tuple-element.3), kind=kOutput, calls=%fused_computation.10 | convolution fusion | flops 1359544320 | bytes 2408448 | tf_op jit(solution)/shard_map/dot_general | solution.py:327
  (6 shorter events, 0.1 us)
Async XLA Ops:
  7.2 88.4 %copy-start = (bf16[1024,1024]{1,0:T(8,128)(2,1)S(1)}, bf16[1024,1024]{1,0:T(8,128)(2,1)}, u32[]{:S(2)}) copy-start(bf16[1024,1024]{1,0:T(8,128)(2,1)} %param.17) | copy-start | bytes 6291460
  7.2 122.4 %all-gather.2.cloned.1.call-start = ((), (), s32[]{:S(2)}) async-start(), calls=%async_computation | async-start | bytes 11354112 | tf_op jit(solution)/shard_map/all_gather | solution.py:302
  66.5 29.0 %copy-start.1 = (bf16[1,192,1024]{2,1,0:T(8,128)(2,1)S(1)}, bf16[1,192,1024]{2,1,0:T(8,128)(2,1)}, u32[]{:S(2)}) copy-start(bf16[1,192,1024]{2,1,0:T(8,128)(2,1)} %param.12) | copy-start | bytes 1179652
  67.8 30.1 %copy-start.2 = (f32[1024]{0:T(1024)S(1)}, f32[1024]{0:T(1024)}, u32[]{:S(2)}) copy-start(f32[1024]{0:T(1024)} %param.18) | copy-start | bytes 12292
  98.1 28.6 %copy-start.3 = (f32[1,192,2]{1,2,0:T(2,128)S(1)}, f32[1,192,2]{1,2,0:T(2,128)}, u32[]{:S(2)}) copy-start(f32[1,192,2]{1,2,0:T(2,128)} %param.23) | copy-start | bytes 4612
Sparse Core Ops, SparseCore 0:
  10.8 118.7 all-gather.1
